TPU v7x, 32 devices: a whole 2x2x4 slice. The times are simulated.
32 devices in a mesh: batch: 8 (over y, x, core), tensor: 4 (over z).
Axes of the slice: x: 2, y: 2, z: 4, core: 2. Of those that a mesh axis runs over, the one named last changes fastest.
Arguments:
- patches: bfloat16 [16384, 48], P(('batch', 'tensor')), may hold values from -6 to 6
- valid_mask: int32 [16384], P('batch'), may hold values 0 or 1
- class_ids: int32 [64], P(('batch', 'tensor')), may hold values from 0 to 999
- embed_weight: bfloat16 [48, 768], replicated, may hold values from -0.875 to 0.875
- embed_bias: float32 [768], replicated, may hold values from -3 to 3
- position_table: bfloat16 [256, 768], replicated, may hold values from -3 to 3
- class_table: bfloat16 [1000, 768], replicated, may hold values from -3 to 3
- attn_gain: float32 [2, 768], replicated, may hold values from 0.5 to 1.5
- attn_offset: float32 [2, 768], replicated, may hold values from -2 to 2
- attend_weight: bfloat16 [2, 3, 768, 768], P(None, None, None, 'tensor'), may hold values from -0.21875 to 0.21875
- merge_weight: bfloat16 [2, 768, 768], P(None, 'tensor'), may hold values from -0.625 to 0.625
- mlp_gain: float32 [2, 768], replicated, may hold values from 0.5 to 1.5
- mlp_offset: float32 [2, 768], replicated, may hold values from -2 to 2
- up_weight: bfloat16 [2, 768, 3072], P(None, None, 'tensor'), may hold values from -0.21875 to 0.21875
- up_bias: float32 [2, 3072], P(None, 'tensor'), may hold values from -3 to 3
- down_weight: bfloat16 [2, 3072, 768], P(None, 'tensor'), may hold values from -0.109375 to 0.109375
- down_bias: float32 [2, 768], replicated, may hold values from -2 to 2
- final_gain: float32 [768], replicated, may hold values from 0.5 to 1.5
- final_offset: float32 [768], replicated, may hold values from -2 to 2
- head_weight: bfloat16 [768, 96], replicated, may hold values from -0.109375 to 0.109375
- head_bias: float32 [96], replicated, may hold values from -2 to 2
- latent_cot: float32 [16384, 48], P(('batch', 'tensor')), may hold values from -6 to 6
- logdet_cot: float32 [64], P(('batch', 'tensor')), may hold values from -0.6 to 0.6
Outputs:
- latents: float32 [16384, 48], P(('batch', 'tensor'))
- log_det: float32 [64], P(('batch', 'tensor'))
- patches_grad: float32 [16384, 48], P(('batch', 'tensor'))
- embed_weight_grad: float32 [48, 768], replicated
- embed_bias_grad: float32 [768], replicated
- position_grad: float32 [256, 768], replicated
- class_grad: float32 [1000, 768], replicated
- attn_gain_grad: float32 [2, 768], replicated
- attn_offset_grad: float32 [2, 768], replicated
- attend_weight_grad: float32 [2, 3, 768, 768], P(None, None, None, 'tensor')
- merge_weight_grad: float32 [2, 768, 768], P(None, 'tensor')
- mlp_gain_grad: float32 [2, 768], replicated
- mlp_offset_grad: float32 [2, 768], replicated
- up_weight_grad: float32 [2, 768, 3072], P(None, None, 'tensor')
- up_bias_grad: float32 [2, 3072], P(None, 'tensor')
- down_weight_grad: float32 [2, 3072, 768], P(None, 'tensor')
- down_bias_grad: float32 [2, 768], replicated
- final_gain_grad: float32 [768], replicated
- final_offset_grad: float32 [768], replicated
- head_weight_grad: float32 [768, 96], replicated
- head_bias_grad: float32 [96], replicated
Inputs may be any that keep to these rules, and one draw needn't show every extreme that they name: `valid_mask`: 1 marks a valid patch, 0 a masked one.
All inputs are finite; a program needn't handle non-finite values. No bound on the sum of `valid_mask` on one device may be relied on, other than what follows from the above.
Results may differ from a plain program's by a relative error of at most 0.017.
Values may be sent and summed in bfloat16 or wider, within the bound.
A program may use at most 256 MiB of HBM per device.

v0:
```python
import jax
import jax.numpy as jnp
from jax import lax
from jax.sharding import PartitionSpec as P

D = 768
HEAD_DIM = 64
P_SIZE = 256
PV = 48
CLASSES = 1000
NL = 2


EPSILON = 1e-05
NEGATIVE = -1000000000.0
HIGHEST = lax.Precision.HIGHEST


def layer_norm(values, norm_gain, norm_offset):
    center = values - jnp.mean(values, axis=-1, keepdims=True)
    spread = jnp.mean(center * center, axis=-1, keepdims=True)
    return center * lax.rsqrt(spread + EPSILON) * norm_gain + norm_offset


def norm_backward(values, norm_gain, norm_offset, upstream):
    outputs, pullback = jax.vjp(layer_norm, values, norm_gain, norm_offset)
    return pullback(upstream)


def gelu_exact(values):
    return jax.nn.gelu(values, approximate=False)


def product(former, latter):
    return jnp.dot(former, latter, preferred_element_type=jnp.float32)


def product_back(former, latter):
    return lax.dot_general(
        former, latter, (((1,), (1,)), ((), ())), preferred_element_type=jnp.float32
    )


def contract_rows(former, latter):
    return lax.dot_general(
        former, latter, (((0,), (0,)), ((), ())), preferred_element_type=jnp.float32
    )


def precise_rows(former, latter):
    return lax.dot_general(
        former,
        latter,
        (((0,), (0,)), ((), ())),
        precision=HIGHEST,
        preferred_element_type=jnp.float32,
    )


def build_allowed(mask_rows, span):
    row_index = lax.broadcasted_iota(jnp.int32, (span, span), 0)
    col_index = lax.broadcasted_iota(jnp.int32, (span, span), 1)
    causal = (row_index // P_SIZE == col_index // P_SIZE) & (col_index <= row_index)
    key_valid = mask_rows.reshape(mask_rows.shape[0] // span, 1, span) > 0
    return causal[None] & (key_valid | (row_index == col_index)[None])


def widen_rows(shard_low, multiply):
    gathered = lax.all_gather(shard_low, "tensor", axis=0, tiled=True)
    return (multiply(gathered), gathered)


def weight_grad(kept_rows, contract):
    return contract(kept_rows, 0)


def narrow(term_rows, shard_count):
    return lax.psum_scatter(
        term_rows(jnp.int32(0), shard_count * lax.axis_size("tensor")),
        "tensor",
        scatter_dimension=0,
        tiled=True,
    )


def gather_grad(grad_low):
    return lax.all_gather(grad_low, "tensor", axis=0, tiled=True)


def block_scores(qkv_low, allowed):
    span = allowed.shape[1]
    blocks = qkv_low.reshape(qkv_low.shape[0] // span, span, 3, -1, HEAD_DIM)
    queries = blocks[:, :, 0]
    keys = blocks[:, :, 1]
    values = blocks[:, :, 2]
    scaling = HEAD_DIM ** (-0.5)
    scores = (
        jnp.einsum("bqhd,bkhd->bhqk", queries, keys, preferred_element_type=jnp.float32) * scaling
    )
    scores = jnp.where(allowed[:, None], scores, NEGATIVE)
    return (queries, keys, values, scores)


def attend(qkv_low, allowed):
    queries, keys, values, scores = block_scores(qkv_low, allowed)
    log_total = jax.nn.logsumexp(scores, axis=-1, keepdims=True)
    probs_low = jnp.exp(scores - log_total).astype(jnp.bfloat16)
    mixed = jnp.einsum("bhqk,bkhd->bqhd", probs_low, values, preferred_element_type=jnp.float32)
    return (mixed.reshape(qkv_low.shape[0], -1).astype(jnp.bfloat16), log_total)


def attend_back(qkv_low, allowed, log_total, grad_mixed):
    queries, keys, values, scores = block_scores(qkv_low, allowed)
    probs_full = jnp.exp(scores - log_total)
    probs_low = probs_full.astype(jnp.bfloat16)
    grad_out = grad_mixed.reshape(queries.shape)
    grad_values = jnp.einsum(
        "bhqk,bqhd->bkhd", probs_low, grad_out, preferred_element_type=jnp.float32
    )
    grad_probs = jnp.einsum("bqhd,bkhd->bhqk", grad_out, values, preferred_element_type=jnp.float32)
    inner_sum = jnp.sum(probs_full * grad_probs, axis=-1, keepdims=True)
    grad_scores = (probs_full * (grad_probs - inner_sum)).astype(jnp.bfloat16)
    scaling = HEAD_DIM ** (-0.5)
    grad_queries = (
        jnp.einsum("bhqk,bkhd->bqhd", grad_scores, keys, preferred_element_type=jnp.float32)
        * scaling
    )
    grad_keys = (
        jnp.einsum("bhqk,bqhd->bkhd", grad_scores, queries, preferred_element_type=jnp.float32)
        * scaling
    )
    stacked = jnp.stack([grad_queries, grad_keys, grad_values], axis=2)
    return stacked.reshape(qkv_low.shape).astype(jnp.bfloat16)


def shards(
    patches,
    valid_mask,
    class_ids,
    embed_weight,
    embed_bias,
    position_table,
    class_table,
    attn_gain,
    attn_offset,
    attend_weight,
    merge_weight,
    mlp_gain,
    mlp_offset,
    up_weight,
    up_bias,
    down_weight,
    down_bias,
    final_gain,
    final_offset,
    head_weight,
    head_bias,
    latent_cot,
    logdet_cot,
):
    shard_count = patches.shape[0]
    local_images = shard_count // P_SIZE
    tensor_index = lax.axis_index("tensor")
    patch_values = patches.astype(jnp.float32)
    local_valid = lax.dynamic_slice_in_dim(valid_mask, tensor_index * shard_count, shard_count, 0)
    live_mask = local_valid.astype(jnp.float32)[:, None]
    layer_weights = (attend_weight, merge_weight, up_weight, down_weight)
    allowed = build_allowed(valid_mask, 2 * P_SIZE)
    embed_full = embed_weight.astype(jnp.float32)
    choose = class_ids[:, None] == lax.broadcasted_iota(jnp.int32, (local_images, CLASSES), 1)
    class_rows = product(choose.astype(jnp.bfloat16), class_table)
    hidden = product(patches, embed_weight) + embed_bias
    hidden = hidden.reshape(local_images, P_SIZE, D) + position_table.astype(jnp.float32)[None]
    hidden = (hidden + class_rows[:, None]).reshape(shard_count, D)
    stored = []
    for layer_index in range(NL):
        attend_layer = layer_weights[0][layer_index]
        merge_layer = layer_weights[1][layer_index]
        up_layer = layer_weights[2][layer_index]
        down_layer = layer_weights[3][layer_index]
        normed = layer_norm(hidden, attn_gain[layer_index], attn_offset[layer_index]).astype(
            jnp.bfloat16
        )
        qkv, attn_kept = widen_rows(
            normed,
            lambda portion: jnp.einsum(
                "rd,cde->rce", portion, attend_layer, preferred_element_type=jnp.float32
            ),
        )
        qkv_low = qkv.astype(jnp.bfloat16)
        mixed_low, log_total = attend(qkv_low, allowed)
        attn_sum = narrow(lambda begin_row, length: product(mixed_low, merge_layer), shard_count)
        hidden_mid = hidden + attn_sum
        normed_mlp = layer_norm(hidden_mid, mlp_gain[layer_index], mlp_offset[layer_index]).astype(
            jnp.bfloat16
        )
        inner_sum, mlp_kept = widen_rows(normed_mlp, lambda portion: product(portion, up_layer))
        pre_active = inner_sum + up_bias[layer_index]
        active = gelu_exact(pre_active).astype(jnp.bfloat16)
        mlp_sum = narrow(lambda begin_row, length: product(active, down_layer), shard_count)
        stored.append(
            (hidden, attn_kept, qkv_low, log_total, mixed_low, hidden_mid, mlp_kept, pre_active)
        )
        hidden = hidden_mid + (mlp_sum + down_bias[layer_index])
    final = layer_norm(hidden, final_gain, final_offset)
    final_low = final.astype(jnp.bfloat16)
    head_out = product(final_low, head_weight) + head_bias
    position = lax.broadcasted_iota(jnp.int32, (shard_count, 1), 0) % P_SIZE
    starts = position == 0
    previous = jnp.concatenate([jnp.zeros((1, 2 * PV), jnp.float32), head_out[:-1]], axis=0)
    previous = jnp.where(starts, 0.0, previous)
    shift_part = previous[:, :PV]
    log_scale = previous[:, PV:]
    scale_factor = jnp.exp(-log_scale)
    latents = (
        live_mask * (patch_values - shift_part) * scale_factor + (1.0 - live_mask) * patch_values
    )
    log_det = -jnp.sum((live_mask * log_scale).reshape(local_images, P_SIZE * PV), axis=1)
    image_cot = jnp.repeat(logdet_cot, P_SIZE)[:, None]
    direct_grad = latent_cot * (live_mask * scale_factor + (1.0 - live_mask))
    grad_shift = -live_mask * latent_cot * scale_factor
    grad_scale = -live_mask * (latent_cot * (patch_values - shift_part) * scale_factor + image_cot)
    grad_previous = jnp.where(starts, 0.0, jnp.concatenate([grad_shift, grad_scale], axis=1))
    grad_head = jnp.concatenate([grad_previous[1:], jnp.zeros((1, 2 * PV), jnp.float32)], axis=0)
    grad_head_low = grad_head.astype(jnp.bfloat16)
    head_weight_grad = contract_rows(final_low, grad_head_low)
    head_bias_grad = jnp.sum(grad_head_low.astype(jnp.float32), axis=0)
    grad_final = product_back(grad_head_low, head_weight)
    grad_hidden, final_gain_grad, final_offset_grad = norm_backward(
        hidden, final_gain, final_offset, grad_final
    )
    split_list = [None] * NL
    shared_list = [None] * NL
    for layer_index in reversed(range(NL)):
        hidden_in, attn_kept, qkv_low, log_total, mixed_low, hidden_mid, mlp_kept, pre_active = (
            stored[layer_index]
        )
        attend_layer = layer_weights[0][layer_index]
        merge_layer = layer_weights[1][layer_index]
        up_layer = layer_weights[2][layer_index]
        down_layer = layer_weights[3][layer_index]
        grad_out_mlp = grad_hidden.astype(jnp.bfloat16)
        down_bias_grad = jnp.sum(grad_out_mlp.astype(jnp.float32), axis=0)
        grad_mlp_all = gather_grad(grad_out_mlp)
        active = gelu_exact(pre_active).astype(jnp.bfloat16)
        down_grad = contract_rows(active, grad_mlp_all)
        grad_active = product_back(grad_mlp_all, down_layer)
        outputs, gelu_pull = jax.vjp(gelu_exact, pre_active)
        grad_inner = gelu_pull(grad_active)[0].astype(jnp.bfloat16)
        up_bias_grad = jnp.sum(grad_inner.astype(jnp.float32), axis=0)
        up_grad = weight_grad(
            mlp_kept, lambda portion, begin_row: contract_rows(portion, grad_inner)
        )
        grad_normed = narrow(
            lambda begin_row, length: product_back(grad_inner, up_layer), shard_count
        )
        grad_from, mlp_gain_grad, mlp_offset_grad = norm_backward(
            hidden_mid, mlp_gain[layer_index], mlp_offset[layer_index], grad_normed
        )
        grad_hidden = grad_hidden + grad_from
        grad_out_attn = grad_hidden.astype(jnp.bfloat16)
        grad_attn_all = gather_grad(grad_out_attn)
        merge_grad = contract_rows(mixed_low, grad_attn_all)
        grad_mixed = product_back(grad_attn_all, merge_layer).astype(jnp.bfloat16)
        grad_qkv = attend_back(qkv_low, allowed, log_total, grad_mixed)
        attend_grad = weight_grad(
            attn_kept,
            lambda portion, begin_row: jnp.einsum(
                "rd,rce->cde", portion, grad_qkv, preferred_element_type=jnp.float32
            ),
        )
        grad_normed = narrow(
            lambda begin_row, length: jnp.einsum(
                "rce,cde->rd", grad_qkv, attend_layer, preferred_element_type=jnp.float32
            ),
            shard_count,
        )
        grad_from, attn_gain_grad, attn_offset_grad = norm_backward(
            hidden_in, attn_gain[layer_index], attn_offset[layer_index], grad_normed
        )
        grad_hidden = grad_hidden + grad_from
        split_list[layer_index] = (attend_grad, merge_grad, up_grad, up_bias_grad, down_grad)
        shared_list[layer_index] = (
            attn_gain_grad,
            attn_offset_grad,
            mlp_gain_grad,
            mlp_offset_grad,
            down_bias_grad,
        )
    embed_bias_grad = jnp.sum(grad_hidden, axis=0)
    per_image = grad_hidden.reshape(local_images, P_SIZE, D)
    position_grad = jnp.sum(per_image, axis=0)
    image_sums = jnp.sum(per_image, axis=1)
    class_grad = precise_rows(choose.astype(jnp.float32), image_sums)
    embed_weight_grad = precise_rows(patch_values, grad_hidden)
    patches_grad = direct_grad + lax.dot_general(
        grad_hidden,
        embed_full,
        (((1,), (1,)), ((), ())),
        precision=HIGHEST,
        preferred_element_type=jnp.float32,
    )
    split_stack = tuple((jnp.stack([entry[member] for entry in split_list]) for member in range(5)))
    shared_stack = tuple(
        (jnp.stack([entry[member] for entry in shared_list]) for member in range(5))
    )
    split_stack = lax.psum(
        (split_stack[0], split_stack[1], split_stack[2], split_stack[3], split_stack[4]), "batch"
    )
    joined = lax.psum(
        (
            embed_weight_grad,
            embed_bias_grad,
            position_grad,
            class_grad,
            final_gain_grad,
            final_offset_grad,
            head_weight_grad,
            head_bias_grad,
            shared_stack[0],
            shared_stack[1],
            shared_stack[2],
            shared_stack[3],
            shared_stack[4],
        ),
        ("batch", "tensor"),
    )
    head_sums = joined[:8]
    shared_stack = joined[8:]
    return (
        latents,
        log_det,
        patches_grad,
        head_sums[0],
        head_sums[1],
        head_sums[2],
        head_sums[3],
        shared_stack[0],
        shared_stack[1],
        split_stack[0],
        split_stack[1],
        shared_stack[2],
        shared_stack[3],
        split_stack[2],
        split_stack[3],
        split_stack[4],
        shared_stack[4],
        head_sums[4],
        head_sums[5],
        head_sums[6],
        head_sums[7],
    )


def solution(mesh):
    return jax.shard_map(
        shards,
        mesh=mesh,
        in_specs=(
            P(("batch", "tensor"), None),
            P("batch"),
            P(("batch", "tensor")),
            P(),
            P(),
            P(),
            P(),
            P(),
            P(),
            P(None, None, None, "tensor"),
            P(None, "tensor", None),
            P(),
            P(),
            P(None, None, "tensor"),
            P(None, "tensor"),
            P(None, "tensor", None),
            P(),
            P(),
            P(),
            P(),
            P(),
            P(("batch", "tensor"), None),
            P(("batch", "tensor")),
        ),
        out_specs=(
            P(("batch", "tensor"), None),
            P(("batch", "tensor")),
            P(("batch", "tensor"), None),
            P(),
            P(),
            P(),
            P(),
            P(),
            P(),
            P(None, None, None, "tensor"),
            P(None, "tensor", None),
            P(),
            P(),
            P(None, None, "tensor"),
            P(None, "tensor"),
            P(None, "tensor", None),
            P(),
            P(),
            P(),
            P(),
            P(),
        ),
        check_vma=False,
    )
```

profile of v0, /device:TPU:0, one launch (start us, length us, event | category | flops | bytes accessed | tf_op | source)
XLA Modules:
  0.0 2094.9 jit_solution(18357308917548150727)
XLA Ops:
  17.6 62.2 %all-gather.9.cloned.1.call-done = bf16[2048,768]{1,0:T(8,128)(2,1)} async-done(((bf16[512,768]{1,0:T(8,128)(2,1)}), bf16[2048,768]{1,0:T(8,128)(2,1)}) %all-gather.9.cloned.1.call-update) | async-done | bytes 3145744 | tf_op jit(solution)/shard_map/all_gather | solution.py:69
  100.5 7.3 exponential_reduce_fusion.1
  120.6 108.9 %reduce-scatter.9.cloned.1.call-done = f32[512,768]{1,0:T(8,128)} async-done(((f32[2048,768]{1,0:T(8,128)}), f32[512,768]{1,0:T(8,128)}) %reduce-scatter.9.cloned.1.call-update) | async-done | bytes 1572880 | tf_op jit(solution)/shard_map/reduce_scatter | solution.py:78
  233.7 64.0 %all-gather.11.cloned.1.call-done = bf16[2048,768]{1,0:T(8,128)(2,1)} async-done(((bf16[512,768]{1,0:T(8,128)(2,1)}), bf16[2048,768]{1,0:T(8,128)(2,1)}) %all-gather.11.cloned.1.call-update) | async-done | bytes 3145744 | tf_op jit(solution)/shard_map/all_gather | solution.py:69
  297.7 18.9 multiply_convert_fusion.3
  323.5 108.9 %reduce-scatter.11.cloned.1.call-done = f32[512,768]{1,0:T(8,128)} async-done(((f32[2048,768]{1,0:T(8,128)}), f32[512,768]{1,0:T(8,128)}) %reduce-scatter.11.cloned.1.call-update) | async-done | bytes 1572880 | tf_op jit(solution)/shard_map/reduce_scatter | solution.py:78
  436.5 64.0 %all-gather.13.cloned.1.call-done = bf16[2048,768]{1,0:T(8,128)(2,1)} async-done(((bf16[512,768]{1,0:T(8,128)(2,1)}), bf16[2048,768]{1,0:T(8,128)(2,1)}) %all-gather.13.cloned.1.call-update) | async-done | bytes 3145744 | tf_op jit(solution)/shard_map/all_gather | solution.py:69
  521.3 7.3 exponential_reduce_fusion
  540.7 109.5 %reduce-scatter.13.cloned.1.call-done = f32[512,768]{1,0:T(8,128)} async-done(((f32[2048,768]{1,0:T(8,128)}), f32[512,768]{1,0:T(8,128)}) %reduce-scatter.13.cloned.1.call-update) | async-done | bytes 1572880 | tf_op jit(solution)/shard_map/reduce_scatter | solution.py:78
  654.3 64.0 %all-gather.15.cloned.1.call-done = bf16[2048,768]{1,0:T(8,128)(2,1)} async-done(((bf16[512,768]{1,0:T(8,128)(2,1)}), bf16[2048,768]{1,0:T(8,128)(2,1)}) %all-gather.15.cloned.1.call-update) | async-done | bytes 3145744 | tf_op jit(solution)/shard_map/all_gather | solution.py:69
  718.4 18.9 multiply_convert_fusion.2
  745.5 107.5 %reduce-scatter.15.cloned.1.call-done = f32[512,768]{1,0:T(8,128)} async-done(((f32[2048,768]{1,0:T(8,128)}), f32[512,768]{1,0:T(8,128)}) %reduce-scatter.15.cloned.1.call-update) | async-done | bytes 1572880 | tf_op jit(solution)/shard_map/reduce_scatter | solution.py:78
  862.0 63.8 %all-gather.17.cloned.1.call-done = bf16[2048,768]{1,0:T(8,128)(2,1)} async-done(((bf16[512,768]{1,0:T(8,128)(2,1)}), bf16[2048,768]{1,0:T(8,128)(2,1)}) %all-gather.17.cloned.1.call-update) | async-done | bytes 3145744 | tf_op jit(solution)/shard_map/all_gather | solution.py:87
  925.8 11.2 convert_reduce_fusion
  943.3 109.5 %reduce-scatter.17.cloned.1.call-done = f32[512,768]{1,0:T(8,128)} async-done(((f32[2048,768]{1,0:T(8,128)}), f32[512,768]{1,0:T(8,128)}) %reduce-scatter.17.cloned.1.call-update) | async-done | bytes 1572880 | tf_op jit(solution)/shard_map/reduce_scatter | solution.py:78
  1060.0 64.0 %all-gather.19.cloned.1.call-done = bf16[2048,768]{1,0:T(8,128)(2,1)} async-done(((bf16[512,768]{1,0:T(8,128)(2,1)}), bf16[2048,768]{1,0:T(8,128)(2,1)}) %all-gather.19.cloned.1.call-update) | async-done | bytes 3145744 | tf_op jit(solution)/shard_map/all_gather | solution.py:87
  1131.4 9.3 fusion.28
  1140.7 11.3 multiply_reduce_fusion.1
  1152.0 7.0 multiply_convert_fusion.1
  1189.0 109.5 %reduce-scatter.19.cloned.1.call-done = f32[512,768]{1,0:T(8,128)} async-done(((f32[2048,768]{1,0:T(8,128)}), f32[512,768]{1,0:T(8,128)}) %reduce-scatter.19.cloned.1.call-update) | async-done | bytes 1572880 | tf_op jit(solution)/shard_map/reduce_scatter | solution.py:78
  1303.3 64.0 %all-gather.21.cloned.1.call-done = bf16[2048,768]{1,0:T(8,128)(2,1)} async-done(((bf16[512,768]{1,0:T(8,128)(2,1)}), bf16[2048,768]{1,0:T(8,128)(2,1)}) %all-gather.21.cloned.1.call-update) | async-done | bytes 3145744 | tf_op jit(solution)/shard_map/all_gather | solution.py:87
  1367.4 10.6 convert_reduce_fusion.1
  1384.3 109.5 %reduce-scatter.21.cloned.1.call-done = f32[512,768]{1,0:T(8,128)} async-done(((f32[2048,768]{1,0:T(8,128)}), f32[512,768]{1,0:T(8,128)}) %reduce-scatter.21.cloned.1.call-update) | async-done | bytes 1572880 | tf_op jit(solution)/shard_map/reduce_scatter | solution.py:78
  1499.7 64.0 %all-gather.23.cloned.1.call-done = bf16[2048,768]{1,0:T(8,128)(2,1)} async-done(((bf16[512,768]{1,0:T(8,128)(2,1)}), bf16[2048,768]{1,0:T(8,128)(2,1)}) %all-gather.23.cloned.1.call-update) | async-done | bytes 3145744 | tf_op jit(solution)/shard_map/all_gather | solution.py:87
  1567.4 7.1 fusion.29
  1574.6 11.0 multiply_reduce_fusion
  1585.7 7.0 multiply_convert_fusion
  1649.9 72.8 %reduce-scatter.23.cloned.1.call-done = f32[512,768]{1,0:T(8,128)} async-done(((f32[2048,768]{1,0:T(8,128)}), f32[512,768]{1,0:T(8,128)}) %reduce-scatter.23.cloned.1.call-update) | async-done | bytes 1572880 | tf_op jit(solution)/shard_map/reduce_scatter | solution.py:78
  1734.0 15.7 psum.137
  1749.8 42.5 %all-reduce.2 = (f32[768]{0:T(1024)}, f32[2,768]{1,0:T(2,128)}, f32[2,768]{1,0:T(2,128)}, f32[2,768]{1,0:T(2,128)}, f32[2,768]{1,0:T(2,128)}, /*index=5*/f32[2,7...) all-reduce(f32[768]{0:T(1024)S(1)} %get-tuple-element.69, ...), channel_id=1, replica_groups=mesh['batch'=8,'tensor'=4] {'batch','tensor'}, use_global_device_ids=true, to_apply=%region_38.39 | all-reduce | flops 10080 | bytes 80640 | tf_op jit(solution)/shard_map/psum | solution.py:310
  1793.9 125.0 %all-reduce.10.cloned.1.call-done = (f32[2,3,768,192]{2,3,1,0:T(8,128)}, f32[2,192,768]{2,1,0:T(8,128)}, f32[2,768,768]{2,1,0:T(8,128)}, f32[2,768,768]{2,1,0:T(8,128)}) async-done(((f32[2,3,768,192]{2,3,1,0:T(8,128)}, f32[2,192,768]{2,1,0:T(8,128)}, f32[2,768,768]{2,1,0:T(8,128)}, f32[2,768,768]{2,1,0:T(8,128)}), (f32[2,3,768,192]{2,3,1,0:T(8,128)}, f32[2,192,768]{2,1,0:T(8,128)}, ...) | async-done | bytes 14155792 | tf_op jit(solution)/shard_map/psum | solution.py:307
  1918.9 151.7 %all-reduce.8.cloned.1.call-done = (f32[48,768]{1,0:T(8,128)}, f32[256,768]{1,0:T(8,128)}, f32[1000,768]{1,0:T(8,128)}, f32[768,96]{0,1:T(8,128)}) async-done(((f32[48,768]{1,0:T(8,128)}, f32[256,768]{1,0:T(8,128)}, f32[1000,768]{1,0:T(8,128)}, f32[768,96]{0,1:T(8,128)}), (f32[48,768]{1,0:T(8,128)}, f32[256,768]{1,0:T(8,128)}, f32[1000,768]{1,0:T(8,128)}, f32[768,96]{0,1:T(8,128)})) %all-reduce.8.cloned.1.call-update) | async-done | bytes 4300816 | tf_op jit(solution)/shard_map/psum | solution.py:310
  (480 shorter events, 270.0 us)
Async XLA Ops:
  7.2 72.7 %all-gather.9.cloned.1.call-start = ((), (), s32[]{:S(2)}) async-start(), calls=%async_computation.8 | async-start | bytes 3932160 | tf_op jit(solution)/shard_map/all_gather | solution.py:69
  11.1 218.4 %copy-start.2 = (f32[512,768]{1,0:T(8,128)}, f32[512,768]{1,0:T(8,128)S(1)}, u32[]{:S(2)}) copy-start(f32[512,768]{1,0:T(8,128)S(1)} %get-tuple-element.112) | copy-start | bytes 4718596
  13.6 215.9 %reduce-scatter.9.cloned.1.call-start = ((), (), s32[]{:S(2)}) async-start(), calls=%async_computation.9 | async-start | bytes 7864320 | tf_op jit(solution)/shard_map/reduce_scatter | solution.py:78
  119.9 177.8 %all-gather.11.cloned.1.call-start = ((), (), s32[]{:S(2)}) async-start(), calls=%async_computation.10 | async-start | bytes 3932160 | tf_op jit(solution)/shard_map/all_gather | solution.py:69
  120.6 111.0 %copy-start.70 = (f32[768]{0:T(1024)}, f32[768]{0:T(1024)S(1)}, u32[]{:S(2)}) copy-start(f32[768]{0:T(1024)S(1)} %get-tuple-element.132) | copy-start | bytes 9220
  231.2 85.4 %copy-start.74 = (f32[512]{0:T(512)}, f32[512]{0:T(512)S(1)}, u32[]{:S(2)}) copy-start(f32[512]{0:T(512)S(1)} %broadcast_multiply_fusion.3) | copy-start | bytes 6148
  231.6 85.1 %copy-start.84 = (f32[512]{0:T(512)}, f32[512]{0:T(512)S(1)}, u32[]{:S(2)}) copy-start(f32[512]{0:T(512)S(1)} %multiply_reduce_fusion.15) | copy-start | bytes 6148
  231.6 85.1 %copy-start.79 = (f32[512]{0:T(512)}, f32[512]{0:T(512)S(1)}, u32[]{:S(2)}) copy-start(f32[512]{0:T(512)S(1)} %fusion.102) | copy-start | bytes 6148
  233.6 198.7 %reduce-scatter.11.cloned.1.call-start = ((), (), s32[]{:S(2)}) async-start(), calls=%async_computation.11 | async-start | bytes 7864320 | tf_op jit(solution)/shard_map/reduce_scatter | solution.py:78
  233.7 83.0 %copy-start.99 = (f32[768]{0:T(1024)}, f32[768]{0:T(1024)S(1)}, u32[]{:S(2)}) copy-start(f32[768]{0:T(1024)S(1)} %get-tuple-element.39) | copy-start | bytes 9220
  322.8 109.6 %copy-start.5 = (f32[512,768]{1,0:T(8,128)S(1)}, f32[512,768]{1,0:T(8,128)}, u32[]{:S(2)}) copy-start(f32[512,768]{1,0:T(8,128)} %copy-done.4) | copy-start | bytes 4718596
  322.8 177.7 %all-gather.13.cloned.1.call-start = ((), (), s32[]{:S(2)}) async-start(), calls=%async_computation.12 | async-start | bytes 3932160 | tf_op jit(solution)/shard_map/all_gather | solution.py:69
  436.4 213.8 %reduce-scatter.13.cloned.1.call-start = ((), (), s32[]{:S(2)}) async-start(), calls=%async_computation.13 | async-start | bytes 7864320 | tf_op jit(solution)/shard_map/reduce_scatter | solution.py:78
  540.6 109.6 %copy-start.8 = (f32[512,768]{1,0:T(8,128)S(1)}, f32[512,768]{1,0:T(8,128)}, u32[]{:S(2)}) copy-start(f32[512,768]{1,0:T(8,128)} %copy-done.7) | copy-start | bytes 4718596
  540.6 177.8 %all-gather.15.cloned.1.call-start = ((), (), s32[]{:S(2)}) async-start(), calls=%async_computation.14 | async-start | bytes 3932160 | tf_op jit(solution)/shard_map/all_gather | solution.py:69
  654.3 198.7 %reduce-scatter.15.cloned.1.call-start = ((), (), s32[]{:S(2)}) async-start(), calls=%async_computation.15 | async-start | bytes 7864320 | tf_op jit(solution)/shard_map/reduce_scatter | solution.py:78
  743.5 182.4 %all-gather.17.cloned.1.call-start = ((), (), s32[]{:S(2)}) async-start(), calls=%async_computation.16 | async-start | bytes 3932160 | tf_op jit(solution)/shard_map/all_gather | solution.py:87
  861.7 191.2 %reduce-scatter.17.cloned.1.call-start = ((), (), s32[]{:S(2)}) async-start(), calls=%async_computation.17 | async-start | bytes 7864320 | tf_op jit(solution)/shard_map/reduce_scatter | solution.py:78
  943.3 180.8 %all-gather.19.cloned.1.call-start = ((), (), s32[]{:S(2)}) async-start(), calls=%async_computation.18 | async-start | bytes 3932160 | tf_op jit(solution)/shard_map/all_gather | solution.py:87
  1060.0 238.5 %reduce-scatter.19.cloned.1.call-start = ((), (), s32[]{:S(2)}) async-start(), calls=%async_computation.19 | async-start | bytes 7864320 | tf_op jit(solution)/shard_map/reduce_scatter | solution.py:78
  1188.9 178.4 %all-gather.21.cloned.1.call-start = ((), (), s32[]{:S(2)}) async-start(), calls=%async_computation.20 | async-start | bytes 3932160 | tf_op jit(solution)/shard_map/all_gather | solution.py:87
  1303.3 190.5 %reduce-scatter.21.cloned.1.call-start = ((), (), s32[]{:S(2)}) async-start(), calls=%async_computation.21 | async-start | bytes 7864320 | tf_op jit(solution)/shard_map/reduce_scatter | solution.py:78
  1384.2 109.6 %copy-start.6 = (f32[512,768]{1,0:T(8,128)S(1)}, f32[512,768]{1,0:T(8,128)}, u32[]{:S(2)}) copy-start(f32[512,768]{1,0:T(8,128)} %copy-done.4) | copy-start | bytes 4718596
  1384.2 109.6 %copy-start.71 = (f32[768]{0:T(1024)S(1)}, f32[768]{0:T(1024)}, u32[]{:S(2)}) copy-start(f32[768]{0:T(1024)} %copy-done.70) | copy-start | bytes 9220
  1384.2 109.6 %copy-start.75 = (f32[512]{0:T(512)S(1)}, f32[512]{0:T(512)}, u32[]{:S(2)}) copy-start(f32[512]{0:T(512)} %copy-done.74) | copy-start | bytes 6148
  1384.2 109.6 %copy-start.80 = (f32[512]{0:T(512)S(1)}, f32[512]{0:T(512)}, u32[]{:S(2)}) copy-start(f32[512]{0:T(512)} %copy-done.79) | copy-start | bytes 6148
  1384.2 111.8 %copy-start.85 = (f32[512]{0:T(512)S(1)}, f32[512]{0:T(512)}, u32[]{:S(2)}) copy-start(f32[512]{0:T(512)} %copy-done.84) | copy-start | bytes 6148
  1384.2 179.5 %all-gather.23.cloned.1.call-start = ((), (), s32[]{:S(2)}) async-start(), calls=%async_computation.22 | async-start | bytes 3932160 | tf_op jit(solution)/shard_map/all_gather | solution.py:87
  1499.7 223.0 %reduce-scatter.23.cloned.1.call-start = ((), (), s32[]{:S(2)}) async-start(), calls=%async_computation.23 | async-start | bytes 7864320 | tf_op jit(solution)/shard_map/reduce_scatter | solution.py:78
  1613.1 305.7 %all-reduce.10.cloned.1.call-start = ((), (), s32[]{:S(2)}) async-start(), calls=%async_computation.25 | async-start | bytes 28311552 | tf_op jit(solution)/shard_map/psum | solution.py:307
  1647.8 77.1 %copy-start.83 = (f32[512]{0:T(512)S(1)}, f32[512]{0:T(512)}, u32[]{:S(2)}) copy-start(f32[512]{0:T(512)} %copy-done.82) | copy-start | bytes 6148
  1647.8 422.8 %all-reduce.8.cloned.1.call-start = ((), (), s32[]{:S(2)}) async-start(), calls=%async_computation.24 | async-start | bytes 8601600 | tf_op jit(solution)/shard_map/psum | solution.py:310
  (117 other events, 1191.7 us)
Sparse Core Ops, SparseCore 0:
  13.7 66.1 all-gather.8
  120.0 109.4 reduce-scatter.8
  233.8 63.9 all-gather.10
  322.9 109.4 reduce-scatter.10
  436.5 63.9 all-gather.12
  540.8 109.4 reduce-scatter.12
  654.4 63.9 all-gather.14
  743.6 109.4 reduce-scatter.14
  861.8 63.9 all-gather.16
  943.4 109.4 reduce-scatter.16
  1060.1 63.9 all-gather.18
  1189.0 109.4 reduce-scatter.18
  1303.4 63.9 all-gather.20
  1384.3 109.4 reduce-scatter.20
  1499.8 63.9 all-gather.22
  1613.2 109.4 reduce-scatter.22
  1727.2 191.6 all-reduce.9
  1926.0 144.4 all-reduce.7
where the time goes:
time: 2110 us; the launch traced here: 2090 us
  waiting for transfers between devices  1620 us (77%)
  matrix products  213 us (10%)
  local copies, waits for them, and re-layouts  100 us (5%)
  other arithmetic  82.5 us (4%)
  blocking collectives  58.2 us (3%)
    reduce_scatter x8, waiting for transfers between devices, narrow(): lax.psum_scatter(term_rows(jnp.int32(0), shard_count * lax.axis_size('ten...  836 us
    all_gather x4, waiting for transfers between devices, gather_grad(): return lax.all_gather(grad_low, 'tensor', axis=0, tiled=True)  256 us
    all_gather x4, waiting for transfers between devices, widen_rows(): gathered = lax.all_gather(shard_low, 'tensor', axis=0, tiled=True)  254 us
    psum x1, waiting for transfers between devices, shards(): lax.psum((embed_weight_grad, embed_bias_grad, position_grad, class_grad,...  152 us
    psum x1, waiting for transfers between devices, shards(): lax.psum((split_stack[0], split_stack[1], split_stack[2], split_stack[3],...  125 us
    dot_general x9, matrix products, product(): return jnp.dot(former, latter, preferred_element_type=jnp.float32)  56.9 us
    unnamed x278, local copies, waits for them, and re-layouts  48.6 us
    psum x1, blocking collectives, shards(): lax.psum((embed_weight_grad, embed_bias_grad, position_grad, class_grad,...  42.5 us
  transfers between devices with their start and end apart: 18, of which 18 were waited for; matrix products, arithmetic and copies ran while one was open for 2% of the time, Pallas kernels for 0%

commit v1 on v0

v1 whole, which is shorter than its diff:
```python
import functools

import jax
import jax.numpy as jnp
from jax import lax
from jax.experimental import pallas as pl
from jax.experimental.pallas import tpu as pltpu
from jax.sharding import PartitionSpec as P

D = 768
HEAD_DIM = 64
P_SIZE = 256
PV = 48
CLASSES = 1000
NL = 2


EPSILON = 1e-05
NEGATIVE = -1000000000.0
HIGHEST = lax.Precision.HIGHEST


def layer_norm(values, norm_gain, norm_offset):
    center = values - jnp.mean(values, axis=-1, keepdims=True)
    spread = jnp.mean(center * center, axis=-1, keepdims=True)
    return center * lax.rsqrt(spread + EPSILON) * norm_gain + norm_offset


def norm_backward(values, norm_gain, norm_offset, upstream):
    outputs, pullback = jax.vjp(layer_norm, values, norm_gain, norm_offset)
    return pullback(upstream)


def gelu_exact(values):
    return jax.nn.gelu(values, approximate=False)


def product(former, latter):
    return jnp.dot(former, latter, preferred_element_type=jnp.float32)


def product_back(former, latter):
    return lax.dot_general(
        former, latter, (((1,), (1,)), ((), ())), preferred_element_type=jnp.float32
    )


def contract_rows(former, latter):
    return lax.dot_general(
        former, latter, (((0,), (0,)), ((), ())), preferred_element_type=jnp.float32
    )


def precise_rows(former, latter):
    return lax.dot_general(
        former,
        latter,
        (((0,), (0,)), ((), ())),
        precision=HIGHEST,
        preferred_element_type=jnp.float32,
    )


def build_allowed(mask_rows, span):
    row_index = lax.broadcasted_iota(jnp.int32, (span, span), 0)
    col_index = lax.broadcasted_iota(jnp.int32, (span, span), 1)
    causal = (row_index // P_SIZE == col_index // P_SIZE) & (col_index <= row_index)
    key_valid = mask_rows.reshape(mask_rows.shape[0] // span, 1, span) > 0
    return causal[None] & (key_valid | (row_index == col_index)[None])


def gather_rows(parts):
    batch_count = lax.axis_size("batch")
    batch_index = lax.axis_index("batch")
    pieces = []
    for part in parts:
        rows = part.shape[0] // batch_count
        pieces.append(lax.dynamic_slice_in_dim(part, batch_index * rows, rows, 0))
    piece = jnp.concatenate(pieces, axis=0)
    group = lax.all_gather(piece, "tensor", axis=0)
    whole = lax.all_gather(group, "batch", axis=0)
    results = []
    begin = 0
    for entry in pieces:
        results.append(whole[:, :, begin : begin + entry.shape[0]])
        begin += entry.shape[0]
    return results


def reduce_rows(parts):
    joined = jnp.concatenate([part.astype(jnp.bfloat16) for part in parts], axis=2)
    over_batch = lax.psum_scatter(joined, "batch", scatter_dimension=0)
    own = lax.psum_scatter(over_batch, "tensor", scatter_dimension=0)
    whole = lax.all_gather(own, "batch", axis=0)
    results = []
    begin = 0
    for part in parts:
        results.append(whole[:, begin : begin + part.shape[2]])
        begin += part.shape[2]
    return results


def to_tensor_major(blocks):
    return jnp.swapaxes(blocks, 0, 1).reshape(-1, blocks.shape[-1])


def to_batch_major(rows):
    batch_count = lax.axis_size("batch")
    tensor_count = lax.axis_size("tensor")
    return jnp.swapaxes(rows.reshape(tensor_count, batch_count, -1, rows.shape[-1]), 0, 1)


def split_blocks(rows):
    batch_count = lax.axis_size("batch")
    tensor_count = lax.axis_size("tensor")
    return rows.reshape(batch_count, tensor_count, -1, rows.shape[-1])


MESH = pl.DeviceIdType.MESH
SWAP_TENSOR = (1, 2, 3)


def place():
    batch_index = lax.axis_index("batch")
    tensor_index = lax.axis_index("tensor")
    return (batch_index // 4, batch_index // 2 % 2, batch_index % 2, tensor_index)


def device_at(y, x, core, z):
    return (y * 4 + x * 2 + core, z)


def flipped(index, bits):
    high, low = index // 2, index % 2
    if bits & 2:
        high = 1 - high
    if bits & 1:
        low = 1 - low
    return high * 2 + low


def greet(devices):
    barrier = pltpu.get_barrier_semaphore()
    for device in devices:
        pl.semaphore_signal(barrier, inc=1, device_id=device, device_id_type=MESH)
    pl.semaphore_wait(barrier, len(devices))


def partners():
    y, x, core, z = place()
    devices = [device_at(y, x, core, flipped(z, bits)) for bits in SWAP_TENSOR]
    devices.append(device_at(y, 1 - x, core, z))
    devices.append(device_at(1 - y, x, core, z))
    devices.append(device_at(y, x, 1 - core, z))
    return devices


def halves(count):
    return (slice(0, (count + 1) // 2), slice((count + 1) // 2, count))


class Copies:
    def __init__(self, send_sems):
        self.send_sems = send_sems
        self.count = 0
        self.sent = []

    def send(self, source, target, recv_sem, device, keep=True):
        copy = pltpu.make_async_remote_copy(
            src_ref=source,
            dst_ref=target,
            send_sem=self.send_sems.at[self.count],
            recv_sem=recv_sem,
            device_id=device,
            device_id_type=MESH,
        )
        self.count += 1
        copy.start()
        if keep:
            self.sent.append(copy)
        return copy

    def finish(self):
        for copy in self.sent:
            copy.wait_send()


def wait_arrival(target, recv_sem, send_sem, device):
    pltpu.make_async_remote_copy(
        src_ref=target,
        dst_ref=target,
        send_sem=send_sem,
        recv_sem=recv_sem,
        device_id=device,
        device_id_type=MESH,
    ).wait_recv()


def spread_piece(ref, lead, b):
    if len(ref.shape) == len(lead) + 4:
        return ref.at[(*lead, slice(None), b)]
    return ref.at[(*lead, b)]


def half_piece(ref, lead, b, side):
    if len(ref.shape) == len(lead) + 4:
        return ref.at[(*lead, halves(ref.shape[len(lead)])[side], b)]
    return ref.at[(*lead, b, halves(ref.shape[len(lead) + 1])[side])]


def gather_kernel(layer_count, *refs):
    per_layer = 4
    units = layer_count * per_layer
    shards = refs[:units]
    bias = refs[units]
    fulls = refs[units + 1 : 2 * units + 1]
    bias_full = refs[2 * units + 1]
    send_sems, z_sems, xy_sems, core_sems, local_sems, bias_sems, spare = refs[2 * units + 2 :]
    y, x, core, z = place()
    b = y * 4 + x * 2 + core
    over_x = y * 4 + (1 - x) * 2 + core
    over_y = (1 - y) * 4 + x * 2 + core
    corner = (1 - y) * 4 + (1 - x) * 2 + core
    at_x = device_at(y, 1 - x, core, z)
    at_y = device_at(1 - y, x, core, z)
    at_core = device_at(y, x, 1 - core, z)
    middle = (z + 1) // 2 % 2
    near = flipped(z, 1)
    across = 3 - z
    far = (z + 2) % 4
    at_near = device_at(y, x, core, near)
    at_across = device_at(y, x, core, across)
    order = (
        near,
        middle * across + (1 - middle) * far,
        middle * far + (1 - middle) * across,
    )
    greet(partners())
    copies = Copies(send_sems)
    conditional = []
    locals_ = []
    for unit in range(units):
        copy = pltpu.make_async_copy(shards[unit], fulls[unit].at[z], local_sems.at[unit])
        copy.start()
        locals_.append(copy)
    copy = pltpu.make_async_copy(bias, bias_full.at[z], local_sems.at[units])
    copy.start()
    locals_.append(copy)
    for entry, bits in enumerate(SWAP_TENSOR):
        copies.send(
            bias,
            bias_full.at[z],
            bias_sems.at[entry],
            device_at(y, x, core, flipped(z, bits)),
        )

    def of_layer(layer):
        return range(layer * per_layer, (layer + 1) * per_layer)

    def send_if_middle(source, target, recv_sem, device):
        slot = send_sems.at[copies.count]
        copies.count += 1
        copy = pltpu.make_async_remote_copy(
            src_ref=source,
            dst_ref=target,
            send_sem=slot,
            recv_sem=recv_sem,
            device_id=device,
            device_id_type=MESH,
        )

        @pl.when(middle == 1)
        def _():
            copy.start()

        conditional.append(copy)

    def begin(layer):
        for unit in of_layer(layer):
            mine = spread_piece(shards[unit], (), b)
            target = spread_piece(fulls[unit], (z,), b)
            copies.send(mine, target, z_sems.at[unit, z], at_near)
            send_if_middle(mine, target, z_sems.at[unit, z], at_across)

    def take_z(layer, step):
        t = order[step]
        for unit in of_layer(layer):
            piece = spread_piece(fulls[unit], (t,), b)
            wait_arrival(piece, z_sems.at[unit, t], spare.at[0], at_near)
            send_if_middle(
                piece, piece, z_sems.at[unit, t], at_across if step == 0 else at_near
            )
        for unit in of_layer(layer):
            piece = spread_piece(fulls[unit], (t,), b)
            copies.send(piece, piece, xy_sems.at[unit, step, 0], at_x)
            copies.send(piece, piece, xy_sems.at[unit, step, 1], at_y)
            copies.send(piece, piece, core_sems.at[unit, step, 0], at_core)

    def take_xy(layer, step):
        t = order[step]
        for unit in of_layer(layer):
            piece = spread_piece(fulls[unit], (t,), over_x)
            wait_arrival(piece, xy_sems.at[unit, step, 0], spare.at[0], at_x)
            first = half_piece(fulls[unit], (t,), over_x, 0)
            copies.send(first, first, xy_sems.at[unit, step, 2], at_y)
            copies.send(piece, piece, core_sems.at[unit, step, 1], at_core)
        for unit in of_layer(layer):
            piece = spread_piece(fulls[unit], (t,), over_y)
            wait_arrival(piece, xy_sems.at[unit, step, 1], spare.at[0], at_y)
            second = half_piece(fulls[unit], (t,), over_y, 1)
            copies.send(second, second, xy_sems.at[unit, step, 3], at_x)
            copies.send(piece, piece, core_sems.at[unit, step, 2], at_core)

    def take_corner(layer, step):
        t = order[step]
        for unit in of_layer(layer):
            first = half_piece(fulls[unit], (t,), corner, 0)
            second = half_piece(fulls[unit], (t,), corner, 1)
            wait_arrival(first, xy_sems.at[unit, step, 2], spare.at[0], at_y)
            wait_arrival(second, xy_sems.at[unit, step, 3], spare.at[0], at_x)
            piece = spread_piece(fulls[unit], (t,), corner)
            copies.send(piece, piece, core_sems.at[unit, step, 3], at_core)

    def take_core(layer, step):
        t = order[step]
        for unit in of_layer(layer):
            for entry, owner in enumerate((b, over_x, over_y, corner)):
                other = owner + 1 - 2 * core
                piece = spread_piece(fulls[unit], (t,), other)
                wait_arrival(piece, core_sems.at[unit, step, entry], spare.at[0], at_core)

    begin(0)
    for layer in range(layer_count):
        take_z(layer, 0)
        take_z(layer, 1)
        if layer:
            take_corner(layer - 1, 1)
        take_xy(layer, 0)
        take_z(layer, 2)
        if layer + 1 < layer_count:
            begin(layer + 1)
        if layer:
            take_corner(layer - 1, 2)
        take_xy(layer, 1)
        take_corner(layer, 0)
        take_xy(layer, 2)
    take_corner(layer_count - 1, 1)
    take_corner(layer_count - 1, 2)
    for layer in range(layer_count):
        for step in range(3):
            take_core(layer, step)
    for entry, bits in enumerate(SWAP_TENSOR):
        wait_arrival(
            bias_full.at[flipped(z, bits)],
            bias_sems.at[entry],
            spare.at[0],
            device_at(y, x, core, flipped(z, bits)),
        )
    for copy in locals_:
        copy.wait()
    copies.finish()

    @pl.when(middle == 1)
    def _():
        for copy in conditional:
            copy.wait_send()


def gather_all(shards, bias):
    units = len(shards)
    outs = [jax.ShapeDtypeStruct((4, *shard.shape), shard.dtype) for shard in shards]
    outs.append(jax.ShapeDtypeStruct((4, *bias.shape), bias.dtype))
    vmem = pl.BlockSpec(memory_space=pltpu.VMEM)
    anywhere = pl.BlockSpec(memory_space=pl.ANY)
    dma = pltpu.SemaphoreType.DMA
    return pl.pallas_call(
        functools.partial(gather_kernel, units // 4),
        out_shape=outs,
        in_specs=[vmem] * (units + 1),
        out_specs=[anywhere] * (units + 1),
        scratch_shapes=[
            dma((3 + units * (2 + 3 * 9),)),
            dma((units, 4)),
            dma((units, 3, 4)),
            dma((units, 3, 4)),
            dma((units + 1,)),
            dma((3,)),
            dma((1,)),
        ],
        compiler_params=pltpu.CompilerParams(collective_id=0, has_side_effects=True),
        name="gather_weights",
    )(*shards, bias)


def add_slab(target, addend):
    target[...] = (target[...].astype(jnp.float32) + addend[...].astype(jnp.float32)).astype(
        target.dtype
    )


ITEM_ORDER = (0, 2, 1, 3)


def reduce_kernel(groups, spread_all, *refs):
    units = sum(len(group) for group in groups)
    grads = refs[:units]
    outs = refs[units : 2 * units]
    own, got_core, got_one, got_two, got_z, result = (
        refs[(2 + entry) * units : (3 + entry) * units] for entry in range(6)
    )
    send_sems, load_sems, step_sems, z_sems, spread_sems, core_sems, all_sems, spare = refs[
        8 * units :
    ]
    y, x, core, z = place()
    at_x = device_at(y, 1 - x, core, z)
    at_y = device_at(1 - y, x, core, z)
    at_core = device_at(y, x, 1 - core, z)
    greet(partners())
    copies = Copies(send_sems)
    conditional = []
    items = [(group, t) for group in groups for t in ITEM_ORDER]
    for group, t in items:
        for unit in group:
            grad = grads[unit]
            copies.send(
                grad.at[t, :, :, :, 1 - core],
                got_core[unit].at[t],
                step_sems.at[unit, 0, t],
                at_core,
            )
            pltpu.make_async_copy(
                grad.at[t, :, :, :, core], own[unit].at[t], load_sems.at[unit, t]
            ).start()

    def take_core_sum(group, t):
        for unit in group:
            grad = grads[unit]
            mine, other = own[unit], got_core[unit]
            pltpu.make_async_copy(
                grad.at[t, :, :, :, core], mine.at[t], load_sems.at[unit, t]
            ).wait()
            wait_arrival(other.at[t], step_sems.at[unit, 0, t], spare.at[0], at_core)
            count = mine.shape[1] * 4

            def body(entry, carry):
                spot = (t, entry // 4, entry // 2 % 2, entry % 2)
                add_slab(mine.at[spot], other.at[spot])
                return carry

            lax.fori_loop(0, count, body, 0)
            if t < 2:
                copies.send(
                    mine.at[t, :, :, 1 - x], got_one[unit].at[t], step_sems.at[unit, 1, t], at_x
                )
            else:
                copies.send(
                    mine.at[t, :, 1 - y], got_one[unit].at[t], step_sems.at[unit, 1, t], at_y
                )

    def take_one(group, t):
        for unit in group:
            mine, other = own[unit], got_one[unit]
            wait_arrival(
                other.at[t], step_sems.at[unit, 1, t], spare.at[0], at_x if t < 2 else at_y
            )
            count = mine.shape[1] * 2

            def body(entry, carry):
                first, second = entry // 2, entry % 2
                if t < 2:
                    add_slab(mine.at[t, first, second, x], other.at[t, first, second])
                else:
                    add_slab(mine.at[t, first, y, second], other.at[t, first, second])
                return carry

            lax.fori_loop(0, count, body, 0)
            if t < 2:
                copies.send(
                    mine.at[t, :, 1 - y, x], got_two[unit].at[t], step_sems.at[unit, 2, t], at_y
                )
            else:
                copies.send(
                    mine.at[t, :, y, 1 - x], got_two[unit].at[t], step_sems.at[unit, 2, t], at_x
                )

    def take_two(group, t):
        for unit in group:
            mine, other = own[unit], got_two[unit]
            wait_arrival(
                other.at[t], step_sems.at[unit, 2, t], spare.at[0], at_y if t < 2 else at_x
            )

            def body(entry, carry):
                add_slab(mine.at[t, entry, y, x], other.at[t, entry])
                return carry

            lax.fori_loop(0, mine.shape[1], body, 0)
            copy = pltpu.make_async_remote_copy(
                src_ref=mine.at[t, :, y, x],
                dst_ref=got_z[unit].at[z],
                send_sem=send_sems.at[copies.count],
                recv_sem=z_sems.at[unit, z],
                device_id=device_at(y, x, core, t),
                device_id_type=MESH,
            )
            copies.count += 1

            @pl.when(z != t)
            def _():
                copy.start()

            conditional.append((t, copy))

    def spot_of(unit, where):
        return outs[unit].at[(z, slice(None), *where)]

    def half_spot(unit, where, side):
        count = outs[unit].shape[1]
        if count > 1:
            return outs[unit].at[(z, halves(count)[side], *where)]
        return outs[unit].at[(z, slice(None), *where, halves(outs[unit].shape[5])[side])]

    def take_z(group):
        for unit in group:
            mine, other, total = own[unit], got_z[unit], result[unit]
            for bits in SWAP_TENSOR:
                t = flipped(z, bits)
                wait_arrival(
                    other.at[t], z_sems.at[unit, t], spare.at[0], device_at(y, x, core, t)
                )

            def body(entry, carry):
                value = mine[z, entry, y, x].astype(jnp.float32)
                for bits in SWAP_TENSOR:
                    value = value + other[flipped(z, bits), entry].astype(jnp.float32)
                total[entry] = value.astype(total.dtype)
                return carry

            lax.fori_loop(0, mine.shape[1], body, 0)
            spot = spot_of(unit, (y, x, core))
            pltpu.make_async_copy(total, spot, load_sems.at[unit, 4]).start()
            copies.send(total, spot, spread_sems.at[unit, 0], at_x)
            copies.send(total, spot, spread_sems.at[unit, 1], at_y)
            copies.send(total, spot, core_sems.at[unit, 0], at_core)

    def take_spread(group):
        for unit in group:
            spot = spot_of(unit, (y, 1 - x, core))
            wait_arrival(spot, spread_sems.at[unit, 0], spare.at[0], at_x)
            first = half_spot(unit, (y, 1 - x, core), 0)
            copies.send(first, first, spread_sems.at[unit, 2], at_y)
            copies.send(spot, spot, core_sems.at[unit, 1], at_core)
            spot = spot_of(unit, (1 - y, x, core))
            wait_arrival(spot, spread_sems.at[unit, 1], spare.at[0], at_y)
            second = half_spot(unit, (1 - y, x, core), 1)
            copies.send(second, second, spread_sems.at[unit, 3], at_x)
            copies.send(spot, spot, core_sems.at[unit, 2], at_core)

    def take_corner(group):
        for unit in group:
            where = (1 - y, 1 - x, core)
            wait_arrival(half_spot(unit, where, 0), spread_sems.at[unit, 2], spare.at[0], at_y)
            wait_arrival(half_spot(unit, where, 1), spread_sems.at[unit, 3], spare.at[0], at_x)
            spot = spot_of(unit, where)
            copies.send(spot, spot, core_sems.at[unit, 3], at_core)

    def take_last(group):
        for unit in group:
            pltpu.make_async_copy(
                result[unit], spot_of(unit, (y, x, core)), load_sems.at[unit, 4]
            ).wait()
            for entry, where in enumerate(((y, x), (y, 1 - x), (1 - y, x), (1 - y, 1 - x))):
                spot = spot_of(unit, (*where, 1 - core))
                wait_arrival(spot, core_sems.at[unit, entry], spare.at[0], at_core)

    def run(step):
        if step < len(items):
            take_core_sum(*items[step])
        if 0 <= step - 1 < len(items):
            take_one(*items[step - 1])
        if 0 <= step - 2 < len(items):
            take_two(*items[step - 2])
        for index, group in enumerate(groups):
            last = 4 * index + 3
            if step == last + 4:
                take_z(group)
            if step == last + 5:
                take_spread(group)
            if step == last + 6:
                take_corner(group)

    for step in range(len(items) + 6):
        run(step)
    for group in groups:
        take_last(group)
    for entry, unit in enumerate(spread_all):
        for bits in SWAP_TENSOR:
            copies.send(
                outs[unit].at[z],
                outs[unit].at[z],
                all_sems.at[entry, bits],
                device_at(y, x, core, flipped(z, bits)),
            )
        for bits in SWAP_TENSOR:
            t = flipped(z, bits)
            wait_arrival(
                outs[unit].at[t], all_sems.at[entry, bits], spare.at[0], device_at(y, x, core, t)
            )
    copies.finish()
    for t, copy in conditional:

        @pl.when(z != t)
        def _(copy=copy):
            copy.wait_send()


def reduce_all(grads, groups, spread_all):
    units = len(grads)
    scratch = []
    for lead in ((4, 2, 2), (4, 2, 2), (4, 2), (4,), (4,), ()):
        for grad in grads:
            count, rows = grad.shape[1], grad.shape[5]
            shape = lead[:1] + (count,) + lead[1:] + (rows, D)
            scratch.append(pltpu.VMEM(shape, jnp.bfloat16))
    dma = pltpu.SemaphoreType.DMA
    anywhere = pl.BlockSpec(memory_space=pl.ANY)
    return pl.pallas_call(
        functools.partial(reduce_kernel, groups, spread_all),
        out_shape=[jax.ShapeDtypeStruct(grad.shape, grad.dtype) for grad in grads],
        in_specs=[anywhere] * units,
        out_specs=[anywhere] * units,
        scratch_shapes=scratch
        + [
            dma((units * 24 + 3 * len(spread_all),)),
            dma((units, 5)),
            dma((units, 3, 4)),
            dma((units, 4)),
            dma((units, 4)),
            dma((units, 4)),
            dma((max(len(spread_all), 1), 4)),
            dma((1,)),
        ],
        compiler_params=pltpu.CompilerParams(
            collective_id=1, has_side_effects=True, vmem_limit_bytes=62 * 1024 * 1024
        ),
        name="reduce_gradients",
    )(*grads)


def fast_mesh():
    return lax.axis_size("batch") == 8 and lax.axis_size("tensor") == 4


def gather_weights(shards, bias):
    if not fast_mesh():
        wholes = [to_tensor_major(blocks) for blocks in gather_rows(shards)]
        return (wholes, lax.all_gather(bias, "tensor", axis=0))
    parts = []
    for shard in shards:
        rows = shard.shape[0]
        parts.append(shard.reshape(8, -1, D) if rows == D else shard.reshape(-1, 8, 8, D))
    results = gather_all(parts, jnp.pad(bias, ((0, 8 - NL), (0, 0))))
    return ([whole.reshape(-1, D) for whole in results[:-1]], results[-1][:, :NL])


def reduce_weights(grads, small):
    if not fast_mesh():
        sums = reduce_rows([to_batch_major(grad) for grad in grads] + [split_blocks(small)])
        small_sum = lax.all_gather(sums[-1], "tensor", axis=1).reshape(-1, D)
        return ([entry.reshape(-1, D) for entry in sums[:-1]], small_sum)
    tensor_index = lax.axis_index("tensor")
    parts = []
    for grad in grads:
        count = 1 if grad.shape[0] == 4 * D else grad.shape[0] // 256
        parts.append(grad.reshape(4, count, 2, 2, 2, -1, D))
    parts.append(small.astype(jnp.bfloat16).reshape(4, 1, 2, 2, 2, -1, D))
    groups = ((4, 5, 6, 7), (0, 1, 2, 3, 8))
    sums = reduce_all(parts, groups, (8,))
    own = [lax.dynamic_index_in_dim(entry, tensor_index, 0, keepdims=False) for entry in sums[:-1]]
    return ([entry.reshape(-1, D) for entry in own], sums[-1].reshape(-1, D))


def head_blocks(qkv_low, tensor_count):
    images = qkv_low.shape[0] // P_SIZE
    blocks = qkv_low.reshape(images, P_SIZE, tensor_count, 3, -1, HEAD_DIM)
    blocks = jnp.transpose(blocks, (3, 0, 2, 4, 1, 5))
    return blocks.reshape(3, images, -1, P_SIZE, HEAD_DIM)


def head_rows(mixed):
    images, heads = mixed.shape[:2]
    return jnp.transpose(mixed, (0, 2, 1, 3)).reshape(images * P_SIZE, heads * HEAD_DIM)


def block_scores(blocks, allowed):
    queries, keys, values = blocks[0], blocks[1], blocks[2]
    scores = jnp.einsum("bhqd,bhkd->bhqk", queries, keys, preferred_element_type=jnp.float32) * (
        HEAD_DIM ** (-0.5)
    )
    scores = jnp.where(allowed[:, None], scores, NEGATIVE)
    return (queries, keys, values, scores)


def attend(blocks, allowed):
    queries, keys, values, scores = block_scores(blocks, allowed)
    log_total = jax.nn.logsumexp(scores, axis=-1, keepdims=True)
    probs_low = jnp.exp(scores - log_total).astype(jnp.bfloat16)
    mixed = jnp.einsum("bhqk,bhkd->bhqd", probs_low, values, preferred_element_type=jnp.float32)
    return (head_rows(mixed.astype(jnp.bfloat16)), log_total)


def attend_back(blocks, allowed, log_total, grad_mixed, tensor_count):
    queries, keys, values, scores = block_scores(blocks, allowed)
    probs_full = jnp.exp(scores - log_total)
    probs_low = probs_full.astype(jnp.bfloat16)
    images = queries.shape[0]
    grad_out = jnp.transpose(grad_mixed.reshape(images, P_SIZE, -1, HEAD_DIM), (0, 2, 1, 3))
    grad_values = jnp.einsum(
        "bhqk,bhqd->bhkd", probs_low, grad_out, preferred_element_type=jnp.float32
    )
    grad_probs = jnp.einsum("bhqd,bhkd->bhqk", grad_out, values, preferred_element_type=jnp.float32)
    inner_sum = jnp.sum(probs_full * grad_probs, axis=-1, keepdims=True)
    grad_scores = (probs_full * (grad_probs - inner_sum)).astype(jnp.bfloat16)
    scaling = HEAD_DIM ** (-0.5)
    grad_queries = (
        jnp.einsum("bhqk,bhkd->bhqd", grad_scores, keys, preferred_element_type=jnp.float32)
        * scaling
    )
    grad_keys = (
        jnp.einsum("bhqk,bhqd->bhkd", grad_scores, queries, preferred_element_type=jnp.float32)
        * scaling
    )
    stacked = jnp.stack([grad_queries, grad_keys, grad_values]).astype(jnp.bfloat16)
    stacked = stacked.reshape(3, images, tensor_count, -1, P_SIZE, HEAD_DIM)
    return jnp.transpose(stacked, (1, 4, 2, 0, 3, 5)).reshape(images * P_SIZE, -1)


def shards(
    patches,
    valid_mask,
    class_ids,
    embed_weight,
    embed_bias,
    position_table,
    class_table,
    attn_gain,
    attn_offset,
    attend_weight,
    merge_weight,
    mlp_gain,
    mlp_offset,
    up_weight,
    up_bias,
    down_weight,
    down_bias,
    final_gain,
    final_offset,
    head_weight,
    head_bias,
    latent_cot,
    logdet_cot,
):
    shard_count = patches.shape[0]
    local_images = shard_count // P_SIZE
    tensor_index = lax.axis_index("tensor")
    tensor_count = lax.axis_size("tensor")
    batch_count = lax.axis_size("batch")
    device_index = lax.axis_index("batch") * tensor_count + tensor_index
    device_count = batch_count * tensor_count
    patch_values = patches.astype(jnp.float32)
    local_valid = lax.dynamic_slice_in_dim(valid_mask, tensor_index * shard_count, shard_count, 0)
    live_mask = local_valid.astype(jnp.float32)[:, None]
    allowed = build_allowed(local_valid, P_SIZE)
    embed_full = embed_weight.astype(jnp.float32)
    shards = []
    for layer_index in range(NL):
        shards.append(jnp.swapaxes(attend_weight[layer_index], 1, 2).reshape(-1, D))
        shards.append(merge_weight[layer_index])
        shards.append(jnp.swapaxes(up_weight[layer_index], 0, 1))
        shards.append(down_weight[layer_index])
    wholes, bias_all = gather_weights(shards, up_bias)
    weights = [
        (*wholes[4 * layer_index : 4 * layer_index + 4], bias_all[:, layer_index].reshape(-1))
        for layer_index in range(NL)
    ]
    choose = class_ids[:, None] == lax.broadcasted_iota(jnp.int32, (local_images, CLASSES), 1)
    class_rows = product(choose.astype(jnp.bfloat16), class_table)
    hidden = product(patches, embed_weight) + embed_bias
    hidden = hidden.reshape(local_images, P_SIZE, D) + position_table.astype(jnp.float32)[None]
    hidden = (hidden + class_rows[:, None]).reshape(shard_count, D)
    stored = []
    for layer_index in range(NL):
        attend_full, merge_full, up_full, down_full, bias_full = weights[layer_index]
        normed = layer_norm(hidden, attn_gain[layer_index], attn_offset[layer_index]).astype(
            jnp.bfloat16
        )
        qkv_low = product_back(normed, attend_full).astype(jnp.bfloat16)
        blocks = head_blocks(qkv_low, tensor_count)
        mixed_low, log_total = attend(blocks, allowed)
        hidden_mid = hidden + product(mixed_low, merge_full)
        normed_mlp = layer_norm(hidden_mid, mlp_gain[layer_index], mlp_offset[layer_index]).astype(
            jnp.bfloat16
        )
        pre_active = product_back(normed_mlp, up_full) + bias_full
        active = gelu_exact(pre_active).astype(jnp.bfloat16)
        stored.append(
            (hidden, normed, blocks, log_total, mixed_low, hidden_mid, normed_mlp, pre_active, active)
        )
        hidden = hidden_mid + (product(active, down_full) + down_bias[layer_index])
    final = layer_norm(hidden, final_gain, final_offset)
    final_low = final.astype(jnp.bfloat16)
    head_out = product(final_low, head_weight) + head_bias
    position = lax.broadcasted_iota(jnp.int32, (shard_count, 1), 0) % P_SIZE
    starts = position == 0
    previous = jnp.concatenate([jnp.zeros((1, 2 * PV), jnp.float32), head_out[:-1]], axis=0)
    previous = jnp.where(starts, 0.0, previous)
    shift_part = previous[:, :PV]
    log_scale = previous[:, PV:]
    scale_factor = jnp.exp(-log_scale)
    latents = (
        live_mask * (patch_values - shift_part) * scale_factor + (1.0 - live_mask) * patch_values
    )
    log_det = -jnp.sum((live_mask * log_scale).reshape(local_images, P_SIZE * PV), axis=1)
    image_cot = jnp.repeat(logdet_cot, P_SIZE)[:, None]
    direct_grad = latent_cot * (live_mask * scale_factor + (1.0 - live_mask))
    grad_shift = -live_mask * latent_cot * scale_factor
    grad_scale = -live_mask * (latent_cot * (patch_values - shift_part) * scale_factor + image_cot)
    grad_previous = jnp.where(starts, 0.0, jnp.concatenate([grad_shift, grad_scale], axis=1))
    grad_head = jnp.concatenate([grad_previous[1:], jnp.zeros((1, 2 * PV), jnp.float32)], axis=0)
    grad_head_low = grad_head.astype(jnp.bfloat16)
    head_weight_grad = contract_rows(grad_head_low, final_low)
    head_bias_grad = jnp.sum(grad_head_low.astype(jnp.float32), axis=0)
    grad_final = product_back(grad_head_low, head_weight)
    grad_hidden, final_gain_grad, final_offset_grad = norm_backward(
        hidden, final_gain, final_offset, grad_final
    )
    rows_of = {}
    split_list = [None] * NL
    for layer_index in reversed(range(NL)):
        hidden_in, normed, blocks, log_total, mixed_low, hidden_mid, normed_mlp, pre_active, active = (
            stored[layer_index]
        )
        attend_full, merge_full, up_full, down_full, bias_full = weights[layer_index]
        grad_out_mlp = grad_hidden.astype(jnp.bfloat16)
        down_bias_grad = jnp.sum(grad_out_mlp.astype(jnp.float32), axis=0)
        down_grad = contract_rows(active, grad_out_mlp)
        grad_active = product_back(grad_out_mlp, down_full)
        outputs, gelu_pull = jax.vjp(gelu_exact, pre_active)
        grad_inner = gelu_pull(grad_active)[0].astype(jnp.bfloat16)
        up_bias_grad = jnp.sum(grad_inner.astype(jnp.float32), axis=0)
        up_grad = contract_rows(grad_inner, normed_mlp)
        grad_normed = product(grad_inner, up_full)
        grad_from, mlp_gain_grad, mlp_offset_grad = norm_backward(
            hidden_mid, mlp_gain[layer_index], mlp_offset[layer_index], grad_normed
        )
        grad_hidden = grad_hidden + grad_from
        grad_out_attn = grad_hidden.astype(jnp.bfloat16)
        merge_grad = contract_rows(mixed_low, grad_out_attn)
        grad_mixed = product_back(grad_out_attn, merge_full).astype(jnp.bfloat16)
        grad_qkv = attend_back(blocks, allowed, log_total, grad_mixed, tensor_count)
        attend_grad = contract_rows(grad_qkv, normed)
        grad_normed = product(grad_qkv, attend_full)
        grad_from, attn_gain_grad, attn_offset_grad = norm_backward(
            hidden_in, attn_gain[layer_index], attn_offset[layer_index], grad_normed
        )
        grad_hidden = grad_hidden + grad_from
        rows_of[layer_index] = [
            attn_gain_grad[None],
            attn_offset_grad[None],
            mlp_gain_grad[None],
            mlp_offset_grad[None],
            down_bias_grad[None],
            up_bias_grad.reshape(-1, D),
        ]
        split_list[layer_index] = [
            grad.astype(jnp.bfloat16) for grad in (attend_grad, merge_grad, up_grad, down_grad)
        ]
    per_image = grad_hidden.reshape(local_images, P_SIZE, D)
    image_count = device_count * local_images
    image_index = device_index * local_images
    image_rows = lax.dynamic_update_slice_in_dim(
        jnp.zeros((image_count, D), jnp.float32), jnp.sum(per_image, axis=1), image_index, 0
    )
    id_rows = jnp.stack([class_ids // 32, class_ids % 32]).astype(jnp.float32)
    id_rows = lax.dynamic_update_slice(jnp.zeros((2, D), jnp.float32), id_rows, (0, image_index))
    small = [
        jnp.sum(per_image, axis=0),
        precise_rows(patch_values, grad_hidden),
        head_weight_grad,
        image_rows,
        jnp.sum(grad_hidden, axis=0)[None],
        final_gain_grad[None],
        final_offset_grad[None],
        jnp.pad(head_bias_grad, (0, D - 2 * PV))[None],
    ]
    for entry in rows_of[0] + rows_of[1]:
        small.append(entry)
    small.append(id_rows)
    lengths = [entry.shape[0] for entry in small]
    joined = jnp.concatenate(small, axis=0)
    joined = jnp.pad(joined, ((0, -joined.shape[0] % (8 * device_count)), (0, 0)))
    sums, small_sum = reduce_weights(split_list[0] + split_list[1], joined)
    for layer_index in range(NL):
        attend_sum, merge_sum, up_sum, down_sum = sums[4 * layer_index : 4 * layer_index + 4]
        split_list[layer_index] = (
            jnp.swapaxes(attend_sum.reshape(3, -1, D), 1, 2).astype(jnp.float32),
            merge_sum.astype(jnp.float32),
            jnp.swapaxes(up_sum, 0, 1).astype(jnp.float32),
            down_sum.astype(jnp.float32),
        )
    patches_grad = direct_grad + lax.dot_general(
        grad_hidden,
        embed_full,
        (((1,), (1,)), ((), ())),
        precision=HIGHEST,
        preferred_element_type=jnp.float32,
    )
    small_sum = small_sum.astype(jnp.float32)
    small_list = []
    begin = 0
    for length in lengths:
        small_list.append(small_sum[begin : begin + length])
        begin += length
    id_sums = small_list[20][:, :image_count].astype(jnp.int32)
    all_ids = id_sums[0] * 32 + id_sums[1]
    choose_all = all_ids[:, None] == lax.broadcasted_iota(
        jnp.int32, (image_count, CLASSES), 1
    )
    class_grad = precise_rows(choose_all.astype(jnp.float32), small_list[3])
    layer_rows = [small_list[8:14], small_list[14:20]]
    own_bias = [
        lax.dynamic_slice_in_dim(
            entry[5].reshape(tensor_count, -1), tensor_index, 1, 0
        )
        for entry in layer_rows
    ]
    split_stack = [jnp.stack([entry[member] for entry in split_list]) for member in range(4)]
    shared_stack = [
        jnp.concatenate([entry[member] for entry in layer_rows], axis=0) for member in range(5)
    ]
    return (
        latents,
        log_det,
        patches_grad,
        small_list[1],
        small_list[4][0],
        small_list[0],
        class_grad,
        shared_stack[0],
        shared_stack[1],
        split_stack[0],
        split_stack[1],
        shared_stack[2],
        shared_stack[3],
        split_stack[2],
        jnp.concatenate(own_bias, axis=0),
        split_stack[3],
        shared_stack[4],
        small_list[5][0],
        small_list[6][0],
        jnp.swapaxes(small_list[2], 0, 1),
        small_list[7][0, : 2 * PV],
    )


def solution(mesh):
    return jax.shard_map(
        shards,
        mesh=mesh,
        in_specs=(
            P(("batch", "tensor"), None),
            P("batch"),
            P(("batch", "tensor")),
            P(),
            P(),
            P(),
            P(),
            P(),
            P(),
            P(None, None, None, "tensor"),
            P(None, "tensor", None),
            P(),
            P(),
            P(None, None, "tensor"),
            P(None, "tensor"),
            P(None, "tensor", None),
            P(),
            P(),
            P(),
            P(),
            P(),
            P(("batch", "tensor"), None),
            P(("batch", "tensor")),
        ),
        out_specs=(
            P(("batch", "tensor"), None),
            P(("batch", "tensor")),
            P(("batch", "tensor"), None),
            P(),
            P(),
            P(),
            P(),
            P(),
            P(),
            P(None, None, None, "tensor"),
            P(None, "tensor", None),
            P(),
            P(),
            P(None, None, "tensor"),
            P(None, "tensor"),
            P(None, "tensor", None),
            P(),
            P(),
            P(),
            P(),
            P(),
        ),
        check_vma=False,
    )
```

time: 2110 us -> 605 us (0.29)
  waiting for transfers between devices: 1620 us -> 0 us
  Pallas kernels: 0 us -> 320 us
  matrix products: 213 us -> 150 us
  blocking collectives: 58.2 us -> 0 us
  other arithmetic: 82.5 us -> 36.9 us
    reduce_scatter x8 -> x0, waiting for transfers between devices: 836 us -> none  [narrow(): lax.psum_scatter(term_rows(jnp.int32(0), shard_count * lax.axis_size('ten...]
    all_gather x8 -> x0, waiting for transfers between devices: 510 us -> none  [the longest x4 256 us: gather_grad(): return lax.all_gather(grad_low, 'tensor', axis=0, tiled=True)]
    pallas_call x0 -> x2, Pallas kernels: none -> 320 us  [the longest x1 205 us: reduce_all(): pl.pallas_call(functools.partial(reduce_kernel, groups, spread_all), out_...]
    psum x2 -> x0, waiting for transfers between devices: 277 us -> none  [the longest x1 152 us: shards(): lax.psum((embed_weight_grad, embed_bias_grad, position_grad, class_grad,...]
    dot_general x16 -> x12, matrix products: 85.9 us -> 26.6 us  [the longest x2 10.3 us: attend_back(): jnp.einsum('bhqd,bhkd->bhqk', grad_out, values, preferred_element_type=jn...]
    psum x2 -> x0, blocking collectives: 58.2 us -> none  [the longest x1 42.5 us: shards(): lax.psum((embed_weight_grad, embed_bias_grad, position_grad, class_grad,...]
    dot_general x9 -> x11, matrix products: 56.9 us -> 19 us  [product(): return jnp.dot(former, latter, preferred_element_type=jnp.float32)]
    unnamed x278 -> x289, local copies, waits for them, and re-layouts: 48.6 us -> 17.4 us
  transfers between devices with their start and end apart: 18 -> 0, of which waited for: 18 -> 0; matrix products, arithmetic and copies ran while one was open for 2% -> 0% of each run, Pallas kernels for 0% -> 0%
where the time goes in v1:
time: 605 us; the launch traced here: 597 us
  Pallas kernels  320 us (53%)
  matrix products  150 us (25%)
  local copies, waits for them, and re-layouts  85.9 us (14%)
  other arithmetic  36.9 us (6%)
    pallas_call x1, Pallas kernels, reduce_all(): pl.pallas_call(functools.partial(reduce_kernel, groups, spread_all), out_...  205 us
    pallas_call x1, Pallas kernels, gather_all(): pl.pallas_call(functools.partial(gather_kernel, units // 4), out_shape=ou...  116 us
    dot_general x9, matrix products, product_back(): lax.dot_general(former, latter, (((1,), (1,)), ((), ())), preferred_eleme...  65.9 us
    dot_general x9, matrix products, contract_rows(): lax.dot_general(former, latter, (((0,), (0,)), ((), ())), preferred_eleme...  33.4 us
    dot_general x11, matrix products, product(): return jnp.dot(former, latter, preferred_element_type=jnp.float32)  19 us
    unnamed x289, local copies, waits for them, and re-layouts  17.4 us

profile of v1, /device:TPU:0, one launch (start us, length us, event | category | flops | bytes accessed | tf_op | source)
XLA Modules:
  0.0 596.7 jit_solution(4920347453674023344)
XLA Ops:
  0.7 2.9 slice_bitcast_fusion
  7.4 3.3 fusion.87
  13.5 115.5 %gather_weights.1 = (bf16[4,9,8,8,768]{4,3,2,1,0:T(8,128)(2,1)}, bf16[4,3,8,8,768]{4,3,2,1,0:T(8,128)(2,1)}, bf16[4,8,96,768]{3,2,1,0:T(8,128)(2,1)}, bf16[4,8,9...) custom-call(bf16[9,8,8,768]{3,2,1,0:T(8,128)(2,1)} %bitcast.243, ...), custom_call_target="tpu_custom_call" | custom-call | tf_op jit(solution)/shard_map/gather_weights/pallas_call | solution.py:376
  131.3 3.6 convolution_convert_fusion.7
  134.9 4.3 copy.97
  139.2 6.0 %reshape.614 = bf16[2,256,4,3,3,64]{1,0,5,4,3,2:T(2,128)(2,1)} reshape(bf16[512,2304]{0,1:T(8,128)(2,1)} %copy.97) | data formatting | bytes 4718592 | tf_op jit(solution)/shard_map/reshape | solution.py:685
  145.3 3.8 fusion.86
  162.0 19.9 %multiply_convert_fusion.3 = (bf16[512,3072]{1,0:T(8,128)(2,1)S(1)}, f32[512,3072]{1,0:T(8,128)}, f32[512,3072]{1,0:T(8,128)}) fusion(f32[3072]{0:T(1024)S(1)} %bitcast.276, bf16[3072,768]{1,0:T(8,128)(2,1)S(1)} %bitcast.283, f32[512,768]{1,0:T(8,128)S(1)} %get-tuple-element.192, f32[768]{0:T(1024)S(1)} %get-tuple-element.122, ...), kind=kOutput, calls=%fused_computation.26 | convolution fusion | flops 2521694208 | bytes 22042624 | tf_op jit(solution)/shard_map/dot_general | solution.py:43
  182.0 2.7 fusion.94
  185.1 3.6 convolution_convert_fusion.6
  188.7 4.3 copy.103
  192.9 6.0 %reshape.620 = bf16[2,256,4,3,3,64]{1,0,5,4,3,2:T(2,128)(2,1)} reshape(bf16[512,2304]{0,1:T(8,128)(2,1)} %copy.103) | data formatting | bytes 4718592 | tf_op jit(solution)/shard_map/reshape | solution.py:685
  199.0 3.3 fusion.85
  210.7 19.6 %multiply_convert_fusion.2 = (bf16[512,3072]{1,0:T(8,128)(2,1)S(1)}, f32[512,3072]{1,0:T(8,128)}, f32[512,3072]{1,0:T(8,128)}) fusion(f32[3072]{0:T(1024)S(1)} %bitcast.278, bf16[3072,768]{1,0:T(8,128)(2,1)S(1)} %bitcast.295, f32[512,768]{1,0:T(8,128)S(1)} %get-tuple-element.199, f32[768]{0:T(1024)S(1)} %get-tuple-element.121, ...), kind=kOutput, calls=%fused_computation.10 | convolution fusion | flops 2521694208 | bytes 22042624 | tf_op jit(solution)/shard_map/dot_general | solution.py:43
  230.4 2.7 fusion.96
  238.7 8.3 %fusion.71 = (bf16[3072]{0:T(1024)(128)(2,1)S(1)}, bf16[512,3072]{1,0:T(8,128)(2,1)S(1)}) fusion(f32[512,3072]{1,0:T(8,128)} %get-tuple-element.150, f32[512,3072]{1,0:T(8,128)} %get-tuple-element.200, f32[3072]{0:T(1024)S(1)} %bitcast.279, bf16[512,768]{1,0:T(8,128)(2,1)S(1)} %get-tuple-element.130, bf16[3072,768]{1,0:T(8,128)(2,1)S(1)} %bitcast.300), kind=kOutput, calls=%fused_computation.258 | convolution fusion | flops 2441081856 | bytes 21252096 | tf_op jit(solution)/shard_map/dot_general | solution.py:43
  247.0 2.9 multiply_reduce_fusion.2
  254.2 5.1 multiply_reduce_fusion.1
  268.4 4.0 pad_maximum_fusion
  278.0 8.1 %fusion.73 = (bf16[3072]{0:T(1024)(128)(2,1)S(1)}, bf16[512,3072]{1,0:T(8,128)(2,1)S(1)}) fusion(f32[512,3072]{1,0:T(8,128)} %get-tuple-element.152, f32[512,3072]{1,0:T(8,128)} %get-tuple-element.193, f32[3072]{0:T(1024)S(1)} %bitcast.277, bf16[512,768]{1,0:T(8,128)(2,1)S(1)} %get-tuple-element.134, bf16[3072,768]{1,0:T(8,128)(2,1)S(1)} %bitcast.292), kind=kOutput, calls=%fused_computation.260 | convolution fusion | flops 2441081856 | bytes 21252096 | tf_op jit(solution)/shard_map/dot_general | solution.py:43
  286.2 2.9 multiply_reduce_fusion.4
  293.6 5.1 multiply_reduce_fusion
  308.0 4.0 pad_maximum_fusion.1
  320.4 7.0 %convolution_convert_fusion = bf16[3072,768]{1,0:T(8,128)(2,1)} fusion(bf16[512,3072]{1,0:T(8,128)(2,1)} %copy-done.120, bf16[512,768]{1,0:T(8,128)(2,1)} %copy-done.50), kind=kOutput, calls=%fused_computation.44 | convolution fusion | flops 2418278400 | bytes 8650752 | tf_op jit(solution)/shard_map/dot_general | solution.py:49
  327.5 4.9 convolution_convert_fusion.1
  334.3 4.0 convolution_convert_fusion.2
  338.4 4.3 convolution_convert_fusion.3
  342.8 4.6 convolution_convert_fusion.4
  349.2 4.0 convolution_convert_fusion.5
  353.2 204.6 %reduce_gradients.1 = (bf16[4,9,2,2,2,8,768]{6,5,4,3,2,1,0:T(8,128)(2,1)}, bf16[4,3,2,2,2,8,768]{6,5,4,3,2,1,0:T(8,128)(2,1)}, bf16[4,1,2,2,2,96,768]{6,5,4,3,2,...) custom-call(bf16[4,9,2,2,2,8,768]{6,5,4,3,2,1,0:T(8,128)(2,1)} %bitc, ...), custom_call_target="tpu_custom_call" | custom-call | tf_op jit(solution)/shard_map/reduce_gradients/pallas_call | solution.py:627
  571.3 6.0 %copy.127 = f32[2,768,768]{2,1,0:T(8,128)} copy(f32[2,768,768]{1,2,0:T(8,128)} %maximum_convert_fusion) | data formatting | bytes 9437184
  587.4 3.3 fusion.30
  (468 shorter events, 108.4 us)
Async XLA Ops:
  0.7 128.5 %copy-start = (bf16[1000,768]{1,0:T(8,128)(2,1)S(1)}, bf16[1000,768]{1,0:T(8,128)(2,1)}, u32[]{:S(2)}) copy-start(bf16[1000,768]{1,0:T(8,128)(2,1)} %param.29) | copy-start | bytes 4608004
  13.5 115.6 %copy-start.56 = (bf16[256,768]{1,0:T(8,128)(2,1)S(1)}, bf16[256,768]{1,0:T(8,128)(2,1)}, u32[]{:S(2)}) copy-start(bf16[256,768]{1,0:T(8,128)(2,1)} %param.28) | copy-start | bytes 1179652
  13.5 115.7 %copy-start.111 = (s32[2]{0:T(128)S(1)}, s32[2]{0:T(128)}, u32[]{:S(2)}) copy-start(s32[2]{0:T(128)} %param.25) | copy-start | bytes 28
  13.5 116.0 %copy-start.49 = (bf16[512,48]{0,1:T(8,128)(2,1)S(1)}, bf16[512,48]{0,1:T(8,128)(2,1)}, u32[]{:S(2)}) copy-start(bf16[512,48]{0,1:T(8,128)(2,1)} %param.23) | copy-start | bytes 147460
  13.5 116.0 %copy-start.61 = (bf16[48,768]{1,0:T(8,128)(2,1)S(1)}, bf16[48,768]{1,0:T(8,128)(2,1)}, u32[]{:S(2)}) copy-start(bf16[48,768]{1,0:T(8,128)(2,1)} %param.26) | copy-start | bytes 221188
  13.5 116.0 %copy-start.99 = (f32[768]{0:T(1024)S(1)}, f32[768]{0:T(1024)}, u32[]{:S(2)}) copy-start(f32[768]{0:T(1024)} %param.27) | copy-start | bytes 9220
  130.1 28.5 %copy-start.9 = (f32[512,768]{1,0:T(8,128)}, f32[512,768]{1,0:T(8,128)S(1)}, u32[]{:S(2)}) copy-start(f32[512,768]{1,0:T(8,128)S(1)} %get-tuple-element.188) | copy-start | bytes 4718596
  130.5 54.5 %copy-start.103 = (f32[768]{0:T(1024)}, f32[768]{0:T(1024)S(1)}, u32[]{:S(2)}) copy-start(f32[768]{0:T(1024)S(1)} %get-tuple-element.125) | copy-start | bytes 9220
  130.5 145.8 %copy-start.77 = (f32[768]{0:T(1024)}, f32[768]{0:T(1024)S(1)}, u32[]{:S(2)}) copy-start(f32[768]{0:T(1024)S(1)} %get-tuple-element.213) | copy-start | bytes 9220
  158.8 23.2 %slice-start.8 = ((s8[4718592]{0:T(1024)(128)(4,1)}), s8[4194304]{0:T(1024)(128)(4,1)S(1)}, s32[]{:S(2)}) async-start(s8[4718592]{0:T(1024)(128)(4,1)} %bitcast.287), calls=%async_computation.8 | async-start | bytes 8388608
  159.7 22.3 %copy-start.15 = (f32[512,768]{1,0:T(8,128)}, f32[512,768]{1,0:T(8,128)S(1)}, u32[]{:S(2)}) copy-start(f32[512,768]{1,0:T(8,128)S(1)} %get-tuple-element.192) | copy-start | bytes 4718596
  160.0 21.9 %copy-start.73 = (f32[512]{0:T(512)}, f32[512]{0:T(512)S(1)}, u32[]{:S(2)}) copy-start(f32[512]{0:T(512)S(1)} %multiply_reduce_fusion.15) | copy-start | bytes 6148
  160.1 129.1 %copy-start.85 = (f32[512]{0:T(512)}, f32[512]{0:T(512)S(1)}, u32[]{:S(2)}) copy-start(f32[512]{0:T(512)S(1)} %fusion.49) | copy-start | bytes 6148
  161.9 20.0 %copy-start.105 = (f32[768]{0:T(1024)}, f32[768]{0:T(1024)S(1)}, u32[]{:S(2)}) copy-start(f32[768]{0:T(1024)S(1)} %get-tuple-element.122) | copy-start | bytes 9220
  161.9 48.7 %copy-start.107 = (f32[768]{0:T(1024)}, f32[768]{0:T(1024)S(1)}, u32[]{:S(2)}) copy-start(f32[768]{0:T(1024)S(1)} %get-tuple-element.121) | copy-start | bytes 9220
  161.9 87.9 %copy-start.81 = (f32[768]{0:T(1024)}, f32[768]{0:T(1024)S(1)}, u32[]{:S(2)}) copy-start(f32[768]{0:T(1024)S(1)} %get-tuple-element.219) | copy-start | bytes 9220
  162.0 127.2 %copy-start.79 = (f32[768]{0:T(1024)}, f32[768]{0:T(1024)S(1)}, u32[]{:S(2)}) copy-start(f32[768]{0:T(1024)S(1)} %get-tuple-element.218) | copy-start | bytes 9220
  162.0 19.9 %copy-start.97 = (f32[2,768]{1,0:T(2,128)S(1)}, f32[2,768]{1,0:T(2,128)}, u32[]{:S(2)}) copy-start(f32[2,768]{1,0:T(2,128)} %param.39) | copy-start | bytes 18436
  162.0 20.0 %slice-start.9 = ((s8[4718592]{0:T(1024)(128)(4,1)}), s8[524288]{0:T(1024)(128)(4,1)S(1)}, s32[]{:S(2)}) async-start(s8[4718592]{0:T(1024)(128)(4,1)} %bitcast.287), calls=%async_computation.9 | async-start | bytes 1048576
  184.7 24.4 %copy-start.18 = (f32[512,768]{1,0:T(8,128)}, f32[512,768]{1,0:T(8,128)S(1)}, u32[]{:S(2)}) copy-start(f32[512,768]{1,0:T(8,128)S(1)} %get-tuple-element.195) | copy-start | bytes 4718596
  184.7 91.6 %copy-start.67 = (f32[512]{0:T(512)}, f32[512]{0:T(512)S(1)}, u32[]{:S(2)}) copy-start(f32[512]{0:T(512)S(1)} %broadcast_multiply_fusion.2) | copy-start | bytes 6148
  185.0 91.3 %copy-start.87 = (f32[512]{0:T(512)}, f32[512]{0:T(512)S(1)}, u32[]{:S(2)}) copy-start(f32[512]{0:T(512)S(1)} %fusion.50) | copy-start | bytes 6148
  209.4 21.0 %slice-start.14 = ((s8[4718592]{0:T(1024)(128)(4,1)}), s8[4194304]{0:T(1024)(128)(4,1)S(1)}, s32[]{:S(2)}) async-start(s8[4718592]{0:T(1024)(128)(4,1)} %bitcast.297), calls=%async_computation.14 | async-start | bytes 8388608
  210.3 39.6 %copy-start.21 = (f32[512,768]{1,0:T(8,128)}, f32[512,768]{1,0:T(8,128)S(1)}, u32[]{:S(2)}) copy-start(f32[512,768]{1,0:T(8,128)S(1)} %get-tuple-element.199) | copy-start | bytes 4718596
  210.3 39.6 %copy-start.69 = (f32[512]{0:T(512)}, f32[512]{0:T(512)S(1)}, u32[]{:S(2)}) copy-start(f32[512]{0:T(512)S(1)} %broadcast_multiply_fusion.1) | copy-start | bytes 6148
  210.6 39.3 %copy-start.89 = (f32[512]{0:T(512)}, f32[512]{0:T(512)S(1)}, u32[]{:S(2)}) copy-start(f32[512]{0:T(512)S(1)} %fusion.51) | copy-start | bytes 6148
  210.7 19.6 %slice-start.15 = ((s8[4718592]{0:T(1024)(128)(4,1)}), s8[524288]{0:T(1024)(128)(4,1)S(1)}, s32[]{:S(2)}) async-start(s8[4718592]{0:T(1024)(128)(4,1)} %bitcast.297), calls=%async_computation.15 | async-start | bytes 1048576
  238.6 8.3 %copy-start.50 = (bf16[512,768]{1,0:T(8,128)(2,1)}, bf16[512,768]{1,0:T(8,128)(2,1)S(1)}, u32[]{:S(2)}) copy-start(bf16[512,768]{1,0:T(8,128)(2,1)S(1)} %get-tuple-element.130) | copy-start | bytes 2359300
  268.4 9.6 %slice-start.10 = ((s8[4718592]{0:T(1024)(128)(4,1)}), s8[4194304]{0:T(1024)(128)(4,1)S(1)}, s32[]{:S(2)}) async-start(s8[4718592]{0:T(1024)(128)(4,1)} %bitcast.290), calls=%async_computation.10 | async-start | bytes 8388608
  276.4 9.8 %slice-start.6 = ((s8[4718592]{0:T(1024)(128)(4,1)}), s8[4194304]{0:T(1024)(128)(4,1)S(1)}, s32[]{:S(2)}) async-start(s8[4718592]{0:T(1024)(128)(4,1)} %bitcast.284), calls=%async_computation.6 | async-start | bytes 8388608
  278.0 8.2 %copy-start.51 = (bf16[512,768]{1,0:T(8,128)(2,1)}, bf16[512,768]{1,0:T(8,128)(2,1)S(1)}, u32[]{:S(2)}) copy-start(bf16[512,768]{1,0:T(8,128)(2,1)S(1)} %get-tuple-element.134) | copy-start | bytes 2359300
  587.4 9.1 %copy-start.1 = (bf16[1000,768]{1,0:T(8,128)(2,1)S(1)}, bf16[1000,768]{1,0:T(8,128)(2,1)}, u32[]{:S(2)}) copy-start(bf16[1000,768]{1,0:T(8,128)(2,1)} %param.29) | copy-start | bytes 4608004
  (109 other events, 378.4 us)

commit v2 on v1

--- a/solution.py
+++ b/solution.py
@@ -31,18 +31,14 @@
     return pullback(upstream)
 
 
-def gelu_exact(values):
-    return jax.nn.gelu(values, approximate=False)
+def gelu_parts(values):
+    share = 0.5 + 0.5 * lax.erf(values * (0.5**0.5))
+    slope = share + values * (jnp.exp(-0.5 * values * values) * ((0.5 / jnp.pi) ** 0.5))
+    return (values * share, slope)
 
 
 def product(former, latter):
     return jnp.dot(former, latter, preferred_element_type=jnp.float32)
-
-
-def product_back(former, latter):
-    return lax.dot_general(
-        former, latter, (((1,), (1,)), ((), ())), preferred_element_type=jnp.float32
-    )
 
 
 def contract_rows(former, latter):
@@ -399,6 +395,7 @@
 
 
 ITEM_ORDER = (0, 2, 1, 3)
+AHEAD = 3
 
 
 def reduce_kernel(groups, spread_all, *refs):
@@ -419,7 +416,8 @@
     copies = Copies(send_sems)
     conditional = []
     items = [(group, t) for group in groups for t in ITEM_ORDER]
-    for group, t in items:
+
+    def load(group, t):
         for unit in group:
             grad = grads[unit]
             copies.send(
@@ -511,14 +509,18 @@
 
             conditional.append((t, copy))
 
+    def slot_of(unit):
+        return z if unit in spread_all else 0
+
     def spot_of(unit, where):
-        return outs[unit].at[(z, slice(None), *where)]
+        return outs[unit].at[(slot_of(unit), slice(None), *where)]
 
     def half_spot(unit, where, side):
         count = outs[unit].shape[1]
         if count > 1:
-            return outs[unit].at[(z, halves(count)[side], *where)]
-        return outs[unit].at[(z, slice(None), *where, halves(outs[unit].shape[5])[side])]
+            return outs[unit].at[(slot_of(unit), halves(count)[side], *where)]
+        rows = halves(outs[unit].shape[5])[side]
+        return outs[unit].at[(slot_of(unit), slice(None), *where, rows)]
 
     def take_z(group):
         for unit in group:
@@ -589,7 +591,11 @@
             if step == last + 6:
                 take_corner(group)
 
+    for item in items[:AHEAD]:
+        load(*item)
     for step in range(len(items) + 6):
+        if step + AHEAD < len(items):
+            load(*items[step + AHEAD])
         run(step)
     for group in groups:
         take_last(group)
@@ -626,7 +632,10 @@
     anywhere = pl.BlockSpec(memory_space=pl.ANY)
     return pl.pallas_call(
         functools.partial(reduce_kernel, groups, spread_all),
-        out_shape=[jax.ShapeDtypeStruct(grad.shape, grad.dtype) for grad in grads],
+        out_shape=[
+            jax.ShapeDtypeStruct((4 if unit in spread_all else 1, *grad.shape[1:]), grad.dtype)
+            for unit, grad in enumerate(grads)
+        ],
         in_specs=[anywhere] * units,
         out_specs=[anywhere] * units,
         scratch_shapes=scratch
@@ -663,76 +672,619 @@
     return ([whole.reshape(-1, D) for whole in results[:-1]], results[-1][:, :NL])
 
 
-def reduce_weights(grads, small):
+def reduce_weights(split_list, small):
     if not fast_mesh():
+        grads = [grad.reshape(-1, D) for grad in split_list[0] + split_list[1]]
         sums = reduce_rows([to_batch_major(grad) for grad in grads] + [split_blocks(small)])
         small_sum = lax.all_gather(sums[-1], "tensor", axis=1).reshape(-1, D)
         return ([entry.reshape(-1, D) for entry in sums[:-1]], small_sum)
-    tensor_index = lax.axis_index("tensor")
-    parts = []
-    for grad in grads:
-        count = 1 if grad.shape[0] == 4 * D else grad.shape[0] // 256
-        parts.append(grad.reshape(4, count, 2, 2, 2, -1, D))
-    parts.append(small.astype(jnp.bfloat16).reshape(4, 1, 2, 2, 2, -1, D))
-    groups = ((4, 5, 6, 7), (0, 1, 2, 3, 8))
-    sums = reduce_all(parts, groups, (8,))
-    own = [lax.dynamic_index_in_dim(entry, tensor_index, 0, keepdims=False) for entry in sums[:-1]]
-    return ([entry.reshape(-1, D) for entry in own], sums[-1].reshape(-1, D))
-
-
-def head_blocks(qkv_low, tensor_count):
-    images = qkv_low.shape[0] // P_SIZE
-    blocks = qkv_low.reshape(images, P_SIZE, tensor_count, 3, -1, HEAD_DIM)
-    blocks = jnp.transpose(blocks, (3, 0, 2, 4, 1, 5))
-    return blocks.reshape(3, images, -1, P_SIZE, HEAD_DIM)
-
-
-def head_rows(mixed):
-    images, heads = mixed.shape[:2]
-    return jnp.transpose(mixed, (0, 2, 1, 3)).reshape(images * P_SIZE, heads * HEAD_DIM)
-
-
-def block_scores(blocks, allowed):
-    queries, keys, values = blocks[0], blocks[1], blocks[2]
-    scores = jnp.einsum("bhqd,bhkd->bhqk", queries, keys, preferred_element_type=jnp.float32) * (
-        HEAD_DIM ** (-0.5)
+    part = small.astype(jnp.bfloat16).reshape(4, 1, 2, 2, 2, -1, D)
+    (small_sum,) = reduce_all([part], ((0,),), (0,))
+    return (split_list[0] + split_list[1], small_sum.reshape(-1, D))
+
+
+def back_dot(former, latter):
+    return lax.dot_general(
+        former, latter, (((1,), (1,)), ((), ())), preferred_element_type=jnp.float32
     )
-    scores = jnp.where(allowed[:, None], scores, NEGATIVE)
-    return (queries, keys, values, scores)
-
-
-def attend(blocks, allowed):
-    queries, keys, values, scores = block_scores(blocks, allowed)
-    log_total = jax.nn.logsumexp(scores, axis=-1, keepdims=True)
-    probs_low = jnp.exp(scores - log_total).astype(jnp.bfloat16)
-    mixed = jnp.einsum("bhqk,bhkd->bhqd", probs_low, values, preferred_element_type=jnp.float32)
-    return (head_rows(mixed.astype(jnp.bfloat16)), log_total)
-
-
-def attend_back(blocks, allowed, log_total, grad_mixed, tensor_count):
-    queries, keys, values, scores = block_scores(blocks, allowed)
-    probs_full = jnp.exp(scores - log_total)
-    probs_low = probs_full.astype(jnp.bfloat16)
-    images = queries.shape[0]
-    grad_out = jnp.transpose(grad_mixed.reshape(images, P_SIZE, -1, HEAD_DIM), (0, 2, 1, 3))
-    grad_values = jnp.einsum(
-        "bhqk,bhqd->bhkd", probs_low, grad_out, preferred_element_type=jnp.float32
+
+
+def row_blocks(count, size, body, carry=0):
+    def step(index, carry):
+        return body(pl.ds(pl.multiple_of(index * size, size), size), carry)
+
+    return lax.fori_loop(0, count // size, step, carry)
+
+
+def norm_into(source, gain, offset, target):
+    def body(rows, carry):
+        target[rows] = layer_norm(source[rows], gain, offset).astype(target.dtype)
+        return carry
+
+    row_blocks(source.shape[0], 128, body)
+
+
+def norm_back_into(grad, source, upstream, gain):
+    def body(rows, carry):
+        gain_sum, offset_sum = carry
+        values, above = source[rows], upstream[rows]
+        center = values - jnp.mean(values, axis=-1, keepdims=True)
+        spread = jnp.mean(center * center, axis=-1, keepdims=True)
+        scale = lax.rsqrt(spread + EPSILON)
+        normal = center * scale
+        part = above * gain
+        gain_sum = gain_sum + jnp.sum(above * normal, axis=0, keepdims=True)
+        offset_sum = offset_sum + jnp.sum(above, axis=0, keepdims=True)
+        inner = jnp.mean(part, axis=-1, keepdims=True)
+        along = jnp.mean(part * normal, axis=-1, keepdims=True)
+        grad[rows] = grad[rows] + scale * (part - inner - normal * along)
+        return (gain_sum, offset_sum)
+
+    zero = jnp.zeros((1, D), jnp.float32)
+    return row_blocks(source.shape[0], 128, body, (zero, zero))
+
+
+def head_probs(qkv, allowed, t, rows, image, head):
+    span = qkv.shape[2] // 3
+    queries, keys, values = (
+        qkv[t, rows, c * span + head * HEAD_DIM : c * span + (head + 1) * HEAD_DIM]
+        for c in range(3)
     )
-    grad_probs = jnp.einsum("bhqd,bhkd->bhqk", grad_out, values, preferred_element_type=jnp.float32)
-    inner_sum = jnp.sum(probs_full * grad_probs, axis=-1, keepdims=True)
-    grad_scores = (probs_full * (grad_probs - inner_sum)).astype(jnp.bfloat16)
-    scaling = HEAD_DIM ** (-0.5)
-    grad_queries = (
-        jnp.einsum("bhqk,bhkd->bhqd", grad_scores, keys, preferred_element_type=jnp.float32)
-        * scaling
+    scores = back_dot(queries, keys) * (HEAD_DIM ** (-0.5))
+    scores = jnp.where(allowed[image] > 0, scores, NEGATIVE)
+    top = jnp.max(scores, axis=-1, keepdims=True)
+    powers = jnp.exp(scores - top)
+    total = jnp.sum(powers, axis=-1, keepdims=True)
+    return (queries, keys, values, powers * (1.0 / total))
+
+
+def each_image(qkv, body, begin=0, end=4):
+    images = qkv.shape[1] // P_SIZE
+
+    def step(index, carry):
+        t, image = index // images, index % images
+        body(t, image, pl.ds(pl.multiple_of(image * P_SIZE, P_SIZE), P_SIZE))
+        return carry
+
+    lax.fori_loop(begin * images, end * images, step, 0)
+
+
+def attend_into(qkv, allowed, mixed):
+    def body(t, image, rows):
+        blocks = []
+        for head in range(qkv.shape[2] // (3 * HEAD_DIM)):
+            queries, keys, values, probs = head_probs(qkv, allowed, t, rows, image, head)
+            blocks.append(product(probs.astype(jnp.bfloat16), values))
+        mixed[t, rows] = jnp.concatenate(blocks, axis=1).astype(mixed.dtype)
+
+    each_image(qkv, body)
+
+
+def attend_back_into(qkv, allowed, grad_mixed, grad_qkv, begin=0, end=4):
+    def body(t, image, rows):
+        parts = ([], [], [])
+        for head in range(qkv.shape[2] // (3 * HEAD_DIM)):
+            queries, keys, values, probs = head_probs(qkv, allowed, t, rows, image, head)
+            above = grad_mixed[t, rows, head * HEAD_DIM : (head + 1) * HEAD_DIM]
+            grad_values = contract_rows(probs.astype(jnp.bfloat16), above)
+            grad_probs = back_dot(above, values)
+            inner = jnp.sum(probs * grad_probs, axis=-1, keepdims=True)
+            grad_scores = (probs * (grad_probs - inner)).astype(jnp.bfloat16)
+            scaling = HEAD_DIM ** (-0.5)
+            parts[0].append(product(grad_scores, keys) * scaling)
+            parts[1].append(contract_rows(grad_scores, queries) * scaling)
+            parts[2].append(grad_values)
+        grad_qkv[t, rows] = jnp.concatenate(parts[0] + parts[1] + parts[2], axis=1).astype(
+            grad_qkv.dtype
+        )
+
+    each_image(qkv, body, begin, end)
+
+
+def each_part(body, count=4):
+    def step(t, carry):
+        body(t)
+        return carry
+
+    lax.fori_loop(0, count, step, 0)
+
+
+def layer_forward_chunks(
+    hidden, allowed, gains, weights, bias, normed, qkv, mixed, hidden_mid, normed_mlp, slope, active,
+    hidden_next,
+):
+    attend_w, merge_w, up_w, down_w = weights
+
+    def start():
+        norm_into(hidden, gains[0:1], gains[1:2], normed)
+
+        def project(t):
+            qkv[t] = back_dot(normed[...], attend_w[t]).astype(qkv.dtype)
+
+        each_part(project)
+
+    def attention():
+        attend_into(qkv, allowed, mixed)
+
+    def merge():
+        total = hidden[...]
+        for t in range(4):
+            total = total + product(mixed[t], merge_w[t])
+        hidden_mid[...] = total
+        norm_into(hidden_mid, gains[2:3], gains[3:4], normed_mlp)
+
+    def up(t):
+        inner = product(normed_mlp[...], up_w[t]) + bias[pl.ds(t, 1)]
+        value, rise = gelu_parts(inner)
+        active[t] = value.astype(active.dtype)
+        slope[t] = rise.astype(slope.dtype)
+
+    def down():
+        total = hidden_mid[...] + gains[4:5]
+        for t in range(4):
+            total = total + product(active[t], down_w[t])
+        hidden_next[...] = total
+
+    return [start, attention, merge, lambda: each_part(up), down]
+
+
+def layer_forward_kernel(*refs):
+    hidden, allowed, gains, bias = refs[:4]
+    weights = refs[4:8]
+    for chunk in layer_forward_chunks(hidden, allowed, gains, weights, bias, *refs[8:]):
+        chunk()
+
+
+def layer_shapes(rows, heads):
+    low, full = jnp.bfloat16, jnp.float32
+    return [
+        jax.ShapeDtypeStruct((rows, D), low),
+        jax.ShapeDtypeStruct((4, rows, heads * 3 * HEAD_DIM), low),
+        jax.ShapeDtypeStruct((4, rows, heads * HEAD_DIM), low),
+        jax.ShapeDtypeStruct((rows, D), full),
+        jax.ShapeDtypeStruct((rows, D), low),
+        jax.ShapeDtypeStruct((4, rows, D), low),
+        jax.ShapeDtypeStruct((4, rows, D), low),
+        jax.ShapeDtypeStruct((rows, D), full),
+    ]
+
+
+VMEM_LIMIT = 62 * 1024 * 1024
+
+
+def layer_forward(hidden, allowed, gains, bias, weights):
+    rows, heads = hidden.shape[0], weights[0].shape[1] // (3 * HEAD_DIM)
+    vmem = pl.BlockSpec(memory_space=pltpu.VMEM)
+    outs = layer_shapes(rows, heads)
+    return pl.pallas_call(
+        layer_forward_kernel,
+        out_shape=outs,
+        in_specs=[vmem] * 8,
+        out_specs=[vmem] * len(outs),
+        compiler_params=pltpu.CompilerParams(vmem_limit_bytes=VMEM_LIMIT),
+        name="layer_forward",
+    )(hidden, allowed, gains, bias, *weights)
+
+
+def layer_backward_chunks(
+    grad, allowed, gains, weights, stored, low, grad_inner, grad_mixed, grad_qkv, upstream, rows_out,
+    attend_grad, merge_grad, up_grad, down_grad,
+):
+    attend_w, merge_w, up_w, down_w = weights
+    hidden, normed, qkv, mixed, hidden_mid, normed_mlp, slope, active = stored
+
+    def start():
+        low[...] = grad[...].astype(low.dtype)
+        rows_out[4:5] = jnp.sum(low[...].astype(jnp.float32), axis=0, keepdims=True)
+        upstream[...] = jnp.zeros_like(upstream)
+
+    def mlp(t):
+        inner = (back_dot(low[...], down_w[t]) * slope[t]).astype(jnp.bfloat16)
+        grad_inner[...] = inner
+        rows_out[pl.ds(8 + t, 1)] = jnp.sum(inner.astype(jnp.float32), axis=0, keepdims=True)
+        up_grad[t] = contract_rows(normed_mlp[...], grad_inner[...]).astype(jnp.bfloat16)
+        down_grad[t] = contract_rows(active[t], low[...]).astype(jnp.bfloat16)
+        upstream[...] += back_dot(grad_inner[...], up_w[t])
+
+    def middle():
+        sums = norm_back_into(grad, hidden_mid, upstream, gains[2:3])
+        rows_out[2:3], rows_out[3:4] = sums
+        low[...] = grad[...].astype(low.dtype)
+
+        def part(t):
+            merge_grad[t] = contract_rows(mixed[t], low[...]).astype(jnp.bfloat16)
+            grad_mixed[t] = back_dot(low[...], merge_w[t]).astype(jnp.bfloat16)
+
+        each_part(part)
+
+    def attention():
+        attend_back_into(qkv, allowed, grad_mixed, grad_qkv)
+
+    def finish():
+        upstream[...] = jnp.zeros_like(upstream)
+
+        def part(t):
+            attend_grad[t] = contract_rows(grad_qkv[t], normed[...]).astype(jnp.bfloat16)
+            upstream[...] += product(grad_qkv[t], attend_w[t])
+
+        each_part(part)
+        sums = norm_back_into(grad, hidden, upstream, gains[0:1])
+        rows_out[0:1], rows_out[1:2] = sums
+
+    return [start, lambda: each_part(mlp), middle, attention, finish]
+
+
+def layer_backward_kernel(*refs):
+    grad_in, allowed, gains = refs[:3]
+    weights, stored = refs[3:7], refs[7:15]
+    grad, rows_out, attend_grad, merge_grad, up_grad, down_grad = refs[15:21]
+    low, grad_inner, grad_mixed, grad_qkv, upstream = refs[21:]
+    grad[...] = grad_in[...]
+    rows_out[...] = jnp.zeros_like(rows_out)
+    for chunk in layer_backward_chunks(
+        grad, allowed, gains, weights, stored, low, grad_inner, grad_mixed, grad_qkv, upstream,
+        rows_out, attend_grad, merge_grad, up_grad, down_grad,
+    ):
+        chunk()
+
+
+def layer_backward(grad, allowed, gains, weights, stored):
+    rows, heads = grad.shape[0], weights[0].shape[1] // (3 * HEAD_DIM)
+    vmem = pl.BlockSpec(memory_space=pltpu.VMEM)
+    low, full = jnp.bfloat16, jnp.float32
+    outs = [jax.ShapeDtypeStruct((rows, D), full), jax.ShapeDtypeStruct((16, D), full)]
+    outs += [jax.ShapeDtypeStruct(weight.shape, low) for weight in weights]
+    return pl.pallas_call(
+        layer_backward_kernel,
+        out_shape=outs,
+        in_specs=[vmem] * 15,
+        out_specs=[vmem] * len(outs),
+        scratch_shapes=[
+            pltpu.VMEM((rows, D), low),
+            pltpu.VMEM((rows, D), low),
+            pltpu.VMEM((4, rows, heads * HEAD_DIM), low),
+            pltpu.VMEM((4, rows, heads * 3 * HEAD_DIM), low),
+            pltpu.VMEM((rows, D), full),
+        ],
+        compiler_params=pltpu.CompilerParams(vmem_limit_bytes=VMEM_LIMIT),
+        name="layer_backward",
+    )(grad, allowed, gains, *weights, *stored)
+
+
+MLP_GROUP, ATTEND_GROUP = (2, 3), (0, 1)
+
+
+def layer_back_kernel(*refs):
+    grad_in, hidden, hidden_mid, normed, normed_mlp, slope, active, up_w, down_w = refs[:9]
+    qkv, mixed, allowed, gains, attend_w, merge_w = refs[9:15]
+    grad, rows_out = refs[15:17]
+    outs = refs[17:21]
+    grads, got_core, got_one, got_two, got_z, result = (
+        refs[21 + 4 * entry : 25 + 4 * entry] for entry in range(6)
     )
-    grad_keys = (
-        jnp.einsum("bhqk,bhqd->bhkd", grad_scores, queries, preferred_element_type=jnp.float32)
-        * scaling
+    low, grad_inner, grad_mixed, grad_qkv, upstream, values, rounded = refs[45:52]
+    slopes, actives, ups, downs = refs[52:56]
+    send_sems, step_sems, z_sems, spread_sems, core_sems, spare, load_sems, stream_sems = refs[56:]
+    y, x, core, z = place()
+    at_x = device_at(y, 1 - x, core, z)
+    at_y = device_at(1 - y, x, core, z)
+    at_core = device_at(y, x, 1 - core, z)
+
+    def load(source, target, sem):
+        copy = pltpu.make_async_copy(source, target, load_sems.at[sem])
+        copy.start()
+        return copy
+
+    def stream(step):
+        t, slot = ITEM_ORDER[step], step % 2
+        pairs = ((down_w, downs), (slope, slopes), (active, actives), (up_w, ups))
+        copies = []
+        for entry, (source, target) in enumerate(pairs):
+            copy = pltpu.make_async_copy(
+                source.at[t], target.at[slot], stream_sems.at[slot, entry]
+            )
+            copy.start()
+            copies.append(copy)
+        return copies
+
+    first_loads = [load(grad_in, grad, 0)]
+    streams = [stream(0), stream(1)]
+    first_loads += [load(normed_mlp, rounded, 1), load(hidden_mid, values, 2)]
+    greet(partners())
+    copies = Copies(send_sems)
+    conditional = []
+    items = [(group, t) for group in (MLP_GROUP, ATTEND_GROUP) for t in ITEM_ORDER]
+
+    def put(unit, t, value):
+        target = grads[unit]
+        target[t] = value.reshape(target.shape[1:]).astype(target.dtype)
+
+    def share(k):
+        group, t = items[k]
+        for unit in group:
+            copies.send(
+                grads[unit].at[t, :, :, :, 1 - core],
+                got_core[unit].at[t],
+                step_sems.at[unit, 0, t],
+                at_core,
+            )
+
+    def core_sum(k):
+        group, t = items[k]
+        for unit in group:
+            mine, other = grads[unit], got_core[unit]
+            wait_arrival(other.at[t], step_sems.at[unit, 0, t], spare.at[0], at_core)
+
+            def body(entry, carry):
+                spot = (t, entry // 4, entry // 2 % 2, entry % 2)
+                add_slab(mine.at[(*spot, core)], other.at[spot])
+                return carry
+
+            lax.fori_loop(0, mine.shape[1] * 4, body, 0)
+            if t < 2:
+                source, device = mine.at[t, :, :, 1 - x, core], at_x
+            else:
+                source, device = mine.at[t, :, 1 - y, :, core], at_y
+            copies.send(source, got_one[unit].at[t], step_sems.at[unit, 1, t], device)
+
+    def one(k):
+        group, t = items[k]
+        for unit in group:
+            mine, other = grads[unit], got_one[unit]
+            wait_arrival(
+                other.at[t], step_sems.at[unit, 1, t], spare.at[0], at_x if t < 2 else at_y
+            )
+
+            def body(entry, carry):
+                first, second = entry // 2, entry % 2
+                spot = (t, first, second, x, core) if t < 2 else (t, first, y, second, core)
+                add_slab(mine.at[spot], other.at[t, first, second])
+                return carry
+
+            lax.fori_loop(0, mine.shape[1] * 2, body, 0)
+            if t < 2:
+                source, device = mine.at[t, :, 1 - y, x, core], at_y
+            else:
+                source, device = mine.at[t, :, y, 1 - x, core], at_x
+            copies.send(source, got_two[unit].at[t], step_sems.at[unit, 2, t], device)
+
+    def two(k):
+        group, t = items[k]
+        for unit in group:
+            mine, other = grads[unit], got_two[unit]
+            wait_arrival(
+                other.at[t], step_sems.at[unit, 2, t], spare.at[0], at_y if t < 2 else at_x
+            )
+
+            def body(entry, carry):
+                add_slab(mine.at[t, entry, y, x, core], other.at[t, entry])
+                return carry
+
+            lax.fori_loop(0, mine.shape[1], body, 0)
+            copy = pltpu.make_async_remote_copy(
+                src_ref=mine.at[t, :, y, x, core],
+                dst_ref=got_z[unit].at[z],
+                send_sem=send_sems.at[copies.count],
+                recv_sem=z_sems.at[unit, z],
+                device_id=device_at(y, x, core, t),
+                device_id_type=MESH,
+            )
+            copies.count += 1
+
+            @pl.when(z != t)
+            def _():
+                copy.start()
+
+            conditional.append((t, copy))
+
+    def spot_of(unit, where):
+        return outs[unit].at[(slice(None), *where)]
+
+    def half_spot(unit, where, side):
+        count = outs[unit].shape[0]
+        if count > 1:
+            return outs[unit].at[(halves(count)[side], *where)]
+        return outs[unit].at[(slice(None), *where, halves(outs[unit].shape[4])[side])]
+
+    def over_z(group):
+        for unit in group:
+            mine, other, total = grads[unit], got_z[unit], result[unit]
+            for bits in SWAP_TENSOR:
+                t = flipped(z, bits)
+                wait_arrival(
+                    other.at[t], z_sems.at[unit, t], spare.at[0], device_at(y, x, core, t)
+                )
+
+            def body(entry, carry):
+                value = mine[z, entry, y, x, core].astype(jnp.float32)
+                for bits in SWAP_TENSOR:
+                    value = value + other[flipped(z, bits), entry].astype(jnp.float32)
+                total[entry] = value.astype(total.dtype)
+                return carry
+
+            lax.fori_loop(0, mine.shape[1], body, 0)
+            spot = spot_of(unit, (y, x, core))
+            pltpu.make_async_copy(total, spot, load_sems.at[3 + unit]).start()
+            copies.send(total, spot, spread_sems.at[unit, 0], at_x)
+            copies.send(total, spot, spread_sems.at[unit, 1], at_y)
+            copies.send(total, spot, core_sems.at[unit, 0], at_core)
+
+    def spread(group):
+        for unit in group:
+            spot = spot_of(unit, (y, 1 - x, core))
+            wait_arrival(spot, spread_sems.at[unit, 0], spare.at[0], at_x)
+            first = half_spot(unit, (y, 1 - x, core), 0)
+            copies.send(first, first, spread_sems.at[unit, 2], at_y)
+            copies.send(spot, spot, core_sems.at[unit, 1], at_core)
+            spot = spot_of(unit, (1 - y, x, core))
+            wait_arrival(spot, spread_sems.at[unit, 1], spare.at[0], at_y)
+            second = half_spot(unit, (1 - y, x, core), 1)
+            copies.send(second, second, spread_sems.at[unit, 3], at_x)
+            copies.send(spot, spot, core_sems.at[unit, 2], at_core)
+
+    def corner(group):
+        for unit in group:
+            where = (1 - y, 1 - x, core)
+            wait_arrival(half_spot(unit, where, 0), spread_sems.at[unit, 2], spare.at[0], at_y)
+            wait_arrival(half_spot(unit, where, 1), spread_sems.at[unit, 3], spare.at[0], at_x)
+            spot = spot_of(unit, where)
+            copies.send(spot, spot, core_sems.at[unit, 3], at_core)
+
+    def finish(group):
+        for unit in group:
+            pltpu.make_async_copy(
+                result[unit], spot_of(unit, (y, x, core)), load_sems.at[3 + unit]
+            ).wait()
+            for entry, where in enumerate(((y, x), (y, 1 - x), (1 - y, x), (1 - y, 1 - x))):
+                spot = spot_of(unit, (*where, 1 - core))
+                wait_arrival(spot, core_sems.at[unit, entry], spare.at[0], at_core)
+
+    def mlp(step):
+        t, slot = ITEM_ORDER[step], step % 2
+        for copy in streams[step]:
+            copy.wait()
+        inner = (back_dot(low[...], downs[slot]) * slopes[slot]).astype(jnp.bfloat16)
+        grad_inner[...] = inner
+        rows_out[8 + t : 9 + t] = jnp.sum(inner.astype(jnp.float32), axis=0, keepdims=True)
+        put(2, t, contract_rows(rounded[...], grad_inner[...]))
+        put(3, t, contract_rows(actives[slot], low[...]))
+        upstream[...] += back_dot(grad_inner[...], ups[slot])
+        if step < 2:
+            streams.append(stream(step + 2))
+        share(step)
+
+    def project(step):
+        t = ITEM_ORDER[step]
+        put(0, t, contract_rows(grad_qkv[t], rounded[...]))
+        upstream[...] += product(grad_qkv[t], attend_w[t])
+        share(4 + step)
+
+    rows_out[...] = jnp.zeros_like(rows_out)
+    for copy in first_loads:
+        copy.wait()
+    low[...] = grad[...].astype(low.dtype)
+    rows_out[4:5] = jnp.sum(low[...].astype(jnp.float32), axis=0, keepdims=True)
+    upstream[...] = jnp.zeros_like(upstream)
+    mlp(0)
+    mlp(1)
+    core_sum(0)
+    mlp(2)
+    core_sum(1)
+    mlp(3)
+    core_sum(2)
+    one(0)
+    rows_out[2:3], rows_out[3:4] = norm_back_into(grad, values, upstream, gains[2:3])
+    later_loads = [load(hidden, values, 2), load(normed, rounded, 1)]
+    low[...] = grad[...].astype(low.dtype)
+    for t in range(4):
+        put(1, t, contract_rows(mixed[t], low[...]))
+        grad_mixed[t] = back_dot(low[...], merge_w[t]).astype(grad_mixed.dtype)
+    core_sum(3)
+    one(1)
+    attend_back_into(qkv, allowed, grad_mixed, grad_qkv, 0, 2)
+    one(2)
+    two(0)
+    attend_back_into(qkv, allowed, grad_mixed, grad_qkv, 2, 4)
+    one(3)
+    two(1)
+    upstream[...] = jnp.zeros_like(upstream)
+    for copy in later_loads:
+        copy.wait()
+    project(0)
+    project(1)
+    core_sum(4)
+    two(2)
+    project(2)
+    core_sum(5)
+    two(3)
+    project(3)
+    core_sum(6)
+    one(4)
+    rows_out[0:1], rows_out[1:2] = norm_back_into(grad, values, upstream, gains[0:1])
+    core_sum(7)
+    one(5)
+    over_z(MLP_GROUP)
+    two(4)
+    one(6)
+    two(5)
+    one(7)
+    spread(MLP_GROUP)
+    two(6)
+    corner(MLP_GROUP)
+    two(7)
+    over_z(ATTEND_GROUP)
+    spread(ATTEND_GROUP)
+    corner(ATTEND_GROUP)
+    finish(MLP_GROUP)
+    finish(ATTEND_GROUP)
+    copies.finish()
+    for t, copy in conditional:
+
+        @pl.when(z != t)
+        def _(copy=copy):
+            copy.wait_send()
+
+
+def owner_shape(weight):
+    count = 1 if weight.shape[1] == D else weight.shape[1] // 64
+    return (count, 2, 2, 2, weight.shape[1] // (8 * count), D)
+
+
+def layer_back_reduce(layer_index, grad, allowed, gains, weights, stored):
+    hidden, normed, qkv, mixed, hidden_mid, normed_mlp, slope, active = stored
+    attend_w, merge_w, up_w, down_w = weights
+    rows, heads = grad.shape[0], attend_w.shape[1] // (3 * HEAD_DIM)
+    low, full = jnp.bfloat16, jnp.float32
+    vmem = pl.BlockSpec(memory_space=pltpu.VMEM)
+    anywhere = pl.BlockSpec(memory_space=pl.ANY)
+    shapes = [owner_shape(weight) for weight in weights]
+    scratch = []
+    for lead in ((4, 2, 2, 2), (4, 2, 2), (4, 2), (4,), (4,), ()):
+        for shape in shapes:
+            whole = lead[:1] + shape[:1] + lead[1:] + shape[4:]
+            scratch.append(pltpu.VMEM(whole, low))
+    dma = pltpu.SemaphoreType.DMA
+    scratch += [
+        pltpu.VMEM((rows, D), low),
+        pltpu.VMEM((rows, D), low),
+        pltpu.VMEM((4, rows, heads * HEAD_DIM), low),
+        pltpu.VMEM((4, rows, heads * 3 * HEAD_DIM), low),
+        pltpu.VMEM((rows, D), full),
+        pltpu.VMEM((rows, D), full),
+        pltpu.VMEM((rows, D), low),
+        pltpu.VMEM((2, rows, D), slope.dtype),
+        pltpu.VMEM((2, rows, D), low),
+        pltpu.VMEM((2, D, D), low),
+        pltpu.VMEM((2, D, D), low),
+        dma((4 * 24,)),
+        dma((4, 3, 4)),
+        dma((4, 4)),
+        dma((4, 4)),
+        dma((4, 4)),
+        dma((1,)),
+        dma((7,)),
+        dma((2, 4)),
+    ]
+    outs = [jax.ShapeDtypeStruct((rows, D), full), jax.ShapeDtypeStruct((16, D), full)]
+    outs += [jax.ShapeDtypeStruct(shape, low) for shape in shapes]
+    after, rows_out, *sums = pl.pallas_call(
+        layer_back_kernel,
+        out_shape=outs,
+        in_specs=[anywhere] * 9 + [vmem] * 6,
+        out_specs=[vmem] * 2 + [anywhere] * 4,
+        scratch_shapes=scratch,
+        compiler_params=pltpu.CompilerParams(
+            collective_id=2 + layer_index, has_side_effects=True, vmem_limit_bytes=BACK_LIMIT
+        ),
+        name="layer_back_reduce",
+    )(
+        grad, hidden, hidden_mid, normed, normed_mlp, slope, active, up_w, down_w,
+        qkv, mixed, allowed, gains, attend_w, merge_w,
     )
-    stacked = jnp.stack([grad_queries, grad_keys, grad_values]).astype(jnp.bfloat16)
-    stacked = stacked.reshape(3, images, tensor_count, -1, P_SIZE, HEAD_DIM)
-    return jnp.transpose(stacked, (1, 4, 2, 0, 3, 5)).reshape(images * P_SIZE, -1)
+    return (after, rows_out, [entry.reshape(-1, D) for entry in sums])
+
+
+BACK_LIMIT = 66 * 1000 * 1000
 
 
 def shards(
@@ -770,19 +1322,26 @@
     patch_values = patches.astype(jnp.float32)
     local_valid = lax.dynamic_slice_in_dim(valid_mask, tensor_index * shard_count, shard_count, 0)
     live_mask = local_valid.astype(jnp.float32)[:, None]
-    allowed = build_allowed(local_valid, P_SIZE)
+    allowed = build_allowed(local_valid, P_SIZE).astype(jnp.float32)
     embed_full = embed_weight.astype(jnp.float32)
     shards = []
     for layer_index in range(NL):
         shards.append(jnp.swapaxes(attend_weight[layer_index], 1, 2).reshape(-1, D))
         shards.append(merge_weight[layer_index])
-        shards.append(jnp.swapaxes(up_weight[layer_index], 0, 1))
+        shards.append(up_weight[layer_index])
         shards.append(down_weight[layer_index])
     wholes, bias_all = gather_weights(shards, up_bias)
-    weights = [
-        (*wholes[4 * layer_index : 4 * layer_index + 4], bias_all[:, layer_index].reshape(-1))
-        for layer_index in range(NL)
-    ]
+    layers = []
+    for layer_index in range(NL):
+        weights = [
+            whole.reshape(tensor_count, -1, D)
+            for whole in wholes[4 * layer_index : 4 * layer_index + 4]
+        ]
+        gains = jnp.stack(
+            [attn_gain[layer_index], attn_offset[layer_index], mlp_gain[layer_index]]
+            + [mlp_offset[layer_index], down_bias[layer_index]]
+        )
+        layers.append((gains, bias_all[:, layer_index], weights))
     choose = class_ids[:, None] == lax.broadcasted_iota(jnp.int32, (local_images, CLASSES), 1)
     class_rows = product(choose.astype(jnp.bfloat16), class_table)
     hidden = product(patches, embed_weight) + embed_bias
@@ -790,23 +1349,10 @@
     hidden = (hidden + class_rows[:, None]).reshape(shard_count, D)
     stored = []
     for layer_index in range(NL):
-        attend_full, merge_full, up_full, down_full, bias_full = weights[layer_index]
-        normed = layer_norm(hidden, attn_gain[layer_index], attn_offset[layer_index]).astype(
-            jnp.bfloat16
-        )
-        qkv_low = product_back(normed, attend_full).astype(jnp.bfloat16)
-        blocks = head_blocks(qkv_low, tensor_count)
-        mixed_low, log_total = attend(blocks, allowed)
-        hidden_mid = hidden + product(mixed_low, merge_full)
-        normed_mlp = layer_norm(hidden_mid, mlp_gain[layer_index], mlp_offset[layer_index]).astype(
-            jnp.bfloat16
-        )
-        pre_active = product_back(normed_mlp, up_full) + bias_full
-        active = gelu_exact(pre_active).astype(jnp.bfloat16)
-        stored.append(
-            (hidden, normed, blocks, log_total, mixed_low, hidden_mid, normed_mlp, pre_active, active)
-        )
-        hidden = hidden_mid + (product(active, down_full) + down_bias[layer_index])
+        gains, bias, weights = layers[layer_index]
+        *kept, after = layer_forward(hidden, allowed, gains, bias, weights)
+        stored.append((hidden, *kept))
+        hidden = after
     final = layer_norm(hidden, final_gain, final_offset)
     final_low = final.astype(jnp.bfloat16)
     head_out = product(final_low, head_weight) + head_bias
@@ -830,51 +1376,22 @@
     grad_head_low = grad_head.astype(jnp.bfloat16)
     head_weight_grad = contract_rows(grad_head_low, final_low)
     head_bias_grad = jnp.sum(grad_head_low.astype(jnp.float32), axis=0)
-    grad_final = product_back(grad_head_low, head_weight)
+    grad_final = back_dot(grad_head_low, head_weight)
     grad_hidden, final_gain_grad, final_offset_grad = norm_backward(
         hidden, final_gain, final_offset, grad_final
     )
     rows_of = {}
     split_list = [None] * NL
     for layer_index in reversed(range(NL)):
-        hidden_in, normed, blocks, log_total, mixed_low, hidden_mid, normed_mlp, pre_active, active = (
-            stored[layer_index]
-        )
-        attend_full, merge_full, up_full, down_full, bias_full = weights[layer_index]
-        grad_out_mlp = grad_hidden.astype(jnp.bfloat16)
-        down_bias_grad = jnp.sum(grad_out_mlp.astype(jnp.float32), axis=0)
-        down_grad = contract_rows(active, grad_out_mlp)
-        grad_active = product_back(grad_out_mlp, down_full)
-        outputs, gelu_pull = jax.vjp(gelu_exact, pre_active)
-        grad_inner = gelu_pull(grad_active)[0].astype(jnp.bfloat16)
-        up_bias_grad = jnp.sum(grad_inner.astype(jnp.float32), axis=0)
-        up_grad = contract_rows(grad_inner, normed_mlp)
-        grad_normed = product(grad_inner, up_full)
-        grad_from, mlp_gain_grad, mlp_offset_grad = norm_backward(
-            hidden_mid, mlp_gain[layer_index], mlp_offset[layer_index], grad_normed
-        )
-        grad_hidden = grad_hidden + grad_from
-        grad_out_attn = grad_hidden.astype(jnp.bfloat16)
-        merge_grad = contract_rows(mixed_low, grad_out_attn)
-        grad_mixed = product_back(grad_out_attn, merge_full).astype(jnp.bfloat16)
-        grad_qkv = attend_back(blocks, allowed, log_total, grad_mixed, tensor_count)
-        attend_grad = contract_rows(grad_qkv, normed)
-        grad_normed = product(grad_qkv, attend_full)
-        grad_from, attn_gain_grad, attn_offset_grad = norm_backward(
-            hidden_in, attn_gain[layer_index], attn_offset[layer_index], grad_normed
-        )
-        grad_hidden = grad_hidden + grad_from
-        rows_of[layer_index] = [
-            attn_gain_grad[None],
-            attn_offset_grad[None],
-            mlp_gain_grad[None],
-            mlp_offset_grad[None],
-            down_bias_grad[None],
-            up_bias_grad.reshape(-1, D),
-        ]
-        split_list[layer_index] = [
-            grad.astype(jnp.bfloat16) for grad in (attend_grad, merge_grad, up_grad, down_grad)
-        ]
+        gains, bias, weights = layers[layer_index]
+        if fast_mesh():
+            grad_hidden, rows_of[layer_index], split_list[layer_index] = layer_back_reduce(
+                layer_index, grad_hidden, allowed, gains, weights, stored[layer_index]
+            )
+        else:
+            grad_hidden, rows_of[layer_index], *split_list[layer_index] = layer_backward(
+                grad_hidden, allowed, gains, weights, stored[layer_index]
+            )
     per_image = grad_hidden.reshape(local_images, P_SIZE, D)
     image_count = device_count * local_images
     image_index = device_index * local_images
@@ -893,19 +1410,17 @@
         final_offset_grad[None],
         jnp.pad(head_bias_grad, (0, D - 2 * PV))[None],
     ]
-    for entry in rows_of[0] + rows_of[1]:
-        small.append(entry)
-    small.append(id_rows)
+    small += [rows_of[0], rows_of[1], id_rows]
     lengths = [entry.shape[0] for entry in small]
     joined = jnp.concatenate(small, axis=0)
     joined = jnp.pad(joined, ((0, -joined.shape[0] % (8 * device_count)), (0, 0)))
-    sums, small_sum = reduce_weights(split_list[0] + split_list[1], joined)
+    sums, small_sum = reduce_weights(split_list, joined)
     for layer_index in range(NL):
         attend_sum, merge_sum, up_sum, down_sum = sums[4 * layer_index : 4 * layer_index + 4]
         split_list[layer_index] = (
             jnp.swapaxes(attend_sum.reshape(3, -1, D), 1, 2).astype(jnp.float32),
             merge_sum.astype(jnp.float32),
-            jnp.swapaxes(up_sum, 0, 1).astype(jnp.float32),
+            up_sum.astype(jnp.float32),
             down_sum.astype(jnp.float32),
         )
     patches_grad = direct_grad + lax.dot_general(
@@ -921,22 +1436,17 @@
     for length in lengths:
         small_list.append(small_sum[begin : begin + length])
         begin += length
-    id_sums = small_list[20][:, :image_count].astype(jnp.int32)
+    id_sums = small_list[10][:, :image_count].astype(jnp.int32)
     all_ids = id_sums[0] * 32 + id_sums[1]
     choose_all = all_ids[:, None] == lax.broadcasted_iota(
         jnp.int32, (image_count, CLASSES), 1
     )
     class_grad = precise_rows(choose_all.astype(jnp.float32), small_list[3])
-    layer_rows = [small_list[8:14], small_list[14:20]]
-    own_bias = [
-        lax.dynamic_slice_in_dim(
-            entry[5].reshape(tensor_count, -1), tensor_index, 1, 0
-        )
-        for entry in layer_rows
-    ]
+    layer_rows = small_list[8:10]
+    own_bias = [lax.dynamic_slice_in_dim(entry, 8 + tensor_index, 1, 0) for entry in layer_rows]
     split_stack = [jnp.stack([entry[member] for entry in split_list]) for member in range(4)]
     shared_stack = [
-        jnp.concatenate([entry[member] for entry in layer_rows], axis=0) for member in range(5)
+        jnp.stack([entry[member] for entry in layer_rows]) for member in range(5)
     ]
     return (
         latents,

time: 605 us -> 495 us (0.82)
  matrix products: 150 us -> 9.41 us
  Pallas kernels: 320 us -> 436 us
  local copies, waits for them, and re-layouts: 85.9 us -> 17.5 us
  other arithmetic: 36.9 us -> 25.1 us
    pallas_call x0 -> x4, Pallas kernels: none -> 271 us  [the longest x2 211 us: layer_back_reduce(): pl.pallas_call(layer_back_kernel, out_shape=outs, in_specs=[anywhere] * 9...]
    pallas_call x1, Pallas kernels: 205 us -> 50 us  [reduce_all(): pl.pallas_call(functools.partial(reduce_kernel, groups, spread_all), out_...]
    dot_general x21 -> x1, matrix products: 92.5 us -> 0.76 us  [back_dot(): lax.dot_general(former, latter, (((1,), (1,)), ((), ())), preferred_eleme...]
    dot_general x9 -> x1, matrix products: 33.4 us -> 0.93 us  [contract_rows(): lax.dot_general(former, latter, (((0,), (0,)), ((), ())), preferred_eleme...]
    dot_general x11 -> x3, matrix products: 19 us -> 2.28 us  [product(): return jnp.dot(former, latter, preferred_element_type=jnp.float32)]
    unnamed x289 -> x82, local copies, waits for them, and re-layouts: 17.4 us -> 1.42 us
    reshape x6 -> x0, local copies, waits for them, and re-layouts: 14.2 us -> none  [the longest x2 12.1 us: head_blocks(): blocks = qkv_low.reshape(images, P_SIZE, tensor_count, 3, -1, HEAD_DIM)]
    convert_element_type x6 -> x0, local copies, waits for them, and re-layouts: 10.7 us -> none  [the longest x2 8.56 us: shards(): qkv_low = product_back(normed, attend_full).astype(jnp.bfloat16)]
where the time goes in v2:
time: 495 us; the launch traced here: 489 us
  Pallas kernels  436 us (88%)
  other arithmetic  25.1 us (5%)
  local copies, waits for them, and re-layouts  17.5 us (4%)
  matrix products  9.41 us (2%)
    pallas_call x2, Pallas kernels, layer_back_reduce(): pl.pallas_call(layer_back_kernel, out_shape=outs, in_specs=[anywhere] * 9...  211 us
    pallas_call x1, Pallas kernels, gather_all(): pl.pallas_call(functools.partial(gather_kernel, units // 4), out_shape=ou...  116 us
    pallas_call x2, Pallas kernels, layer_forward(): pl.pallas_call(layer_forward_kernel, out_shape=outs, in_specs=[vmem] * 8,...  59.5 us
    pallas_call x1, Pallas kernels, reduce_all(): pl.pallas_call(functools.partial(reduce_kernel, groups, spread_all), out_...  50 us

profile of v2, /device:TPU:0, one launch (start us, length us, event | category | flops | bytes accessed | tf_op | source)
XLA Modules:
  0.0 489.5 jit_solution(7824709248589258290)
XLA Ops:
  0.7 0.8 dynamic-slice_compare_fusion
  1.7 0.9 and_convert_fusion.refs_1_.refs_11_
  2.6 3.3 fusion.27
  5.9 1.6 fusion.26
  7.5 0.8 copy-done.7
  8.3 1.3 fusion.28
  9.6 0.8 fusion.30
  11.1 115.6 %gather_weights.1 = (bf16[4,9,8,8,768]{4,3,2,1,0:T(8,128)(2,1)}, bf16[4,3,8,8,768]{4,3,2,1,0:T(8,128)(2,1)}, bf16[4,8,96,768]{3,2,1,0:T(8,128)(2,1)}, bf16[4,8,9...) custom-call(bf16[9,8,8,768]{3,2,1,0:T(8,128)(2,1)} %bitcast.104, ...), custom_call_target="tpu_custom_call" | custom-call | tf_op jit(solution)/shard_map/gather_weights/pallas_call | solution.py:372
  126.7 1.0 copy.46
  129.5 1.6 bitcast_add_fusion.refs_0_.refs_1_
  131.1 29.8 %layer_forward.2 = (bf16[512,768]{1,0:T(8,128)(2,1)}, bf16[4,512,576]{2,1,0:T(8,128)(2,1)}, bf16[4,512,192]{2,1,0:T(8,128)(2,1)}, f32[512,768]{1,0:T(8,128)}, bf...) custom-call(f32[512,768]{1,0:T(8,128)} %bitcast_add_fusion.refs_0_.ref, ...), custom_call_target="tpu_custom_call" | custom-call | tf_op jit(solution)/shard_map/layer_forward/pallas_call | solution.py:859
  161.5 29.7 %layer_forward.3 = (bf16[512,768]{1,0:T(8,128)(2,1)}, bf16[4,512,576]{2,1,0:T(8,128)(2,1)}, bf16[4,512,192]{2,1,0:T(8,128)(2,1)}, f32[512,768]{1,0:T(8,128)}, bf...) custom-call(f32[512,768]{1,0:T(8,128)} %get-tuple-element.63.refs_0_.r, ...), custom_call_target="tpu_custom_call" | custom-call | tf_op jit(solution)/shard_map/layer_forward/pallas_call | solution.py:859
  191.2 1.7 reduce_sum.107
  194.4 0.8 fusion.25
  195.5 0.9 convolution_convert_fusion
  196.4 0.8 multiply_reduce_fusion
  197.8 1.3 broadcast_add_fusion.refs_0_
  199.1 102.9 %layer_back_reduce.2 = (f32[512,768]{1,0:T(8,128)}, f32[16,768]{1,0:T(8,128)}, bf16[9,2,2,2,8,768]{5,4,3,2,1,0:T(8,128)(2,1)}, bf16[3,2,2,2,8,768]{5,4,3,2,1,0:T...) custom-call(f32[512,768]{1,0:T(8,128)} %broadcast_add_fusion.refs_0_, ...), custom_call_target="tpu_custom_call" | custom-call | tf_op jit(solution)/shard_map/layer_back_reduce/pallas_call | solution.py:1270
  302.0 108.2 %layer_back_reduce.3 = (f32[512,768]{1,0:T(8,128)}, f32[16,768]{1,0:T(8,128)}, bf16[9,2,2,2,8,768]{5,4,3,2,1,0:T(8,128)(2,1)}, bf16[3,2,2,2,8,768]{5,4,3,2,1,0:T...) custom-call(f32[512,768]{1,0:T(8,128)} %get-tuple-element.76.refs_0_, ...), custom_call_target="tpu_custom_call" | custom-call | tf_op jit(solution)/shard_map/layer_back_reduce/pallas_call | solution.py:1270
  410.2 1.6 reduce_sum.137
  414.1 0.9 pad.19
  415.0 50.0 %reduce_gradients.1 = bf16[4,1,2,2,2,16,768]{6,5,4,3,2,1,0:T(8,128)(2,1)} custom-call(bf16[4,1,2,2,2,16,768]{6,5,4,3,2,1,0:T(8,128)(2,1)} %bitcast.105), custom_call_target="tpu_custom_call" | custom-call | tf_op jit(solution)/shard_map/reduce_gradients/pallas_call | solution.py:633
  465.0 1.4 bitcast_convert_fusion
  466.5 0.7 slice_reduce_fusion
  467.8 2.5 maximum_convert_fusion.1
  471.0 3.8 maximum_convert_fusion
  476.0 1.1 maximum_convert_fusion.3
  477.1 2.0 maximum_convert_fusion.2
  480.3 3.2 fusion.2
  483.6 0.9 slice.214
  484.5 0.7 slice_bitcast_fusion
  486.4 1.5 convolution_add_fusion
  (145 shorter events, 13.9 us)
Async XLA Ops:
  0.7 193.1 %copy-start = (bf16[768,96]{0,1:T(8,128)(2,1)S(1)}, bf16[768,96]{0,1:T(8,128)(2,1)}, u32[]{:S(2)}) copy-start(bf16[768,96]{0,1:T(8,128)(2,1)} %param.42) | copy-start | bytes 442372
  2.6 3.3 copy-start.6
  5.9 2.3 copy-start.7
  8.3 2.2 copy-start.34
  11.0 117.3 %copy-start.30 = (f32[2,768]{1,0:T(2,128)S(1)}, f32[2,768]{1,0:T(2,128)}, u32[]{:S(2)}) copy-start(f32[2,768]{1,0:T(2,128)} %param.39) | copy-start | bytes 18436
  11.0 117.3 %copy-start.31 = (f32[2,768]{1,0:T(2,128)S(1)}, f32[2,768]{1,0:T(2,128)}, u32[]{:S(2)}) copy-start(f32[2,768]{1,0:T(2,128)} %param.35) | copy-start | bytes 18436
  11.0 117.3 %copy-start.32 = (f32[2,768]{1,0:T(2,128)S(1)}, f32[2,768]{1,0:T(2,128)}, u32[]{:S(2)}) copy-start(f32[2,768]{1,0:T(2,128)} %param.34) | copy-start | bytes 18436
  11.1 117.4 %copy-start.33 = (f32[2,768]{1,0:T(2,128)S(1)}, f32[2,768]{1,0:T(2,128)}, u32[]{:S(2)}) copy-start(f32[2,768]{1,0:T(2,128)} %param.31) | copy-start | bytes 18436
  11.1 117.4 %copy-start.29 = (f32[2,768]{1,0:T(2,128)S(1)}, f32[2,768]{1,0:T(2,128)}, u32[]{:S(2)}) copy-start(f32[2,768]{1,0:T(2,128)} %param.30) | copy-start | bytes 18436
  11.1 118.0 %copy-start.19 = (bf16[256,768]{1,0:T(8,128)(2,1)S(1)}, bf16[256,768]{1,0:T(8,128)(2,1)}, u32[]{:S(2)}) copy-start(bf16[256,768]{1,0:T(8,128)(2,1)} %param.28) | copy-start | bytes 1179652
  11.1 118.1 %copy-start.38 = (s32[2]{0:T(128)S(1)}, s32[2]{0:T(128)}, u32[]{:S(2)}) copy-start(s32[2]{0:T(128)} %param.25) | copy-start | bytes 28
  126.7 2.5 copy-start.8
  126.7 2.8 copy-start.14
  126.7 2.8 copy-start.24
  126.7 2.8 copy-start.35
  191.2 2.2 copy-start.28
  191.2 2.2 copy-start.36
  410.2 1.9 copy-start.3
  410.2 2.0 copy-start.15
  465.0 2.8 copy-start.10
  465.0 2.8 copy-start.11
  466.4 3.9 copy-start.4
  467.8 3.2 copy-start.9
  471.0 5.0 %copy-start.22 = (bf16[3,2,2,2,8,768]{5,4,3,2,1,0:T(8,128)(2,1)S(1)}, bf16[3,2,2,2,8,768]{5,4,3,2,1,0:T(8,128)(2,1)}, u32[]{:S(2)}) copy-start(bf16[3,2,2,2,8,768]{5,4,3,2,1,0:T(8,128)(2,1)} %get-tuple-element.90) | copy-start | bytes 884740
  471.0 5.0 %copy-start.23 = (bf16[3,2,2,2,8,768]{5,4,3,2,1,0:T(8,128)(2,1)S(1)}, bf16[3,2,2,2,8,768]{5,4,3,2,1,0:T(8,128)(2,1)}, u32[]{:S(2)}) copy-start(bf16[3,2,2,2,8,768]{5,4,3,2,1,0:T(8,128)(2,1)} %get-tuple-element.89) | copy-start | bytes 884740
  474.8 2.3 copy-start.12
  474.8 2.3 copy-start.13
  477.1 3.2 copy-start.5
  483.6 2.9 copy-start.21
  483.6 2.9 copy-start.25
  483.6 5.7 %copy-start.1 = (bf16[768,96]{0,1:T(8,128)(2,1)S(1)}, bf16[768,96]{0,1:T(8,128)(2,1)}, u32[]{:S(2)}) copy-start(bf16[768,96]{0,1:T(8,128)(2,1)} %param.42) | copy-start | bytes 442372
  484.5 3.5 copy-start.16
  (8 other events, 10.5 us)

commit v3 on v2

--- a/solution.py
+++ b/solution.py
@@ -204,14 +204,22 @@
     return ref.at[(*lead, b, halves(ref.shape[len(lead) + 1])[side])]
 
 
-def gather_kernel(layer_count, *refs):
-    per_layer = 4
-    units = layer_count * per_layer
+GROUP = 2
+
+
+def forward_kernel(*refs):
+    units = 4 * NL
     shards = refs[:units]
-    bias = refs[units]
-    fulls = refs[units + 1 : 2 * units + 1]
-    bias_full = refs[2 * units + 1]
-    send_sems, z_sems, xy_sems, core_sems, local_sems, bias_sems, spare = refs[2 * units + 2 :]
+    bias, patches, embed_w, embed_b, table, class_rows, valid = refs[units : units + 7]
+    gains = refs[units + 7 : units + 7 + NL]
+    outs = refs[units + 7 + NL :]
+    fulls, bias_full, hidden_out = outs[:units], outs[units], outs[units + 1]
+    kept = [outs[units + 2 + 8 * layer : units + 10 + 8 * layer] for layer in range(NL)]
+    rest = outs[units + 2 + 8 * NL :]
+    weights, (bias_v, allowed, hidden_a, hidden_b) = rest[:4], rest[4:8]
+    stores = rest[8:15]
+    send_sems, z_sems, xy_sems, core_sems, local_sems, bias_sems, spare = rest[15:22]
+    weight_sems, keep_sems = rest[22:]
     y, x, core, z = place()
     b = y * 4 + x * 2 + core
     over_x = y * 4 + (1 - x) * 2 + core
@@ -234,14 +242,13 @@
     greet(partners())
     copies = Copies(send_sems)
     conditional = []
-    locals_ = []
+    local_of = {}
     for unit in range(units):
         copy = pltpu.make_async_copy(shards[unit], fulls[unit].at[z], local_sems.at[unit])
         copy.start()
-        locals_.append(copy)
-    copy = pltpu.make_async_copy(bias, bias_full.at[z], local_sems.at[units])
-    copy.start()
-    locals_.append(copy)
+        local_of[unit] = copy
+    local_bias = pltpu.make_async_copy(bias, bias_full.at[z], local_sems.at[units])
+    local_bias.start()
     for entry, bits in enumerate(SWAP_TENSOR):
         copies.send(
             bias,
@@ -251,7 +258,7 @@
         )
 
     def of_layer(layer):
-        return range(layer * per_layer, (layer + 1) * per_layer)
+        return range(layer * GROUP, (layer + 1) * GROUP)
 
     def send_if_middle(source, target, recv_sem, device):
         slot = send_sems.at[copies.count]
@@ -270,6 +277,17 @@
             copy.start()
 
         conditional.append(copy)
+
+    def take_bias():
+        for entry, bits in enumerate(SWAP_TENSOR):
+            t = flipped(z, bits)
+            wait_arrival(
+                bias_full.at[t], bias_sems.at[entry], spare.at[0], device_at(y, x, core, t)
+            )
+        local_bias.wait()
+        copy = pltpu.make_async_copy(bias_full, bias_v, weight_sems.at[units])
+        copy.start()
+        copy.wait()
 
     def begin(layer):
         for unit in of_layer(layer):
@@ -317,7 +335,7 @@
             piece = spread_piece(fulls[unit], (t,), corner)
             copies.send(piece, piece, core_sems.at[unit, step, 3], at_core)
 
-    def take_core(layer, step):
+    def take_core_step(layer, step):
         t = order[step]
         for unit in of_layer(layer):
             for entry, owner in enumerate((b, over_x, over_y, corner)):
@@ -325,35 +343,159 @@
                 piece = spread_piece(fulls[unit], (t,), other)
                 wait_arrival(piece, core_sems.at[unit, step, entry], spare.at[0], at_core)
 
+    pending = {}
+
+    def keep(entry, layer, source, target):
+        copy = pltpu.make_async_copy(source, target, keep_sems.at[layer, entry])
+        copy.start()
+        pending[entry] = copy
+
+    def free(*entries):
+        for entry in entries:
+            if entry in pending:
+                pending.pop(entry).wait()
+
+    def fetch(group):
+        take_core(group)
+        copies = []
+        for unit in of_layer(group):
+            if unit in local_of:
+                local_of.pop(unit).wait()
+            target = weights[unit % 4]
+            copy = pltpu.make_async_copy(
+                fulls[unit].reshape(target.shape), target, weight_sems.at[unit]
+            )
+            copy.start()
+            copies.append(copy)
+        return copies
+
+    def take_core(group):
+        for step in range(3):
+            take_core_step(group, step)
+
+    def embed():
+        row_index = lax.broadcasted_iota(jnp.int32, (P_SIZE, P_SIZE), 0)
+        col_index = lax.broadcasted_iota(jnp.int32, (P_SIZE, P_SIZE), 1)
+        for image in range(patches.shape[0] // P_SIZE):
+            key_valid = jnp.where(row_index == col_index, 1.0, valid[image : image + 1])
+            allowed[image] = jnp.where(col_index <= row_index, key_valid, 0.0)
+            rows = slice(image * P_SIZE, (image + 1) * P_SIZE)
+            value = product(patches[rows], embed_w[...]) + embed_b[...]
+            value = value + table[...].astype(jnp.float32)
+            hidden_a[rows] = value + class_rows[image : image + 1]
+        keep(7, 0, hidden_a, hidden_out)
+
+    normed, qkv, mixed, hidden_mid, normed_mlp, slope, active = stores
+    attend_w, merge_w, up_w, down_w = weights
+
+    def chunks(group):
+        layer = group // 2
+        gain, outputs = gains[layer], kept[layer]
+        before, after = (hidden_a, hidden_b) if layer % 2 == 0 else (hidden_b, hidden_a)
+
+        def start():
+            free(0, 1)
+            norm_into(before, gain[0:1], gain[1:2], normed)
+
+            def project(t):
+                qkv[t] = back_dot(normed[...], attend_w[t]).astype(qkv.dtype)
+
+            each_part(project)
+            keep(0, layer, normed, outputs[0])
+            keep(1, layer, qkv, outputs[1])
+
+        def attend_first():
+            free(2)
+            attend_into(qkv, allowed, mixed, 0, 2)
+
+        def attend_second():
+            attend_into(qkv, allowed, mixed, 2, 4)
+            keep(2, layer, mixed, outputs[2])
+
+        def merge():
+            free(3, 4)
+            total = before[...]
+            for t in range(4):
+                total = total + product(mixed[t], merge_w[t])
+            hidden_mid[...] = total
+            norm_into(hidden_mid, gain[2:3], gain[3:4], normed_mlp)
+            keep(3, layer, hidden_mid, outputs[3])
+            keep(4, layer, normed_mlp, outputs[4])
+
+        def up(t):
+            inner = product(normed_mlp[...], up_w[t]) + bias_v[t, layer : layer + 1]
+            value, rise = gelu_parts(inner)
+            active[t] = value.astype(active.dtype)
+            slope[t] = rise.astype(slope.dtype)
+
+        def up_first():
+            free(5, 6)
+            each_part(up, 0, 2)
+
+        def up_second():
+            each_part(up, 2, 4)
+            keep(5, layer, slope, outputs[5])
+            keep(6, layer, active, outputs[6])
+
+        def down():
+            free(7 if layer % 2 else 8)
+            total = hidden_mid[...] + gain[4:5]
+            for t in range(4):
+                total = total + product(active[t], down_w[t])
+            after[...] = total
+            keep(8 - layer % 2, layer, after, outputs[7])
+
+        def nothing():
+            pass
+
+        if group % 2 == 0:
+            return [start, attend_first, attend_second, merge]
+        return [up_first, up_second, down, nothing]
+
+    groups = units // GROUP
     begin(0)
-    for layer in range(layer_count):
-        take_z(layer, 0)
-        take_z(layer, 1)
-        if layer:
-            take_corner(layer - 1, 1)
-        take_xy(layer, 0)
-        take_z(layer, 2)
-        if layer + 1 < layer_count:
-            begin(layer + 1)
-        if layer:
-            take_corner(layer - 1, 2)
-        take_xy(layer, 1)
-        take_corner(layer, 0)
-        take_xy(layer, 2)
-    take_corner(layer_count - 1, 1)
-    take_corner(layer_count - 1, 2)
-    for layer in range(layer_count):
-        for step in range(3):
-            take_core(layer, step)
-    for entry, bits in enumerate(SWAP_TENSOR):
-        wait_arrival(
-            bias_full.at[flipped(z, bits)],
-            bias_sems.at[entry],
-            spare.at[0],
-            device_at(y, x, core, flipped(z, bits)),
-        )
-    for copy in locals_:
+    embed()
+    work = None
+    for group in range(groups):
+        take_z(group, 0)
+        if work:
+            work[1]()
+        take_z(group, 1)
+        if work:
+            work[2]()
+        if group:
+            take_corner(group - 1, 1)
+        if work:
+            work[3]()
+        take_xy(group, 0)
+        take_z(group, 2)
+        if group + 1 < groups:
+            begin(group + 1)
+        if group:
+            take_corner(group - 1, 2)
+        take_xy(group, 1)
+        loads = fetch(group - 1) if group else ()
+        if group == 1:
+            take_bias()
+        take_corner(group, 0)
+        for copy in loads:
+            copy.wait()
+        work = chunks(group - 1) if group else None
+        if work:
+            work[0]()
+        take_xy(group, 2)
+    take_corner(groups - 1, 1)
+    if work:
+        work[1]()
+    take_corner(groups - 1, 2)
+    if work:
+        work[2]()
+        work[3]()
+    for copy in fetch(groups - 1):
         copy.wait()
+    for chunk in chunks(groups - 1):
+        chunk()
+    free(*list(pending))
     copies.finish()
 
     @pl.when(middle == 1)
@@ -362,19 +504,32 @@
             copy.wait_send()
 
 
-def gather_all(shards, bias):
+def forward_all(shards, bias, embedding, valid, gains):
     units = len(shards)
+    rows = embedding[0].shape[0]
+    heads = shards[0].size // (3 * HEAD_DIM * D)
+    low, full = jnp.bfloat16, jnp.float32
     outs = [jax.ShapeDtypeStruct((4, *shard.shape), shard.dtype) for shard in shards]
     outs.append(jax.ShapeDtypeStruct((4, *bias.shape), bias.dtype))
+    outs.append(jax.ShapeDtypeStruct((rows, D), full))
+    shapes = layer_shapes(rows, heads)
+    outs += shapes * NL
     vmem = pl.BlockSpec(memory_space=pltpu.VMEM)
     anywhere = pl.BlockSpec(memory_space=pl.ANY)
     dma = pltpu.SemaphoreType.DMA
+    inputs = [*shards, bias, *embedding, valid, *gains]
+    scratch = [pltpu.VMEM((4, shard.size // D, D), low) for shard in shards[:4]]
+    scratch.append(pltpu.VMEM((4, *bias.shape), full))
+    scratch.append(pltpu.VMEM((rows // P_SIZE, P_SIZE, P_SIZE), full))
+    scratch += [pltpu.VMEM((rows, D), full)] * 2
+    scratch += [pltpu.VMEM(shape.shape, shape.dtype) for shape in shapes[:7]]
     return pl.pallas_call(
-        functools.partial(gather_kernel, units // 4),
+        forward_kernel,
         out_shape=outs,
-        in_specs=[vmem] * (units + 1),
-        out_specs=[anywhere] * (units + 1),
-        scratch_shapes=[
+        in_specs=[vmem] * len(inputs),
+        out_specs=[anywhere] * len(outs),
+        scratch_shapes=scratch
+        + [
             dma((3 + units * (2 + 3 * 9),)),
             dma((units, 4)),
             dma((units, 3, 4)),
@@ -382,10 +537,14 @@
             dma((units + 1,)),
             dma((3,)),
             dma((1,)),
+            dma((units + 1,)),
+            dma((NL, 9)),
         ],
-        compiler_params=pltpu.CompilerParams(collective_id=0, has_side_effects=True),
-        name="gather_weights",
-    )(*shards, bias)
+        compiler_params=pltpu.CompilerParams(
+            collective_id=0, has_side_effects=True, vmem_limit_bytes=BACK_LIMIT
+        ),
+        name="gather_forward",
+    )(*inputs)
 
 
 def add_slab(target, addend):
@@ -395,292 +554,45 @@
 
 
 ITEM_ORDER = (0, 2, 1, 3)
-AHEAD = 3
-
-
-def reduce_kernel(groups, spread_all, *refs):
-    units = sum(len(group) for group in groups)
-    grads = refs[:units]
-    outs = refs[units : 2 * units]
-    own, got_core, got_one, got_two, got_z, result = (
-        refs[(2 + entry) * units : (3 + entry) * units] for entry in range(6)
-    )
-    send_sems, load_sems, step_sems, z_sems, spread_sems, core_sems, all_sems, spare = refs[
-        8 * units :
-    ]
-    y, x, core, z = place()
-    at_x = device_at(y, 1 - x, core, z)
-    at_y = device_at(1 - y, x, core, z)
-    at_core = device_at(y, x, 1 - core, z)
-    greet(partners())
-    copies = Copies(send_sems)
-    conditional = []
-    items = [(group, t) for group in groups for t in ITEM_ORDER]
-
-    def load(group, t):
-        for unit in group:
-            grad = grads[unit]
-            copies.send(
-                grad.at[t, :, :, :, 1 - core],
-                got_core[unit].at[t],
-                step_sems.at[unit, 0, t],
-                at_core,
-            )
-            pltpu.make_async_copy(
-                grad.at[t, :, :, :, core], own[unit].at[t], load_sems.at[unit, t]
-            ).start()
-
-    def take_core_sum(group, t):
-        for unit in group:
-            grad = grads[unit]
-            mine, other = own[unit], got_core[unit]
-            pltpu.make_async_copy(
-                grad.at[t, :, :, :, core], mine.at[t], load_sems.at[unit, t]
-            ).wait()
-            wait_arrival(other.at[t], step_sems.at[unit, 0, t], spare.at[0], at_core)
-            count = mine.shape[1] * 4
-
-            def body(entry, carry):
-                spot = (t, entry // 4, entry // 2 % 2, entry % 2)
-                add_slab(mine.at[spot], other.at[spot])
-                return carry
-
-            lax.fori_loop(0, count, body, 0)
-            if t < 2:
-                copies.send(
-                    mine.at[t, :, :, 1 - x], got_one[unit].at[t], step_sems.at[unit, 1, t], at_x
-                )
-            else:
-                copies.send(
-                    mine.at[t, :, 1 - y], got_one[unit].at[t], step_sems.at[unit, 1, t], at_y
-                )
-
-    def take_one(group, t):
-        for unit in group:
-            mine, other = own[unit], got_one[unit]
-            wait_arrival(
-                other.at[t], step_sems.at[unit, 1, t], spare.at[0], at_x if t < 2 else at_y
-            )
-            count = mine.shape[1] * 2
-
-            def body(entry, carry):
-                first, second = entry // 2, entry % 2
-                if t < 2:
-                    add_slab(mine.at[t, first, second, x], other.at[t, first, second])
-                else:
-                    add_slab(mine.at[t, first, y, second], other.at[t, first, second])
-                return carry
-
-            lax.fori_loop(0, count, body, 0)
-            if t < 2:
-                copies.send(
-                    mine.at[t, :, 1 - y, x], got_two[unit].at[t], step_sems.at[unit, 2, t], at_y
-                )
-            else:
-                copies.send(
-                    mine.at[t, :, y, 1 - x], got_two[unit].at[t], step_sems.at[unit, 2, t], at_x
-                )
-
-    def take_two(group, t):
-        for unit in group:
-            mine, other = own[unit], got_two[unit]
-            wait_arrival(
-                other.at[t], step_sems.at[unit, 2, t], spare.at[0], at_y if t < 2 else at_x
-            )
-
-            def body(entry, carry):
-                add_slab(mine.at[t, entry, y, x], other.at[t, entry])
-                return carry
-
-            lax.fori_loop(0, mine.shape[1], body, 0)
-            copy = pltpu.make_async_remote_copy(
-                src_ref=mine.at[t, :, y, x],
-                dst_ref=got_z[unit].at[z],
-                send_sem=send_sems.at[copies.count],
-                recv_sem=z_sems.at[unit, z],
-                device_id=device_at(y, x, core, t),
-                device_id_type=MESH,
-            )
-            copies.count += 1
-
-            @pl.when(z != t)
-            def _():
-                copy.start()
-
-            conditional.append((t, copy))
-
-    def slot_of(unit):
-        return z if unit in spread_all else 0
-
-    def spot_of(unit, where):
-        return outs[unit].at[(slot_of(unit), slice(None), *where)]
-
-    def half_spot(unit, where, side):
-        count = outs[unit].shape[1]
-        if count > 1:
-            return outs[unit].at[(slot_of(unit), halves(count)[side], *where)]
-        rows = halves(outs[unit].shape[5])[side]
-        return outs[unit].at[(slot_of(unit), slice(None), *where, rows)]
-
-    def take_z(group):
-        for unit in group:
-            mine, other, total = own[unit], got_z[unit], result[unit]
-            for bits in SWAP_TENSOR:
-                t = flipped(z, bits)
-                wait_arrival(
-                    other.at[t], z_sems.at[unit, t], spare.at[0], device_at(y, x, core, t)
-                )
-
-            def body(entry, carry):
-                value = mine[z, entry, y, x].astype(jnp.float32)
-                for bits in SWAP_TENSOR:
-                    value = value + other[flipped(z, bits), entry].astype(jnp.float32)
-                total[entry] = value.astype(total.dtype)
-                return carry
-
-            lax.fori_loop(0, mine.shape[1], body, 0)
-            spot = spot_of(unit, (y, x, core))
-            pltpu.make_async_copy(total, spot, load_sems.at[unit, 4]).start()
-            copies.send(total, spot, spread_sems.at[unit, 0], at_x)
-            copies.send(total, spot, spread_sems.at[unit, 1], at_y)
-            copies.send(total, spot, core_sems.at[unit, 0], at_core)
-
-    def take_spread(group):
-        for unit in group:
-            spot = spot_of(unit, (y, 1 - x, core))
-            wait_arrival(spot, spread_sems.at[unit, 0], spare.at[0], at_x)
-            first = half_spot(unit, (y, 1 - x, core), 0)
-            copies.send(first, first, spread_sems.at[unit, 2], at_y)
-            copies.send(spot, spot, core_sems.at[unit, 1], at_core)
-            spot = spot_of(unit, (1 - y, x, core))
-            wait_arrival(spot, spread_sems.at[unit, 1], spare.at[0], at_y)
-            second = half_spot(unit, (1 - y, x, core), 1)
-            copies.send(second, second, spread_sems.at[unit, 3], at_x)
-            copies.send(spot, spot, core_sems.at[unit, 2], at_core)
-
-    def take_corner(group):
-        for unit in group:
-            where = (1 - y, 1 - x, core)
-            wait_arrival(half_spot(unit, where, 0), spread_sems.at[unit, 2], spare.at[0], at_y)
-            wait_arrival(half_spot(unit, where, 1), spread_sems.at[unit, 3], spare.at[0], at_x)
-            spot = spot_of(unit, where)
-            copies.send(spot, spot, core_sems.at[unit, 3], at_core)
-
-    def take_last(group):
-        for unit in group:
-            pltpu.make_async_copy(
-                result[unit], spot_of(unit, (y, x, core)), load_sems.at[unit, 4]
-            ).wait()
-            for entry, where in enumerate(((y, x), (y, 1 - x), (1 - y, x), (1 - y, 1 - x))):
-                spot = spot_of(unit, (*where, 1 - core))
-                wait_arrival(spot, core_sems.at[unit, entry], spare.at[0], at_core)
-
-    def run(step):
-        if step < len(items):
-            take_core_sum(*items[step])
-        if 0 <= step - 1 < len(items):
-            take_one(*items[step - 1])
-        if 0 <= step - 2 < len(items):
-            take_two(*items[step - 2])
-        for index, group in enumerate(groups):
-            last = 4 * index + 3
-            if step == last + 4:
-                take_z(group)
-            if step == last + 5:
-                take_spread(group)
-            if step == last + 6:
-                take_corner(group)
-
-    for item in items[:AHEAD]:
-        load(*item)
-    for step in range(len(items) + 6):
-        if step + AHEAD < len(items):
-            load(*items[step + AHEAD])
-        run(step)
-    for group in groups:
-        take_last(group)
-    for entry, unit in enumerate(spread_all):
-        for bits in SWAP_TENSOR:
-            copies.send(
-                outs[unit].at[z],
-                outs[unit].at[z],
-                all_sems.at[entry, bits],
-                device_at(y, x, core, flipped(z, bits)),
-            )
-        for bits in SWAP_TENSOR:
-            t = flipped(z, bits)
-            wait_arrival(
-                outs[unit].at[t], all_sems.at[entry, bits], spare.at[0], device_at(y, x, core, t)
-            )
-    copies.finish()
-    for t, copy in conditional:
-
-        @pl.when(z != t)
-        def _(copy=copy):
-            copy.wait_send()
-
-
-def reduce_all(grads, groups, spread_all):
-    units = len(grads)
-    scratch = []
-    for lead in ((4, 2, 2), (4, 2, 2), (4, 2), (4,), (4,), ()):
-        for grad in grads:
-            count, rows = grad.shape[1], grad.shape[5]
-            shape = lead[:1] + (count,) + lead[1:] + (rows, D)
-            scratch.append(pltpu.VMEM(shape, jnp.bfloat16))
-    dma = pltpu.SemaphoreType.DMA
-    anywhere = pl.BlockSpec(memory_space=pl.ANY)
-    return pl.pallas_call(
-        functools.partial(reduce_kernel, groups, spread_all),
-        out_shape=[
-            jax.ShapeDtypeStruct((4 if unit in spread_all else 1, *grad.shape[1:]), grad.dtype)
-            for unit, grad in enumerate(grads)
-        ],
-        in_specs=[anywhere] * units,
-        out_specs=[anywhere] * units,
-        scratch_shapes=scratch
-        + [
-            dma((units * 24 + 3 * len(spread_all),)),
-            dma((units, 5)),
-            dma((units, 3, 4)),
-            dma((units, 4)),
-            dma((units, 4)),
-            dma((units, 4)),
-            dma((max(len(spread_all), 1), 4)),
-            dma((1,)),
-        ],
-        compiler_params=pltpu.CompilerParams(
-            collective_id=1, has_side_effects=True, vmem_limit_bytes=62 * 1024 * 1024
-        ),
-        name="reduce_gradients",
-    )(*grads)
 
 
 def fast_mesh():
     return lax.axis_size("batch") == 8 and lax.axis_size("tensor") == 4
 
 
-def gather_weights(shards, bias):
+def forward_layers(shards, bias, embedding, valid, allowed, gains):
     if not fast_mesh():
-        wholes = [to_tensor_major(blocks) for blocks in gather_rows(shards)]
-        return (wholes, lax.all_gather(bias, "tensor", axis=0))
-    parts = []
-    for shard in shards:
-        rows = shard.shape[0]
-        parts.append(shard.reshape(8, -1, D) if rows == D else shard.reshape(-1, 8, 8, D))
-    results = gather_all(parts, jnp.pad(bias, ((0, 8 - NL), (0, 0))))
-    return ([whole.reshape(-1, D) for whole in results[:-1]], results[-1][:, :NL])
-
-
-def reduce_weights(split_list, small):
-    if not fast_mesh():
-        grads = [grad.reshape(-1, D) for grad in split_list[0] + split_list[1]]
-        sums = reduce_rows([to_batch_major(grad) for grad in grads] + [split_blocks(small)])
-        small_sum = lax.all_gather(sums[-1], "tensor", axis=1).reshape(-1, D)
-        return ([entry.reshape(-1, D) for entry in sums[:-1]], small_sum)
-    part = small.astype(jnp.bfloat16).reshape(4, 1, 2, 2, 2, -1, D)
-    (small_sum,) = reduce_all([part], ((0,),), (0,))
-    return (split_list[0] + split_list[1], small_sum.reshape(-1, D))
+        tensor_count = lax.axis_size("tensor")
+        wholes = [
+            to_tensor_major(blocks).reshape(tensor_count, -1, D) for blocks in gather_rows(shards)
+        ]
+        bias_all = lax.all_gather(bias, "tensor", axis=0)
+        patches, embed_weight, embed_bias, table, class_rows = embedding
+        hidden = product(patches, embed_weight) + embed_bias
+        hidden = hidden.reshape(-1, P_SIZE, D) + table.astype(jnp.float32)[None]
+        hidden = (hidden + class_rows[:, None]).reshape(-1, D)
+        stored = []
+        for layer_index in range(NL):
+            weights = wholes[4 * layer_index : 4 * layer_index + 4]
+            *kept, after = layer_forward(
+                hidden, allowed, gains[layer_index], bias_all[:, layer_index], weights
+            )
+            stored.append((hidden, *kept))
+            hidden = after
+        return (wholes, stored, hidden)
+    parts = [
+        shard.reshape((8, -1, D) if shard.shape[0] == D else (-1, 8, 8, D)) for shard in shards
+    ]
+    results = forward_all(parts, jnp.pad(bias, ((0, 8 - NL), (0, 0))), embedding, valid, gains)
+    units = len(shards)
+    wholes = [whole.reshape(4, -1, D) for whole in results[:units]]
+    hidden = results[units + 1]
+    stored = []
+    for layer_index in range(NL):
+        *kept, after = results[units + 2 + 8 * layer_index : units + 10 + 8 * layer_index]
+        stored.append((hidden, *kept))
+        hidden = after
+    return (wholes, stored, hidden)
 
 
 def back_dot(former, latter):
@@ -749,7 +661,7 @@
     lax.fori_loop(begin * images, end * images, step, 0)
 
 
-def attend_into(qkv, allowed, mixed):
+def attend_into(qkv, allowed, mixed, begin=0, end=4):
     def body(t, image, rows):
         blocks = []
         for head in range(qkv.shape[2] // (3 * HEAD_DIM)):
@@ -757,7 +669,7 @@
             blocks.append(product(probs.astype(jnp.bfloat16), values))
         mixed[t, rows] = jnp.concatenate(blocks, axis=1).astype(mixed.dtype)
 
-    each_image(qkv, body)
+    each_image(qkv, body, begin, end)
 
 
 def attend_back_into(qkv, allowed, grad_mixed, grad_qkv, begin=0, end=4):
@@ -781,12 +693,12 @@
     each_image(qkv, body, begin, end)
 
 
-def each_part(body, count=4):
+def each_part(body, begin=0, end=4):
     def step(t, carry):
         body(t)
         return carry
 
-    lax.fori_loop(0, count, step, 0)
+    lax.fori_loop(begin, end, step, 0)
 
 
 def layer_forward_chunks(
@@ -951,20 +863,46 @@
     )(grad, allowed, gains, *weights, *stored)
 
 
-MLP_GROUP, ATTEND_GROUP = (2, 3), (0, 1)
-
-
-def layer_back_kernel(*refs):
+ATTEND_GROUP, MLP_GROUP, SMALL_GROUP, LATE_GROUP = (0, 1), (2, 3), (4,), (5, 6)
+OF_UNIT = (0, 1, 2, 3, 4, 0, 1)
+POSITION_ROW, EMBED_ROW, LAYER_ROW, IMAGE_ROW, OTHER_ROW, SMALL_ROWS = 0, 256, 304, 320, 384, 512
+
+
+def layer_back_kernel(last, *refs):
     grad_in, hidden, hidden_mid, normed, normed_mlp, slope, active, up_w, down_w = refs[:9]
     qkv, mixed, allowed, gains, attend_w, merge_w = refs[9:15]
-    grad, rows_out = refs[15:17]
-    outs = refs[17:21]
-    grads, got_core, got_one, got_two, got_z, result = (
-        refs[21 + 4 * entry : 25 + 4 * entry] for entry in range(6)
-    )
-    low, grad_inner, grad_mixed, grad_qkv, upstream, values, rounded = refs[45:52]
-    slopes, actives, ups, downs = refs[52:56]
-    send_sems, step_sems, z_sems, spread_sems, core_sems, spare, load_sems, stream_sems = refs[56:]
+    refs = refs[15:]
+    if last:
+        late, extra, patches = refs[:2], refs[2], refs[3]
+        refs = refs[4:]
+    grad, rows_out = refs[:2]
+    refs = refs[2:]
+    if last:
+        outs = [refs[unit] for unit in range(7)]
+        refs = refs[7:]
+        units = 5
+    else:
+        outs = [None, None, *refs[:2]]
+        raw = refs[2:4]
+        refs = refs[4:]
+        units = 4
+    groups = []
+    for entry in range(6):
+        found = list(refs[:units])
+        refs = refs[units:]
+        if last:
+            found += [found[0], found[1]]
+        groups.append(found)
+    grads, got_core, got_one, got_two, got_z, result = groups
+    if last:
+        got_z[5:], result[5:], small_v = refs[:2], refs[2:4], refs[4]
+        refs = refs[5:]
+    low, grad_inner, grad_mixed, grad_qkv, upstream, values, rounded = refs[:7]
+    slopes, actives, ups, downs = refs[7:11]
+    send_sems, step_sems, z_sems, spread_sems, core_sems, spare, load_sems, stream_sems = refs[11:19]
+    total_sems = refs[19]
+    if last:
+        all_sems = refs[20]
     y, x, core, z = place()
     at_x = device_at(y, 1 - x, core, z)
     at_y = device_at(1 - y, x, core, z)
@@ -992,75 +930,68 @@
     first_loads += [load(normed_mlp, rounded, 1), load(hidden_mid, values, 2)]
     greet(partners())
     copies = Copies(send_sems)
-    conditional = []
-    items = [(group, t) for group in (MLP_GROUP, ATTEND_GROUP) for t in ITEM_ORDER]
+    sent_of = {unit: [] for unit in range(len(grads))}
+    conditional_of = {unit: [] for unit in range(len(grads))}
+
+    def send_own(unit, *args):
+        sent_of[unit].append(copies.send(*args))
 
     def put(unit, t, value):
         target = grads[unit]
         target[t] = value.reshape(target.shape[1:]).astype(target.dtype)
 
-    def share(k):
-        group, t = items[k]
+    def share(group, step):
+        t = ITEM_ORDER[step]
         for unit in group:
+            source = grads[unit] if unit < 5 else late[unit - 5]
             copies.send(
-                grads[unit].at[t, :, :, :, 1 - core],
+                source.at[t, :, :, :, 1 - core],
                 got_core[unit].at[t],
                 step_sems.at[unit, 0, t],
                 at_core,
             )
 
-    def core_sum(k):
-        group, t = items[k]
+    def core_sum(group, step):
+        t = ITEM_ORDER[step]
         for unit in group:
             mine, other = grads[unit], got_core[unit]
             wait_arrival(other.at[t], step_sems.at[unit, 0, t], spare.at[0], at_core)
 
-            def body(entry, carry):
-                spot = (t, entry // 4, entry // 2 % 2, entry % 2)
-                add_slab(mine.at[(*spot, core)], other.at[spot])
-                return carry
-
-            lax.fori_loop(0, mine.shape[1] * 4, body, 0)
+            for spot in ((0, 0), (0, 1), (1, 0), (1, 1)):
+                where = (t, slice(None), *spot)
+                add_slab(mine.at[(*where, core)], other.at[where])
             if t < 2:
                 source, device = mine.at[t, :, :, 1 - x, core], at_x
             else:
                 source, device = mine.at[t, :, 1 - y, :, core], at_y
-            copies.send(source, got_one[unit].at[t], step_sems.at[unit, 1, t], device)
-
-    def one(k):
-        group, t = items[k]
+            send_own(unit, source, got_one[unit].at[t], step_sems.at[unit, 1, t], device, False)
+
+    def one(group, step):
+        t = ITEM_ORDER[step]
         for unit in group:
             mine, other = grads[unit], got_one[unit]
             wait_arrival(
                 other.at[t], step_sems.at[unit, 1, t], spare.at[0], at_x if t < 2 else at_y
             )
 
-            def body(entry, carry):
-                first, second = entry // 2, entry % 2
-                spot = (t, first, second, x, core) if t < 2 else (t, first, y, second, core)
-                add_slab(mine.at[spot], other.at[t, first, second])
-                return carry
-
-            lax.fori_loop(0, mine.shape[1] * 2, body, 0)
+            for entry in range(2):
+                spot = (entry, x, core) if t < 2 else (y, entry, core)
+                add_slab(mine.at[(t, slice(None), *spot)], other.at[t, :, entry])
             if t < 2:
                 source, device = mine.at[t, :, 1 - y, x, core], at_y
             else:
                 source, device = mine.at[t, :, y, 1 - x, core], at_x
-            copies.send(source, got_two[unit].at[t], step_sems.at[unit, 2, t], device)
-
-    def two(k):
-        group, t = items[k]
+            send_own(unit, source, got_two[unit].at[t], step_sems.at[unit, 2, t], device, False)
+
+    def two(group, step):
+        t = ITEM_ORDER[step]
         for unit in group:
             mine, other = grads[unit], got_two[unit]
             wait_arrival(
                 other.at[t], step_sems.at[unit, 2, t], spare.at[0], at_y if t < 2 else at_x
             )
 
-            def body(entry, carry):
-                add_slab(mine.at[t, entry, y, x, core], other.at[t, entry])
-                return carry
-
-            lax.fori_loop(0, mine.shape[1], body, 0)
+            add_slab(mine.at[t, :, y, x, core], other.at[t])
             copy = pltpu.make_async_remote_copy(
                 src_ref=mine.at[t, :, y, x, core],
                 dst_ref=got_z[unit].at[z],
@@ -1075,16 +1006,20 @@
             def _():
                 copy.start()
 
-            conditional.append((t, copy))
+            conditional_of[unit].append((t, copy))
+
+    def place_of(unit):
+        return outs[unit].at[z] if unit in SMALL_GROUP else outs[unit]
 
     def spot_of(unit, where):
-        return outs[unit].at[(slice(None), *where)]
+        return place_of(unit).at[(slice(None), *where)]
 
     def half_spot(unit, where, side):
-        count = outs[unit].shape[0]
+        spot = place_of(unit)
+        count = spot.shape[0]
         if count > 1:
-            return outs[unit].at[(halves(count)[side], *where)]
-        return outs[unit].at[(slice(None), *where, halves(outs[unit].shape[4])[side])]
+            return spot.at[(halves(count)[side], *where)]
+        return spot.at[(slice(None), *where, halves(spot.shape[4])[side])]
 
     def over_z(group):
         for unit in group:
@@ -1095,16 +1030,12 @@
                     other.at[t], z_sems.at[unit, t], spare.at[0], device_at(y, x, core, t)
                 )
 
-            def body(entry, carry):
-                value = mine[z, entry, y, x, core].astype(jnp.float32)
-                for bits in SWAP_TENSOR:
-                    value = value + other[flipped(z, bits), entry].astype(jnp.float32)
-                total[entry] = value.astype(total.dtype)
-                return carry
-
-            lax.fori_loop(0, mine.shape[1], body, 0)
+            value = mine[z, :, y, x, core].astype(jnp.float32)
+            for bits in SWAP_TENSOR:
+                value = value + other[flipped(z, bits)].astype(jnp.float32)
+            total[...] = value.astype(total.dtype)
             spot = spot_of(unit, (y, x, core))
-            pltpu.make_async_copy(total, spot, load_sems.at[3 + unit]).start()
+            pltpu.make_async_copy(total, spot, total_sems.at[unit]).start()
             copies.send(total, spot, spread_sems.at[unit, 0], at_x)
             copies.send(total, spot, spread_sems.at[unit, 1], at_y)
             copies.send(total, spot, core_sems.at[unit, 0], at_core)
@@ -1133,11 +1064,28 @@
     def finish(group):
         for unit in group:
             pltpu.make_async_copy(
-                result[unit], spot_of(unit, (y, x, core)), load_sems.at[3 + unit]
+                result[unit], spot_of(unit, (y, x, core)), total_sems.at[unit]
             ).wait()
             for entry, where in enumerate(((y, x), (y, 1 - x), (1 - y, x), (1 - y, 1 - x))):
+                if entry == 0 and unit in settled:
+                    continue
                 spot = spot_of(unit, (*where, 1 - core))
                 wait_arrival(spot, core_sems.at[unit, entry], spare.at[0], at_core)
+
+    def settle(group):
+        for unit in group:
+            for copy in sent_of.pop(unit):
+                copy.wait_send()
+            for t, copy in conditional_of.pop(unit):
+
+                @pl.when(z != t)
+                def _(copy=copy):
+                    copy.wait_send()
+
+            wait_arrival(
+                spot_of(unit, (y, x, 1 - core)), core_sems.at[unit, 0], spare.at[0], at_core
+            )
+            settled.append(unit)
 
     def mlp(step):
         t, slot = ITEM_ORDER[step], step % 2
@@ -1151,78 +1099,176 @@
         upstream[...] += back_dot(grad_inner[...], ups[slot])
         if step < 2:
             streams.append(stream(step + 2))
-        share(step)
+        share(MLP_GROUP, step)
 
     def project(step):
         t = ITEM_ORDER[step]
         put(0, t, contract_rows(grad_qkv[t], rounded[...]))
+        put(1, t, contract_rows(mixed[t], low[...]))
         upstream[...] += product(grad_qkv[t], attend_w[t])
-        share(4 + step)
-
+        if last:
+            share(ATTEND_GROUP, step)
+            return
+        for unit in ATTEND_GROUP:
+            copy = pltpu.make_async_copy(
+                grads[unit].at[t], raw[unit].at[t], step_sems.at[unit, 0, t]
+            )
+            copy.start()
+            left.append(copy)
+
+    def collect_small():
+        rows_out[5:6] = jnp.sum(grad[...], axis=0, keepdims=True)
+        small_v[LAYER_ROW : LAYER_ROW + 16] = rows_out[...]
+        images = grad.shape[0] // P_SIZE
+        total = grad[:P_SIZE]
+        for image in range(1, images):
+            total = total + grad[image * P_SIZE : (image + 1) * P_SIZE]
+        small_v[POSITION_ROW : POSITION_ROW + P_SIZE] = total
+        first = grad[...].astype(jnp.bfloat16)
+        second = (grad[...] - first.astype(jnp.float32)).astype(jnp.bfloat16)
+        small_v[EMBED_ROW : EMBED_ROW + PV] = contract_rows(patches[...], first) + contract_rows(
+            patches[...], second
+        )
+        device_index = lax.axis_index("batch") * 4 + z
+        for image in range(images):
+            rows = grad[image * P_SIZE : (image + 1) * P_SIZE]
+            spot = IMAGE_ROW + device_index * images + image
+            small_v[pl.ds(spot, 1)] = jnp.sum(rows, axis=0, keepdims=True)
+        for t in range(4):
+            part = small_v.shape[0] // 4
+            put(4, t, small_v[t * part : (t + 1) * part])
+
+    left = []
+    settled = []
     rows_out[...] = jnp.zeros_like(rows_out)
+    if last:
+        for step in range(4):
+            share(LATE_GROUP, step)
+        late_loads = [load(late[entry], grads[entry], 8 + entry) for entry in range(2)]
+        late_loads.append(load(extra, small_v, 7))
     for copy in first_loads:
         copy.wait()
     low[...] = grad[...].astype(low.dtype)
     rows_out[4:5] = jnp.sum(low[...].astype(jnp.float32), axis=0, keepdims=True)
     upstream[...] = jnp.zeros_like(upstream)
     mlp(0)
+    if last:
+        for copy in late_loads:
+            copy.wait()
+        core_sum(LATE_GROUP, 0)
+        core_sum(LATE_GROUP, 1)
     mlp(1)
-    core_sum(0)
+    core_sum(MLP_GROUP, 0)
+    if last:
+        core_sum(LATE_GROUP, 2)
+        core_sum(LATE_GROUP, 3)
     mlp(2)
-    core_sum(1)
+    core_sum(MLP_GROUP, 1)
+    if last:
+        one(LATE_GROUP, 0)
+        one(LATE_GROUP, 1)
     mlp(3)
-    core_sum(2)
-    one(0)
+    core_sum(MLP_GROUP, 2)
+    if last:
+        one(LATE_GROUP, 2)
+        one(LATE_GROUP, 3)
+        two(LATE_GROUP, 0)
+        two(LATE_GROUP, 1)
     rows_out[2:3], rows_out[3:4] = norm_back_into(grad, values, upstream, gains[2:3])
     later_loads = [load(hidden, values, 2), load(normed, rounded, 1)]
     low[...] = grad[...].astype(low.dtype)
     for t in range(4):
-        put(1, t, contract_rows(mixed[t], low[...]))
         grad_mixed[t] = back_dot(low[...], merge_w[t]).astype(grad_mixed.dtype)
-    core_sum(3)
-    one(1)
+    core_sum(MLP_GROUP, 3)
+    one(MLP_GROUP, 0)
+    if last:
+        two(LATE_GROUP, 2)
+        two(LATE_GROUP, 3)
     attend_back_into(qkv, allowed, grad_mixed, grad_qkv, 0, 2)
-    one(2)
-    two(0)
+    one(MLP_GROUP, 1)
+    two(MLP_GROUP, 0)
+    if last:
+        over_z(LATE_GROUP)
     attend_back_into(qkv, allowed, grad_mixed, grad_qkv, 2, 4)
-    one(3)
-    two(1)
+    one(MLP_GROUP, 2)
+    two(MLP_GROUP, 1)
+    if last:
+        spread(LATE_GROUP)
+        settle(LATE_GROUP)
     upstream[...] = jnp.zeros_like(upstream)
     for copy in later_loads:
         copy.wait()
     project(0)
+    one(MLP_GROUP, 3)
     project(1)
-    core_sum(4)
-    two(2)
+    if last:
+        core_sum(ATTEND_GROUP, 0)
+    two(MLP_GROUP, 2)
     project(2)
-    core_sum(5)
-    two(3)
+    if last:
+        core_sum(ATTEND_GROUP, 1)
+    two(MLP_GROUP, 3)
     project(3)
-    core_sum(6)
-    one(4)
+    if last:
+        core_sum(ATTEND_GROUP, 2)
+        one(ATTEND_GROUP, 0)
     rows_out[0:1], rows_out[1:2] = norm_back_into(grad, values, upstream, gains[0:1])
-    core_sum(7)
-    one(5)
     over_z(MLP_GROUP)
-    two(4)
-    one(6)
-    two(5)
-    one(7)
-    spread(MLP_GROUP)
-    two(6)
-    corner(MLP_GROUP)
-    two(7)
-    over_z(ATTEND_GROUP)
-    spread(ATTEND_GROUP)
-    corner(ATTEND_GROUP)
-    finish(MLP_GROUP)
-    finish(ATTEND_GROUP)
+    if last:
+        collect_small()
+        for step in range(4):
+            share(SMALL_GROUP, step)
+        core_sum(ATTEND_GROUP, 3)
+        one(ATTEND_GROUP, 1)
+        corner(LATE_GROUP)
+        two(ATTEND_GROUP, 0)
+        for step in range(4):
+            core_sum(SMALL_GROUP, step)
+        one(ATTEND_GROUP, 2)
+        two(ATTEND_GROUP, 1)
+        spread(MLP_GROUP)
+        one(ATTEND_GROUP, 3)
+        two(ATTEND_GROUP, 2)
+        for step in range(4):
+            one(SMALL_GROUP, step)
+        two(ATTEND_GROUP, 3)
+        corner(MLP_GROUP)
+        for step in range(4):
+            two(SMALL_GROUP, step)
+        over_z(ATTEND_GROUP)
+        over_z(SMALL_GROUP)
+        spread(ATTEND_GROUP)
+        spread(SMALL_GROUP)
+        corner(ATTEND_GROUP)
+        corner(SMALL_GROUP)
+        finish(SMALL_GROUP)
+        (unit,) = SMALL_GROUP
+        for bits in SWAP_TENSOR:
+            at_t = device_at(y, x, core, flipped(z, bits))
+            copies.send(outs[unit].at[z], outs[unit].at[z], all_sems.at[bits], at_t)
+        finish(LATE_GROUP)
+        finish(MLP_GROUP)
+        finish(ATTEND_GROUP)
+        for bits in SWAP_TENSOR:
+            t = flipped(z, bits)
+            wait_arrival(
+                outs[unit].at[t], all_sems.at[bits], spare.at[0], device_at(y, x, core, t)
+            )
+    else:
+        spread(MLP_GROUP)
+        corner(MLP_GROUP)
+        finish(MLP_GROUP)
+    for copy in left:
+        copy.wait()
     copies.finish()
-    for t, copy in conditional:
-
-        @pl.when(z != t)
-        def _(copy=copy):
+    for unit in sent_of:
+        for copy in sent_of[unit]:
             copy.wait_send()
+        for t, copy in conditional_of[unit]:
+
+            @pl.when(z != t)
+            def _(copy=copy):
+                copy.wait_send()
 
 
 def owner_shape(weight):
@@ -1230,19 +1276,27 @@
     return (count, 2, 2, 2, weight.shape[1] // (8 * count), D)
 
 
-def layer_back_reduce(layer_index, grad, allowed, gains, weights, stored):
+def layer_back_reduce(layer_index, grad, allowed, gains, weights, stored, late=(), extra=None, patches=None):
     hidden, normed, qkv, mixed, hidden_mid, normed_mlp, slope, active = stored
     attend_w, merge_w, up_w, down_w = weights
+    last = layer_index == 0
     rows, heads = grad.shape[0], attend_w.shape[1] // (3 * HEAD_DIM)
     low, full = jnp.bfloat16, jnp.float32
     vmem = pl.BlockSpec(memory_space=pltpu.VMEM)
     anywhere = pl.BlockSpec(memory_space=pl.ANY)
     shapes = [owner_shape(weight) for weight in weights]
+    if last:
+        shapes.append((1, 2, 2, 2, SMALL_ROWS // 32, D))
     scratch = []
     for lead in ((4, 2, 2, 2), (4, 2, 2), (4, 2), (4,), (4,), ()):
         for shape in shapes:
             whole = lead[:1] + shape[:1] + lead[1:] + shape[4:]
             scratch.append(pltpu.VMEM(whole, low))
+    count = 7 if last else 4
+    if last:
+        scratch += [pltpu.VMEM((4, *shape[:1], *shape[4:]), low) for shape in shapes[:2]]
+        scratch += [pltpu.VMEM(shape[:1] + shape[4:], low) for shape in shapes[:2]]
+        scratch.append(pltpu.VMEM((SMALL_ROWS, D), full))
     dma = pltpu.SemaphoreType.DMA
     scratch += [
         pltpu.VMEM((rows, D), low),
@@ -1256,32 +1310,42 @@
         pltpu.VMEM((2, rows, D), low),
         pltpu.VMEM((2, D, D), low),
         pltpu.VMEM((2, D, D), low),
-        dma((4 * 24,)),
-        dma((4, 3, 4)),
-        dma((4, 4)),
-        dma((4, 4)),
-        dma((4, 4)),
+        dma((count * 24 + 3,)),
+        dma((count, 3, 4)),
+        dma((count, 4)),
+        dma((count, 4)),
+        dma((count, 4)),
         dma((1,)),
-        dma((7,)),
+        dma((10,)),
         dma((2, 4)),
+        dma((count,)),
     ]
+    if last:
+        scratch.append(dma((4,)))
     outs = [jax.ShapeDtypeStruct((rows, D), full), jax.ShapeDtypeStruct((16, D), full)]
-    outs += [jax.ShapeDtypeStruct(shape, low) for shape in shapes]
-    after, rows_out, *sums = pl.pallas_call(
-        layer_back_kernel,
+    sums = [jax.ShapeDtypeStruct(shape, low) for shape in shapes]
+    parts = [jax.ShapeDtypeStruct((4, *shape), low) for shape in shapes]
+    if last:
+        outs += sums[:4] + [parts[4]] + sums[:2]
+    else:
+        outs += sums[2:4] + parts[:2]
+    inputs = [grad, hidden, hidden_mid, normed, normed_mlp, slope, active, up_w, down_w]
+    specs = [anywhere] * 9 + [vmem] * 6
+    inputs += [qkv, mixed, allowed, gains, attend_w, merge_w]
+    if last:
+        inputs += [*late, extra, patches]
+        specs += [anywhere] * 3 + [vmem]
+    return pl.pallas_call(
+        functools.partial(layer_back_kernel, last),
         out_shape=outs,
-        in_specs=[anywhere] * 9 + [vmem] * 6,
-        out_specs=[vmem] * 2 + [anywhere] * 4,
+        in_specs=specs,
+        out_specs=[vmem] * 2 + [anywhere] * (len(outs) - 2),
         scratch_shapes=scratch,
         compiler_params=pltpu.CompilerParams(
             collective_id=2 + layer_index, has_side_effects=True, vmem_limit_bytes=BACK_LIMIT
         ),
         name="layer_back_reduce",
-    )(
-        grad, hidden, hidden_mid, normed, normed_mlp, slope, active, up_w, down_w,
-        qkv, mixed, allowed, gains, attend_w, merge_w,
-    )
-    return (after, rows_out, [entry.reshape(-1, D) for entry in sums])
+    )(*inputs)
 
 
 BACK_LIMIT = 66 * 1000 * 1000
@@ -1330,29 +1394,20 @@
         shards.append(merge_weight[layer_index])
         shards.append(up_weight[layer_index])
         shards.append(down_weight[layer_index])
-    wholes, bias_all = gather_weights(shards, up_bias)
-    layers = []
-    for layer_index in range(NL):
-        weights = [
-            whole.reshape(tensor_count, -1, D)
-            for whole in wholes[4 * layer_index : 4 * layer_index + 4]
-        ]
-        gains = jnp.stack(
+    gains = [
+        jnp.stack(
             [attn_gain[layer_index], attn_offset[layer_index], mlp_gain[layer_index]]
             + [mlp_offset[layer_index], down_bias[layer_index]]
         )
-        layers.append((gains, bias_all[:, layer_index], weights))
+        for layer_index in range(NL)
+    ]
     choose = class_ids[:, None] == lax.broadcasted_iota(jnp.int32, (local_images, CLASSES), 1)
     class_rows = product(choose.astype(jnp.bfloat16), class_table)
-    hidden = product(patches, embed_weight) + embed_bias
-    hidden = hidden.reshape(local_images, P_SIZE, D) + position_table.astype(jnp.float32)[None]
-    hidden = (hidden + class_rows[:, None]).reshape(shard_count, D)
-    stored = []
-    for layer_index in range(NL):
-        gains, bias, weights = layers[layer_index]
-        *kept, after = layer_forward(hidden, allowed, gains, bias, weights)
-        stored.append((hidden, *kept))
-        hidden = after
+    embedding = (patches, embed_weight, embed_bias[None], position_table, class_rows)
+    valid_rows = local_valid.astype(jnp.float32).reshape(local_images, P_SIZE)
+    wholes, stored, hidden = forward_layers(
+        shards, up_bias, embedding, valid_rows, allowed, gains
+    )
     final = layer_norm(hidden, final_gain, final_offset)
     final_low = final.astype(jnp.bfloat16)
     head_out = product(final_low, head_weight) + head_bias
@@ -1380,41 +1435,57 @@
     grad_hidden, final_gain_grad, final_offset_grad = norm_backward(
         hidden, final_gain, final_offset, grad_final
     )
-    rows_of = {}
-    split_list = [None] * NL
-    for layer_index in reversed(range(NL)):
-        gains, bias, weights = layers[layer_index]
-        if fast_mesh():
-            grad_hidden, rows_of[layer_index], split_list[layer_index] = layer_back_reduce(
-                layer_index, grad_hidden, allowed, gains, weights, stored[layer_index]
-            )
-        else:
-            grad_hidden, rows_of[layer_index], *split_list[layer_index] = layer_backward(
-                grad_hidden, allowed, gains, weights, stored[layer_index]
-            )
-    per_image = grad_hidden.reshape(local_images, P_SIZE, D)
     image_count = device_count * local_images
     image_index = device_index * local_images
-    image_rows = lax.dynamic_update_slice_in_dim(
-        jnp.zeros((image_count, D), jnp.float32), jnp.sum(per_image, axis=1), image_index, 0
-    )
     id_rows = jnp.stack([class_ids // 32, class_ids % 32]).astype(jnp.float32)
     id_rows = lax.dynamic_update_slice(jnp.zeros((2, D), jnp.float32), id_rows, (0, image_index))
-    small = [
-        jnp.sum(per_image, axis=0),
-        precise_rows(patch_values, grad_hidden),
+    other = [
         head_weight_grad,
-        image_rows,
-        jnp.sum(grad_hidden, axis=0)[None],
         final_gain_grad[None],
         final_offset_grad[None],
         jnp.pad(head_bias_grad, (0, D - 2 * PV))[None],
+        id_rows,
     ]
-    small += [rows_of[0], rows_of[1], id_rows]
-    lengths = [entry.shape[0] for entry in small]
-    joined = jnp.concatenate(small, axis=0)
-    joined = jnp.pad(joined, ((0, -joined.shape[0] % (8 * device_count)), (0, 0)))
-    sums, small_sum = reduce_weights(split_list, joined)
+    if fast_mesh():
+        grad_hidden, layer_rows, up_sum, down_sum, *late = layer_back_reduce(
+            1, grad_hidden, allowed, gains[1], wholes[4:], stored[1]
+        )
+        other = jnp.concatenate([jnp.zeros((OTHER_ROW, D), jnp.float32), layer_rows] + other)
+        other = jnp.pad(other, ((0, SMALL_ROWS - other.shape[0]), (0, 0)))
+        grad_hidden, layer_rows, *sums = layer_back_reduce(
+            0, grad_hidden, allowed, gains[0], wholes[:4], stored[0], late, other, patches
+        )
+        small_sum = sums[4].reshape(-1, D)
+        sums = [entry.reshape(-1, D) for entry in sums[:4] + sums[5:] + [up_sum, down_sum]]
+    else:
+        rows_of = {}
+        split_list = [None] * NL
+        for layer_index in reversed(range(NL)):
+            weights = wholes[4 * layer_index : 4 * layer_index + 4]
+            grad_hidden, rows_of[layer_index], *split_list[layer_index] = layer_backward(
+                grad_hidden, allowed, gains[layer_index], weights, stored[layer_index]
+            )
+        per_image = grad_hidden.reshape(local_images, P_SIZE, D)
+        image_rows = lax.dynamic_update_slice_in_dim(
+            jnp.zeros((image_count, D), jnp.float32), jnp.sum(per_image, axis=1), image_index, 0
+        )
+        first_rows = lax.dynamic_update_slice_in_dim(
+            rows_of[0], jnp.sum(grad_hidden, axis=0)[None], 5, 0
+        )
+        small = [
+            jnp.sum(per_image, axis=0),
+            precise_rows(patch_values, grad_hidden),
+            first_rows,
+            image_rows,
+            rows_of[1],
+        ]
+        joined = jnp.concatenate(small + other, axis=0)
+        joined = jnp.pad(joined, ((0, -joined.shape[0] % (8 * device_count)), (0, 0)))
+        grads = [grad.reshape(-1, D) for grad in split_list[0] + split_list[1]]
+        sums = reduce_rows([to_batch_major(grad) for grad in grads] + [split_blocks(joined)])
+        small_sum = lax.all_gather(sums[-1], "tensor", axis=1).reshape(-1, D)
+        sums = [entry.reshape(-1, D) for entry in sums[:-1]]
+    split_list = [None] * NL
     for layer_index in range(NL):
         attend_sum, merge_sum, up_sum, down_sum = sums[4 * layer_index : 4 * layer_index + 4]
         split_list[layer_index] = (
@@ -1431,18 +1502,17 @@
         preferred_element_type=jnp.float32,
     )
     small_sum = small_sum.astype(jnp.float32)
-    small_list = []
-    begin = 0
-    for length in lengths:
-        small_list.append(small_sum[begin : begin + length])
-        begin += length
-    id_sums = small_list[10][:, :image_count].astype(jnp.int32)
+    other_row = IMAGE_ROW + image_count
+    row = other_row + 16 + 2 * PV
+    id_sums = small_sum[row + 3 : row + 5, :image_count].astype(jnp.int32)
     all_ids = id_sums[0] * 32 + id_sums[1]
     choose_all = all_ids[:, None] == lax.broadcasted_iota(
         jnp.int32, (image_count, CLASSES), 1
     )
-    class_grad = precise_rows(choose_all.astype(jnp.float32), small_list[3])
-    layer_rows = small_list[8:10]
+    class_grad = precise_rows(
+        choose_all.astype(jnp.float32), small_sum[IMAGE_ROW:other_row]
+    )
+    layer_rows = [small_sum[LAYER_ROW : LAYER_ROW + 16], small_sum[other_row : other_row + 16]]
     own_bias = [lax.dynamic_slice_in_dim(entry, 8 + tensor_index, 1, 0) for entry in layer_rows]
     split_stack = [jnp.stack([entry[member] for entry in split_list]) for member in range(4)]
     shared_stack = [
@@ -1452,9 +1522,9 @@
         latents,
         log_det,
         patches_grad,
-        small_list[1],
-        small_list[4][0],
-        small_list[0],
+        small_sum[EMBED_ROW : EMBED_ROW + PV],
+        layer_rows[0][5],
+        small_sum[:P_SIZE],
         class_grad,
         shared_stack[0],
         shared_stack[1],
@@ -1466,10 +1536,10 @@
         jnp.concatenate(own_bias, axis=0),
         split_stack[3],
         shared_stack[4],
-        small_list[5][0],
-        small_list[6][0],
-        jnp.swapaxes(small_list[2], 0, 1),
-        small_list[7][0, : 2 * PV],
+        small_sum[row],
+        small_sum[row + 1],
+        jnp.swapaxes(small_sum[other_row + 16 : row], 0, 1),
+        small_sum[row + 2, : 2 * PV],
     )
 
 

time: 495 us -> 452 us (0.913)
  Pallas kernels: 436 us -> 393 us
    pallas_call x6 -> x3, Pallas kernels: 436 us -> 393 us  [the longest x2 252 us: layer_back_reduce(): pl.pallas_call(functools.partial(layer_back_kernel, last), out_shape=outs...]
where the time goes in v3:
time: 452 us; the launch traced here: 446 us
  Pallas kernels  393 us (87%)
  other arithmetic  23.5 us (5%)
  local copies, waits for them, and re-layouts  21.2 us (5%)
  matrix products  7.09 us (2%)
    pallas_call x2, Pallas kernels, layer_back_reduce(): pl.pallas_call(functools.partial(layer_back_kernel, last), out_shape=outs...  252 us
    pallas_call x1, Pallas kernels, forward_all(): pl.pallas_call(forward_kernel, out_shape=outs, in_specs=[vmem] * len(inpu...  141 us
    another operation x4, other arithmetic, shards(): jnp.stack([entry[member] for entry in split_list])  9.79 us

profile of v3, /device:TPU:0, one launch (start us, length us, event | category | flops | bytes accessed | tf_op | source)
XLA Modules:
  0.0 445.9 jit_solution(16796436011671106892)
XLA Ops:
  0.7 0.8 fusion.25
  2.1 0.8 fusion.31
  2.9 0.8 fusion.33
  3.6 0.8 fusion.35
  5.7 3.3 fusion.27
  9.0 1.6 fusion.26
  10.6 0.8 copy-done.4
  11.4 1.3 fusion.28
  12.7 0.8 fusion.30
  13.6 0.8 copy.46.refs_9_.refs_18_
  14.9 0.9 fusion.11.refs_13_
  16.5 140.8 %gather_forward.1 = (bf16[4,9,8,8,768]{4,3,2,1,0:T(8,128)(2,1)}, bf16[4,3,8,8,768]{4,3,2,1,0:T(8,128)(2,1)}, bf16[4,8,96,768]{3,2,1,0:T(8,128)(2,1)}, bf16[4,8,9...) custom-call(bf16[9,8,8,768]{3,2,1,0:T(8,128)(2,1)} %bitcast.72, ...), custom_call_target="tpu_custom_call" | custom-call | tf_op jit(solution)/shard_map/gather_forward/pallas_call | solution.py:526
  157.4 1.7 reduce_sum.83
  161.1 0.8 multiply_reduce_fusion
  162.5 1.3 broadcast_add_fusion.refs_0_
  163.8 0.8 dynamic-slice_compare_fusion
  164.8 0.9 and_convert_fusion.refs_11_
  165.7 89.2 %layer_back_reduce.2 = (f32[512,768]{1,0:T(8,128)}, f32[16,768]{1,0:T(8,128)}, bf16[1,2,2,2,96,768]{5,4,3,2,1,0:T(8,128)(2,1)}, bf16[1,2,2,2,96,768]{5,4,3,2,1,0...) custom-call(f32[512,768]{1,0:T(8,128)} %broadcast_add_fusion.refs_0_, ...), custom_call_target="tpu_custom_call" | custom-call | tf_op jit(solution)/shard_map/layer_back_reduce/pallas_call | solution.py:1338
  255.4 1.7 concatenate.18
  257.1 1.2 pad.17.refs_17_
  258.4 162.7 %layer_back_reduce.3 = (f32[512,768]{1,0:T(8,128)}, f32[16,768]{1,0:T(8,128)}, bf16[9,2,2,2,8,768]{5,4,3,2,1,0:T(8,128)(2,1)}, bf16[3,2,2,2,8,768]{5,4,3,2,1,0:T...) custom-call(f32[512,768]{1,0:T(8,128)} %get-tuple-element.73.refs_0_, ...), custom_call_target="tpu_custom_call" | custom-call | tf_op jit(solution)/shard_map/layer_back_reduce/pallas_call | solution.py:1338
  421.1 1.4 bitcast_convert_fusion
  423.8 2.5 maximum_convert_fusion.1
  426.9 4.2 maximum_convert_fusion
  432.3 1.1 maximum_convert_fusion.3
  433.4 2.0 maximum_convert_fusion.2
  436.7 3.2 fusion.1
  439.9 0.9 slice.198
  440.8 0.7 slice_bitcast_fusion
  441.6 0.7 slice.196
  442.7 1.5 convolution_add_fusion
  444.3 0.7 multiply_reduce_fusion.3
  (101 shorter events, 11.8 us)
Async XLA Ops:
  0.7 159.2 %copy-start = (bf16[768,96]{0,1:T(8,128)(2,1)S(1)}, bf16[768,96]{0,1:T(8,128)(2,1)}, u32[]{:S(2)}) copy-start(bf16[768,96]{0,1:T(8,128)(2,1)} %param.42) | copy-start | bytes 442372
  5.7 3.3 copy-start.3
  9.0 2.3 copy-start.4
  11.4 1.4 copy-start.11
  11.4 2.2 copy-start.12
  11.4 3.0 copy-start.18
  11.4 3.6 copy-start.6
  11.4 3.6 copy-start.22
  12.7 3.2 copy-start.20
  157.3 1.9 copy-start.2
  157.3 2.2 copy-start.17
  157.3 2.2 copy-start.19
  159.5 0.7 copy-start.21
  159.5 1.0 copy-start.23
  159.6 1.0 copy-start.13
  421.1 2.7 copy-start.7
  421.1 2.7 copy-start.8
  426.9 5.4 %copy-start.14 = (bf16[3,2,2,2,8,768]{5,4,3,2,1,0:T(8,128)(2,1)S(1)}, bf16[3,2,2,2,8,768]{5,4,3,2,1,0:T(8,128)(2,1)}, u32[]{:S(2)}) copy-start(bf16[3,2,2,2,8,768]{5,4,3,2,1,0:T(8,128)(2,1)} %get-tuple-element.93) | copy-start | bytes 884740
  426.9 5.4 %copy-start.15 = (bf16[3,2,2,2,8,768]{5,4,3,2,1,0:T(8,128)(2,1)S(1)}, bf16[3,2,2,2,8,768]{5,4,3,2,1,0:T(8,128)(2,1)}, u32[]{:S(2)}) copy-start(bf16[3,2,2,2,8,768]{5,4,3,2,1,0:T(8,128)(2,1)} %get-tuple-element.94) | copy-start | bytes 884740
  431.1 2.3 copy-start.9
  431.1 2.3 copy-start.10
  439.9 2.9 copy-start.5
  439.9 2.9 copy-start.16
  439.9 5.7 %copy-start.1 = (bf16[768,96]{0,1:T(8,128)(2,1)S(1)}, bf16[768,96]{0,1:T(8,128)(2,1)}, u32[]{:S(2)}) copy-start(bf16[768,96]{0,1:T(8,128)(2,1)} %param.42) | copy-start | bytes 442372

commit v4 on v3

--- a/solution.py
+++ b/solution.py
@@ -204,7 +204,7 @@
     return ref.at[(*lead, b, halves(ref.shape[len(lead) + 1])[side])]
 
 
-GROUP = 2
+WEIGHT_GROUPS = ((0, 1), (2, 3), (4, 5), (6,), (7,))
 
 
 def forward_kernel(*refs):
@@ -258,7 +258,7 @@
         )
 
     def of_layer(layer):
-        return range(layer * GROUP, (layer + 1) * GROUP)
+        return WEIGHT_GROUPS[layer]
 
     def send_if_middle(source, target, recv_sem, device):
         slot = send_sems.at[copies.count]
@@ -389,7 +389,8 @@
     attend_w, merge_w, up_w, down_w = weights
 
     def chunks(group):
-        layer = group // 2
+        layer = WEIGHT_GROUPS[group][0] // 4
+        kinds = [unit % 4 for unit in WEIGHT_GROUPS[group]]
         gain, outputs = gains[layer], kept[layer]
         before, after = (hidden_a, hidden_b) if layer % 2 == 0 else (hidden_b, hidden_a)
 
@@ -448,11 +449,14 @@
         def nothing():
             pass
 
-        if group % 2 == 0:
-            return [start, attend_first, attend_second, merge]
-        return [up_first, up_second, down, nothing]
-
-    groups = units // GROUP
+        steps = [start, attend_first, attend_second, merge] if 0 in kinds else []
+        if 2 in kinds:
+            steps += [up_first, up_second]
+        if 3 in kinds:
+            steps.append(down)
+        return steps + [nothing] * (4 - len(steps))
+
+    groups = len(WEIGHT_GROUPS)
     begin(0)
     embed()
     work = None
@@ -553,7 +557,7 @@
     )
 
 
-ITEM_ORDER = (0, 2, 1, 3)
+ITEM_ORDER = (3, 0, 2, 1)
 
 
 def fast_mesh():
@@ -863,8 +867,7 @@
     )(grad, allowed, gains, *weights, *stored)
 
 
-ATTEND_GROUP, MLP_GROUP, SMALL_GROUP, LATE_GROUP = (0, 1), (2, 3), (4,), (5, 6)
-OF_UNIT = (0, 1, 2, 3, 4, 0, 1)
+ATTEND_GROUP, MLP_GROUP, SMALL_GROUP = (0, 1), (2, 3), (4,)
 POSITION_ROW, EMBED_ROW, LAYER_ROW, IMAGE_ROW, OTHER_ROW, SMALL_ROWS = 0, 256, 304, 320, 384, 512
 
 
@@ -873,30 +876,20 @@
     qkv, mixed, allowed, gains, attend_w, merge_w = refs[9:15]
     refs = refs[15:]
     if last:
-        late, extra, patches = refs[:2], refs[2], refs[3]
-        refs = refs[4:]
+        extra, patches = refs[:2]
+        refs = refs[2:]
     grad, rows_out = refs[:2]
     refs = refs[2:]
-    if last:
-        outs = [refs[unit] for unit in range(7)]
-        refs = refs[7:]
-        units = 5
-    else:
-        outs = [None, None, *refs[:2]]
-        raw = refs[2:4]
-        refs = refs[4:]
-        units = 4
-    groups = []
-    for entry in range(6):
-        found = list(refs[:units])
-        refs = refs[units:]
-        if last:
-            found += [found[0], found[1]]
-        groups.append(found)
-    grads, got_core, got_one, got_two, got_z, result = groups
-    if last:
-        got_z[5:], result[5:], small_v = refs[:2], refs[2:4], refs[4]
-        refs = refs[5:]
+    units = 5 if last else 4
+    outs = refs[:units]
+    refs = refs[units:]
+    grads, got_core, got_one, got_two, got_z, result = (
+        refs[units * entry : units * (entry + 1)] for entry in range(6)
+    )
+    refs = refs[6 * units :]
+    if last:
+        small_v = refs[0]
+        refs = refs[1:]
     low, grad_inner, grad_mixed, grad_qkv, upstream, values, rounded = refs[:7]
     slopes, actives, ups, downs = refs[7:11]
     send_sems, step_sems, z_sems, spread_sems, core_sems, spare, load_sems, stream_sems = refs[11:19]
@@ -943,9 +936,8 @@
     def share(group, step):
         t = ITEM_ORDER[step]
         for unit in group:
-            source = grads[unit] if unit < 5 else late[unit - 5]
             copies.send(
-                source.at[t, :, :, :, 1 - core],
+                grads[unit].at[t, :, :, :, 1 - core],
                 got_core[unit].at[t],
                 step_sems.at[unit, 0, t],
                 at_core,
@@ -1067,25 +1059,8 @@
                 result[unit], spot_of(unit, (y, x, core)), total_sems.at[unit]
             ).wait()
             for entry, where in enumerate(((y, x), (y, 1 - x), (1 - y, x), (1 - y, 1 - x))):
-                if entry == 0 and unit in settled:
-                    continue
                 spot = spot_of(unit, (*where, 1 - core))
                 wait_arrival(spot, core_sems.at[unit, entry], spare.at[0], at_core)
-
-    def settle(group):
-        for unit in group:
-            for copy in sent_of.pop(unit):
-                copy.wait_send()
-            for t, copy in conditional_of.pop(unit):
-
-                @pl.when(z != t)
-                def _(copy=copy):
-                    copy.wait_send()
-
-            wait_arrival(
-                spot_of(unit, (y, x, 1 - core)), core_sems.at[unit, 0], spare.at[0], at_core
-            )
-            settled.append(unit)
 
     def mlp(step):
         t, slot = ITEM_ORDER[step], step % 2
@@ -1106,15 +1081,7 @@
         put(0, t, contract_rows(grad_qkv[t], rounded[...]))
         put(1, t, contract_rows(mixed[t], low[...]))
         upstream[...] += product(grad_qkv[t], attend_w[t])
-        if last:
-            share(ATTEND_GROUP, step)
-            return
-        for unit in ATTEND_GROUP:
-            copy = pltpu.make_async_copy(
-                grads[unit].at[t], raw[unit].at[t], step_sems.at[unit, 0, t]
-            )
-            copy.start()
-            left.append(copy)
+        share(ATTEND_GROUP, step)
 
     def collect_small():
         rows_out[5:6] = jnp.sum(grad[...], axis=0, keepdims=True)
@@ -1138,128 +1105,96 @@
             part = small_v.shape[0] // 4
             put(4, t, small_v[t * part : (t + 1) * part])
 
-    left = []
-    settled = []
     rows_out[...] = jnp.zeros_like(rows_out)
     if last:
-        for step in range(4):
-            share(LATE_GROUP, step)
-        late_loads = [load(late[entry], grads[entry], 8 + entry) for entry in range(2)]
-        late_loads.append(load(extra, small_v, 7))
+        extra_load = load(extra, small_v, 3)
     for copy in first_loads:
         copy.wait()
     low[...] = grad[...].astype(low.dtype)
     rows_out[4:5] = jnp.sum(low[...].astype(jnp.float32), axis=0, keepdims=True)
     upstream[...] = jnp.zeros_like(upstream)
     mlp(0)
-    if last:
-        for copy in late_loads:
-            copy.wait()
-        core_sum(LATE_GROUP, 0)
-        core_sum(LATE_GROUP, 1)
     mlp(1)
     core_sum(MLP_GROUP, 0)
-    if last:
-        core_sum(LATE_GROUP, 2)
-        core_sum(LATE_GROUP, 3)
     mlp(2)
     core_sum(MLP_GROUP, 1)
-    if last:
-        one(LATE_GROUP, 0)
-        one(LATE_GROUP, 1)
     mlp(3)
     core_sum(MLP_GROUP, 2)
-    if last:
-        one(LATE_GROUP, 2)
-        one(LATE_GROUP, 3)
-        two(LATE_GROUP, 0)
-        two(LATE_GROUP, 1)
+    one(MLP_GROUP, 0)
     rows_out[2:3], rows_out[3:4] = norm_back_into(grad, values, upstream, gains[2:3])
     later_loads = [load(hidden, values, 2), load(normed, rounded, 1)]
     low[...] = grad[...].astype(low.dtype)
     for t in range(4):
         grad_mixed[t] = back_dot(low[...], merge_w[t]).astype(grad_mixed.dtype)
     core_sum(MLP_GROUP, 3)
-    one(MLP_GROUP, 0)
-    if last:
-        two(LATE_GROUP, 2)
-        two(LATE_GROUP, 3)
+    one(MLP_GROUP, 1)
     attend_back_into(qkv, allowed, grad_mixed, grad_qkv, 0, 2)
-    one(MLP_GROUP, 1)
+    one(MLP_GROUP, 2)
     two(MLP_GROUP, 0)
-    if last:
-        over_z(LATE_GROUP)
     attend_back_into(qkv, allowed, grad_mixed, grad_qkv, 2, 4)
-    one(MLP_GROUP, 2)
+    one(MLP_GROUP, 3)
     two(MLP_GROUP, 1)
-    if last:
-        spread(LATE_GROUP)
-        settle(LATE_GROUP)
     upstream[...] = jnp.zeros_like(upstream)
     for copy in later_loads:
         copy.wait()
     project(0)
-    one(MLP_GROUP, 3)
     project(1)
-    if last:
-        core_sum(ATTEND_GROUP, 0)
+    core_sum(ATTEND_GROUP, 0)
     two(MLP_GROUP, 2)
     project(2)
-    if last:
-        core_sum(ATTEND_GROUP, 1)
+    core_sum(ATTEND_GROUP, 1)
     two(MLP_GROUP, 3)
     project(3)
-    if last:
-        core_sum(ATTEND_GROUP, 2)
-        one(ATTEND_GROUP, 0)
+    core_sum(ATTEND_GROUP, 2)
+    one(ATTEND_GROUP, 0)
     rows_out[0:1], rows_out[1:2] = norm_back_into(grad, values, upstream, gains[0:1])
-    over_z(MLP_GROUP)
-    if last:
+    if last:
+        extra_load.wait()
         collect_small()
         for step in range(4):
             share(SMALL_GROUP, step)
-        core_sum(ATTEND_GROUP, 3)
-        one(ATTEND_GROUP, 1)
-        corner(LATE_GROUP)
-        two(ATTEND_GROUP, 0)
+    core_sum(ATTEND_GROUP, 3)
+    one(ATTEND_GROUP, 1)
+    over_z(MLP_GROUP)
+    two(ATTEND_GROUP, 0)
+    if last:
         for step in range(4):
             core_sum(SMALL_GROUP, step)
-        one(ATTEND_GROUP, 2)
-        two(ATTEND_GROUP, 1)
-        spread(MLP_GROUP)
-        one(ATTEND_GROUP, 3)
-        two(ATTEND_GROUP, 2)
+    one(ATTEND_GROUP, 2)
+    two(ATTEND_GROUP, 1)
+    if last:
         for step in range(4):
             one(SMALL_GROUP, step)
-        two(ATTEND_GROUP, 3)
-        corner(MLP_GROUP)
+    one(ATTEND_GROUP, 3)
+    spread(MLP_GROUP)
+    two(ATTEND_GROUP, 2)
+    if last:
         for step in range(4):
             two(SMALL_GROUP, step)
-        over_z(ATTEND_GROUP)
+    corner(MLP_GROUP)
+    two(ATTEND_GROUP, 3)
+    over_z(ATTEND_GROUP)
+    if last:
         over_z(SMALL_GROUP)
-        spread(ATTEND_GROUP)
+    spread(ATTEND_GROUP)
+    if last:
         spread(SMALL_GROUP)
-        corner(ATTEND_GROUP)
+    corner(ATTEND_GROUP)
+    if last:
         corner(SMALL_GROUP)
         finish(SMALL_GROUP)
         (unit,) = SMALL_GROUP
         for bits in SWAP_TENSOR:
             at_t = device_at(y, x, core, flipped(z, bits))
             copies.send(outs[unit].at[z], outs[unit].at[z], all_sems.at[bits], at_t)
-        finish(LATE_GROUP)
-        finish(MLP_GROUP)
-        finish(ATTEND_GROUP)
+    finish(MLP_GROUP)
+    finish(ATTEND_GROUP)
+    if last:
         for bits in SWAP_TENSOR:
             t = flipped(z, bits)
             wait_arrival(
                 outs[unit].at[t], all_sems.at[bits], spare.at[0], device_at(y, x, core, t)
             )
-    else:
-        spread(MLP_GROUP)
-        corner(MLP_GROUP)
-        finish(MLP_GROUP)
-    for copy in left:
-        copy.wait()
     copies.finish()
     for unit in sent_of:
         for copy in sent_of[unit]:
@@ -1276,7 +1211,7 @@
     return (count, 2, 2, 2, weight.shape[1] // (8 * count), D)
 
 
-def layer_back_reduce(layer_index, grad, allowed, gains, weights, stored, late=(), extra=None, patches=None):
+def layer_back_reduce(layer_index, grad, allowed, gains, weights, stored, extra=None, patches=None):
     hidden, normed, qkv, mixed, hidden_mid, normed_mlp, slope, active = stored
     attend_w, merge_w, up_w, down_w = weights
     last = layer_index == 0
@@ -1292,10 +1227,8 @@
         for shape in shapes:
             whole = lead[:1] + shape[:1] + lead[1:] + shape[4:]
             scratch.append(pltpu.VMEM(whole, low))
-    count = 7 if last else 4
-    if last:
-        scratch += [pltpu.VMEM((4, *shape[:1], *shape[4:]), low) for shape in shapes[:2]]
-        scratch += [pltpu.VMEM(shape[:1] + shape[4:], low) for shape in shapes[:2]]
+    count = len(shapes)
+    if last:
         scratch.append(pltpu.VMEM((SMALL_ROWS, D), full))
     dma = pltpu.SemaphoreType.DMA
     scratch += [
@@ -1316,25 +1249,22 @@
         dma((count, 4)),
         dma((count, 4)),
         dma((1,)),
-        dma((10,)),
+        dma((4,)),
         dma((2, 4)),
         dma((count,)),
     ]
     if last:
         scratch.append(dma((4,)))
     outs = [jax.ShapeDtypeStruct((rows, D), full), jax.ShapeDtypeStruct((16, D), full)]
-    sums = [jax.ShapeDtypeStruct(shape, low) for shape in shapes]
-    parts = [jax.ShapeDtypeStruct((4, *shape), low) for shape in shapes]
-    if last:
-        outs += sums[:4] + [parts[4]] + sums[:2]
-    else:
-        outs += sums[2:4] + parts[:2]
+    outs += [jax.ShapeDtypeStruct(shape, low) for shape in shapes[:4]]
+    if last:
+        outs.append(jax.ShapeDtypeStruct((4, *shapes[4]), low))
     inputs = [grad, hidden, hidden_mid, normed, normed_mlp, slope, active, up_w, down_w]
     specs = [anywhere] * 9 + [vmem] * 6
     inputs += [qkv, mixed, allowed, gains, attend_w, merge_w]
     if last:
-        inputs += [*late, extra, patches]
-        specs += [anywhere] * 3 + [vmem]
+        inputs += [extra, patches]
+        specs += [anywhere, vmem]
     return pl.pallas_call(
         functools.partial(layer_back_kernel, last),
         out_shape=outs,
@@ -1447,16 +1377,16 @@
         id_rows,
     ]
     if fast_mesh():
-        grad_hidden, layer_rows, up_sum, down_sum, *late = layer_back_reduce(
+        grad_hidden, layer_rows, *later_sums = layer_back_reduce(
             1, grad_hidden, allowed, gains[1], wholes[4:], stored[1]
         )
         other = jnp.concatenate([jnp.zeros((OTHER_ROW, D), jnp.float32), layer_rows] + other)
         other = jnp.pad(other, ((0, SMALL_ROWS - other.shape[0]), (0, 0)))
         grad_hidden, layer_rows, *sums = layer_back_reduce(
-            0, grad_hidden, allowed, gains[0], wholes[:4], stored[0], late, other, patches
+            0, grad_hidden, allowed, gains[0], wholes[:4], stored[0], other, patches
         )
         small_sum = sums[4].reshape(-1, D)
-        sums = [entry.reshape(-1, D) for entry in sums[:4] + sums[5:] + [up_sum, down_sum]]
+        sums = [entry.reshape(-1, D) for entry in sums[:4] + later_sums]
     else:
         rows_of = {}
         split_list = [None] * NL

time: 452 us -> 419 us (0.927)
  Pallas kernels: 393 us -> 360 us
    pallas_call x2, Pallas kernels: 252 us -> 226 us  [layer_back_reduce(): pl.pallas_call(functools.partial(layer_back_kernel, last), out_shape=outs...]
    pallas_call x1, Pallas kernels: 141 us -> 134 us  [forward_all(): pl.pallas_call(forward_kernel, out_shape=outs, in_specs=[vmem] * len(inpu...]
where the time goes in v4:
time: 419 us; the launch traced here: 413 us
  Pallas kernels  360 us (86%)
  other arithmetic  23.5 us (6%)
  local copies, waits for them, and re-layouts  21 us (5%)
  matrix products  7.1 us (2%)
    pallas_call x2, Pallas kernels, layer_back_reduce(): pl.pallas_call(functools.partial(layer_back_kernel, last), out_shape=outs...  226 us
    pallas_call x1, Pallas kernels, forward_all(): pl.pallas_call(forward_kernel, out_shape=outs, in_specs=[vmem] * len(inpu...  134 us
    another operation x4, other arithmetic, shards(): jnp.stack([entry[member] for entry in split_list])  9.79 us

profile of v4, /device:TPU:0, one launch (start us, length us, event | category | flops | bytes accessed | tf_op | source)
XLA Modules:
  0.0 413.2 jit_solution(669704102373728709)
XLA Ops:
  0.7 0.8 fusion.25
  2.1 0.8 fusion.31
  2.9 0.8 fusion.33
  3.6 0.8 fusion.35
  5.7 3.3 fusion.27
  9.0 1.6 fusion.26
  10.6 0.8 copy-done.4
  11.4 1.3 fusion.28
  12.7 0.8 fusion.30
  13.6 0.8 copy.46.refs_9_.refs_16_
  15.0 0.9 fusion.11.refs_13_
  16.5 133.6 %gather_forward.1 = (bf16[4,9,8,8,768]{4,3,2,1,0:T(8,128)(2,1)}, bf16[4,3,8,8,768]{4,3,2,1,0:T(8,128)(2,1)}, bf16[4,8,96,768]{3,2,1,0:T(8,128)(2,1)}, bf16[4,8,9...) custom-call(bf16[9,8,8,768]{3,2,1,0:T(8,128)(2,1)} %bitcast.72, ...), custom_call_target="tpu_custom_call" | custom-call | tf_op jit(solution)/shard_map/gather_forward/pallas_call | solution.py:530
  150.2 1.7 reduce_sum.83
  153.9 0.8 multiply_reduce_fusion
  155.3 1.3 broadcast_add_fusion.refs_0_
  156.6 0.8 dynamic-slice_compare_fusion
  157.6 0.9 and_convert_fusion.refs_11_
  158.5 100.6 %layer_back_reduce.2 = (f32[512,768]{1,0:T(8,128)}, f32[16,768]{1,0:T(8,128)}, bf16[9,2,2,2,8,768]{5,4,3,2,1,0:T(8,128)(2,1)}, bf16[3,2,2,2,8,768]{5,4,3,2,1,0:T...) custom-call(f32[512,768]{1,0:T(8,128)} %broadcast_add_fusion.refs_0_, ...), custom_call_target="tpu_custom_call" | custom-call | tf_op jit(solution)/shard_map/layer_back_reduce/pallas_call | solution.py:1268
  259.6 1.5 concatenate.18
  261.1 1.2 pad.17.refs_15_
  262.4 125.8 %layer_back_reduce.3 = (f32[512,768]{1,0:T(8,128)}, f32[16,768]{1,0:T(8,128)}, bf16[9,2,2,2,8,768]{5,4,3,2,1,0:T(8,128)(2,1)}, bf16[3,2,2,2,8,768]{5,4,3,2,1,0:T...) custom-call(f32[512,768]{1,0:T(8,128)} %get-tuple-element.71.refs_0_, ...), custom_call_target="tpu_custom_call" | custom-call | tf_op jit(solution)/shard_map/layer_back_reduce/pallas_call | solution.py:1268
  388.2 1.4 bitcast_convert_fusion
  390.8 2.5 maximum_convert_fusion.1
  394.0 4.2 %maximum_convert_fusion = f32[2,768,768]{2,1,0:T(8,128)} fusion(bf16[1,768,768]{2,1,0:T(8,128)(2,1)} %bitcast.76, bf16[1,768,768]{2,1,0:T(8,128)(2,1)} %bitcast.78), kind=kLoop, calls=%fused_computation.1 | loop fusion | flops 2359296 | bytes 7077888 | tf_op jit(solution)/shard_map/stack | solution.py:1447
  399.4 1.1 maximum_convert_fusion.3
  400.5 2.0 maximum_convert_fusion.2
  403.7 3.2 fusion.1
  406.9 0.9 slice.198
  407.9 0.7 slice_bitcast_fusion
  408.6 0.7 slice.196
  409.8 1.5 convolution_add_fusion
  411.3 0.7 multiply_reduce_fusion.3
  (101 shorter events, 11.8 us)
Async XLA Ops:
  0.7 152.0 %copy-start = (bf16[768,96]{0,1:T(8,128)(2,1)S(1)}, bf16[768,96]{0,1:T(8,128)(2,1)}, u32[]{:S(2)}) copy-start(bf16[768,96]{0,1:T(8,128)(2,1)} %param.42) | copy-start | bytes 442372
  5.7 3.3 copy-start.3
  9.0 2.3 copy-start.4
  11.4 1.4 copy-start.11
  11.4 2.2 copy-start.12
  11.4 3.0 copy-start.18
  11.4 3.6 copy-start.6
  11.4 3.6 copy-start.22
  12.7 3.2 copy-start.20
  150.1 1.9 copy-start.2
  150.1 2.2 copy-start.17
  150.1 2.2 copy-start.19
  152.3 0.7 copy-start.21
  152.3 1.0 copy-start.23
  152.4 1.0 copy-start.13
  388.1 2.7 copy-start.7
  388.2 2.7 copy-start.8
  394.0 5.4 %copy-start.14 = (bf16[3,2,2,2,8,768]{5,4,3,2,1,0:T(8,128)(2,1)S(1)}, bf16[3,2,2,2,8,768]{5,4,3,2,1,0:T(8,128)(2,1)}, u32[]{:S(2)}) copy-start(bf16[3,2,2,2,8,768]{5,4,3,2,1,0:T(8,128)(2,1)} %get-tuple-element.90) | copy-start | bytes 884740
  394.0 5.4 %copy-start.15 = (bf16[3,2,2,2,8,768]{5,4,3,2,1,0:T(8,128)(2,1)S(1)}, bf16[3,2,2,2,8,768]{5,4,3,2,1,0:T(8,128)(2,1)}, u32[]{:S(2)}) copy-start(bf16[3,2,2,2,8,768]{5,4,3,2,1,0:T(8,128)(2,1)} %get-tuple-element.89) | copy-start | bytes 884740
  398.1 2.3 copy-start.9
  398.1 2.3 copy-start.10
  406.9 2.9 copy-start.5
  406.9 2.9 copy-start.16
  406.9 5.7 %copy-start.1 = (bf16[768,96]{0,1:T(8,128)(2,1)S(1)}, bf16[768,96]{0,1:T(8,128)(2,1)}, u32[]{:S(2)}) copy-start(bf16[768,96]{0,1:T(8,128)(2,1)} %param.42) | copy-start | bytes 442372
